TPU v7x, 32 devices: a whole 2x2x4 slice. The times are simulated.
32 devices in a mesh: dp: 8 (over y, x, core), head: 4 (over z).
Axes of the slice: x: 2, y: 2, z: 4, core: 2. Of those that a mesh axis runs over, the one named last changes fastest.
Arguments:
- block_input: bfloat16 [32, 1024, 768], P('dp', 'head'), may hold values from -6 to 6
- lengths: int32 [32], P('dp'), may hold values from 256 to 1024, as said below
- cotangent: bfloat16 [32, 1024, 768], P('dp', 'head'), may hold values from -6 to 6
- norm1_gain: float32 [768], replicated, may hold values from 0.5 to 1.5
- value_projection_weight: bfloat16 [768, 768], P(None, 'head'), may hold values from -0.21875 to 0.21875
- rand_logits: bfloat16 [12, 1024, 1024], P('head'), may hold values from -8 to 8
- output_projection_weight: bfloat16 [768, 768], P('head'), may hold values from -0.875 to 0.875
- norm2_gain: float32 [768], replicated, may hold values from 0.5 to 1.5
- up_projection_weight: bfloat16 [768, 3072], replicated, may hold values from -0.21875 to 0.21875
- up_bias: float32 [3072], replicated, may hold values from -3 to 3
- down_projection_weight: bfloat16 [3072, 768], replicated, may hold values from -0.109375 to 0.109375
- down_bias: float32 [768], replicated, may hold values from -3 to 3
Outputs:
- block_output: bfloat16 [32, 1024, 768], P('dp', 'head')
- grad_x: bfloat16 [32, 1024, 768], P('dp', 'head')
- grad_rand: float32 [12, 1024, 1024], P('head', 'dp')
- grad_value: float32 [768, 768], P('dp', 'head')
- gradient_output_weight: float32 [768, 768], P('head', 'dp')
- grad_gain1: float32 [768], P(('dp', 'head'))
- grad_gain2: float32 [768], P(('dp', 'head'))
- gradient_up_weight: float32 [768, 3072], P(None, ('dp', 'head'))
- grad_up_bias: float32 [3072], P(('dp', 'head'))
- gradient_down_weight: float32 [3072, 768], P(('dp', 'head'))
- grad_down_bias: float32 [768], P(('dp', 'head'))
Inputs may be any that keep to these rules, and one draw needn't show every extreme that they name: `lengths`: each length is 256 or 1024, and both occur.
All inputs are finite; a program needn't handle non-finite values.
Results may differ from a plain program's by a relative error of at most 0.017.
Values may be sent and summed in bfloat16 or wider, within the bound.
No kernel may reach another device: no remote copies, remote signals or barrier semaphores. Data moves between devices by JAX's collectives and lax.ppermute only.
A program may use at most 256 MiB of HBM per device.

v0:
```python
import jax
import jax.numpy as jnp
from jax import lax
from jax.sharding import PartitionSpec as P

SHORT = 256


epsilon = 1e-05


def normalize(inputs):
    centered = inputs - jnp.mean(inputs, -1, keepdims=True)
    scale_inv = lax.rsqrt(jnp.mean(centered * centered, -1, keepdims=True) + epsilon)
    return (centered * scale_inv, scale_inv)


def normalize_back(grad_norm, gain, normed, scale_inv):
    scaled = grad_norm * gain
    return scale_inv * (
        scaled
        - jnp.mean(scaled, -1, keepdims=True)
        - normed * jnp.mean(scaled * normed, -1, keepdims=True)
    )


def softmax_rows(logits):
    raised = jnp.exp(logits - jnp.max(logits, -1, keepdims=True))
    return raised / jnp.sum(raised, -1, keepdims=True)


def softmax_back(probs, upstream):
    return probs * (upstream - jnp.sum(upstream * probs, -1, keepdims=True))


def local(
    block_input,
    lengths,
    cotangent,
    norm1_gain,
    value_projection_weight,
    rand_logits,
    output_projection_weight,
    norm2_gain,
    up_projection_weight,
    up_bias,
    down_projection_weight,
    down_bias,
):
    seq_count, local_rows, width = block_input.shape
    heads_here = rand_logits.shape[0]
    full_rows = rand_logits.shape[1]
    head_cols = value_projection_weight.shape[1]
    head_size = head_cols // heads_here
    is_long = lengths > SHORT
    tail = ((0, full_rows - SHORT), (0, 0), (0, 0))
    corner_pad = ((0, 0), (0, full_rows - SHORT), (0, full_rows - SHORT))
    inputs = block_input.astype(jnp.float32)
    normed1, inverse1 = normalize(inputs)
    norm1_low = (normed1 * norm1_gain).astype(jnp.bfloat16)
    combined_norm = lax.all_gather(norm1_low, "head", axis=1, tiled=True)
    value_tensor = jnp.einsum(
        "bwc,cm->bwm", combined_norm, value_projection_weight, preferred_element_type=jnp.float32
    )
    value_tensor = value_tensor.astype(jnp.bfloat16).reshape(
        seq_count, full_rows, heads_here, head_size
    )
    logits = rand_logits.astype(jnp.float32)
    probs_long = softmax_rows(logits)
    probs_short = softmax_rows(logits[:, :SHORT, :SHORT])
    long_low = probs_long.astype(jnp.bfloat16)
    short_low = probs_short.astype(jnp.bfloat16)

    def mix_one(item):
        seq_values, flag = item

        def mix_whole():
            return jnp.einsum(
                "hij,jhe->ihe", long_low, seq_values, preferred_element_type=jnp.float32
            )

        def mix_corner():
            part = jnp.einsum(
                "hij,jhe->ihe", short_low, seq_values[:SHORT], preferred_element_type=jnp.float32
            )
            return jnp.pad(part, tail)

        return lax.cond(flag, mix_whole, mix_corner).astype(jnp.bfloat16)

    mixed_output = lax.map(mix_one, (value_tensor, is_long)).reshape(
        seq_count, full_rows, head_cols
    )
    mixed_tokens = jnp.swapaxes(mixed_output, 0, 1)
    rows_in = mixed_tokens
    attended = jnp.swapaxes(
        lax.psum_scatter(
            jnp.einsum(
                "lse,ed->lsd", rows_in, output_projection_weight, preferred_element_type=jnp.float32
            ).astype(jnp.bfloat16),
            "head",
            scatter_dimension=0,
            tiled=True,
        ).astype(jnp.float32),
        0,
        1,
    )
    residual = inputs + attended
    normed2, inverse2 = normalize(residual)
    second_norm_reduced = (normed2 * norm2_gain).astype(jnp.bfloat16)
    before_act = (
        jnp.einsum(
            "nqt,ty->nqy",
            second_norm_reduced,
            up_projection_weight,
            preferred_element_type=jnp.float32,
        )
        + up_bias
    )
    hidden_activation = jax.nn.gelu(before_act).astype(jnp.bfloat16)
    output = (
        residual
        + jnp.einsum(
            "uiq,qy->uiy",
            hidden_activation,
            down_projection_weight,
            preferred_element_type=jnp.float32,
        )
        + down_bias
    )
    result_block = output.astype(jnp.bfloat16)
    upstream = cotangent.astype(jnp.float32)
    grad_down_bias = jnp.sum(upstream, (0, 1))
    gradient_down_weight = jnp.einsum(
        "bma,bmj->aj", hidden_activation, cotangent, preferred_element_type=jnp.float32
    )
    gradient_activation = jnp.einsum(
        "iug,ag->iua", cotangent, down_projection_weight, preferred_element_type=jnp.float32
    )
    gradient_preactivation = jax.vjp(jax.nn.gelu, before_act)[1](gradient_activation)[0].astype(
        jnp.bfloat16
    )
    grad_up_bias = jnp.sum(gradient_preactivation, (0, 1), dtype=jnp.float32)
    gradient_up_weight = jnp.einsum(
        "cqp,cqv->pv",
        second_norm_reduced,
        gradient_preactivation,
        preferred_element_type=jnp.float32,
    )
    gradient_second_norm = jnp.einsum(
        "gqt,bt->gqb",
        gradient_preactivation,
        up_projection_weight,
        preferred_element_type=jnp.float32,
    )
    grad_gain2 = jnp.sum(gradient_second_norm * normed2, (0, 1))
    grad_resid = upstream + normalize_back(gradient_second_norm, norm2_gain, normed2, inverse2)
    grad_attended = grad_resid.astype(jnp.bfloat16)
    gradient_combined = lax.all_gather(grad_attended, "head", axis=1, tiled=True)
    gradient_output_weight = jnp.einsum(
        "tqj,tqu->ju", mixed_output, gradient_combined, preferred_element_type=jnp.float32
    )
    grad_mixed = jnp.einsum(
        "khn,rn->khr",
        gradient_combined,
        output_projection_weight,
        preferred_element_type=jnp.float32,
    ).astype(jnp.bfloat16)
    grad_mixed = grad_mixed.reshape(seq_count, full_rows, heads_here, head_size)

    def back_one(carry, item):
        sum_long, sum_short = carry
        seq_values, seq_grads, flag = item

        def back_whole():
            back = jnp.einsum(
                "hij,ihe->jhe", long_low, seq_grads, preferred_element_type=jnp.float32
            )
            added = jnp.einsum(
                "ihe,jhe->hij", seq_grads, seq_values, preferred_element_type=jnp.float32
            )
            return (sum_long + added, sum_short, back)

        def back_corner():
            back = jnp.einsum(
                "hij,ihe->jhe", short_low, seq_grads[:SHORT], preferred_element_type=jnp.float32
            )
            added = jnp.einsum(
                "ihe,jhe->hij",
                seq_grads[:SHORT],
                seq_values[:SHORT],
                preferred_element_type=jnp.float32,
            )
            return (sum_long, sum_short + added, jnp.pad(back, tail))

        new_long, new_short, back = lax.cond(flag, back_whole, back_corner)
        return ((new_long, new_short), back.astype(jnp.bfloat16))

    start_sums = (
        jnp.zeros((heads_here, full_rows, full_rows), jnp.float32),
        jnp.zeros((heads_here, SHORT, SHORT), jnp.float32),
    )
    (sum_long, sum_short), gradient_value_rows = lax.scan(
        back_one, start_sums, (value_tensor, grad_mixed, is_long)
    )
    gradient_value_rows = gradient_value_rows.reshape(seq_count, full_rows, head_cols)
    grad_value = jnp.einsum(
        "qrf,qrj->fj", combined_norm, gradient_value_rows, preferred_element_type=jnp.float32
    )
    grad_values_tokens = jnp.swapaxes(gradient_value_rows, 0, 1)
    rows_in = grad_values_tokens
    grad_norm1 = jnp.swapaxes(
        lax.psum_scatter(
            jnp.einsum(
                "lse,de->lsd", rows_in, value_projection_weight, preferred_element_type=jnp.float32
            ).astype(jnp.bfloat16),
            "head",
            scatter_dimension=0,
            tiled=True,
        ).astype(jnp.float32),
        0,
        1,
    )
    grad_gain1 = jnp.sum(grad_norm1 * normed1, (0, 1))
    grad_input = (grad_resid + normalize_back(grad_norm1, norm1_gain, normed1, inverse1)).astype(
        jnp.bfloat16
    )
    local_rand = softmax_back(probs_long, sum_long) + jnp.pad(
        softmax_back(probs_short, sum_short), corner_pad
    )
    grad_rand, grad_value, gradient_output_weight = (
        lax.psum_scatter(
            local_rand.astype(jnp.bfloat16), "dp", scatter_dimension=1, tiled=True
        ).astype(jnp.float32),
        lax.psum_scatter(
            grad_value.astype(jnp.bfloat16), "dp", scatter_dimension=0, tiled=True
        ).astype(jnp.float32),
        lax.psum_scatter(
            gradient_output_weight.astype(jnp.bfloat16), "dp", scatter_dimension=1, tiled=True
        ).astype(jnp.float32),
    )
    shared = (
        lax.psum_scatter(gradient_up_weight, ("dp", "head"), scatter_dimension=1, tiled=True),
        lax.psum_scatter(gradient_down_weight, ("dp", "head"), scatter_dimension=0, tiled=True),
        lax.psum_scatter(grad_up_bias, ("dp", "head"), scatter_dimension=0, tiled=True),
        lax.psum_scatter(grad_down_bias, ("dp", "head"), scatter_dimension=0, tiled=True),
        lax.psum_scatter(grad_gain1, ("dp", "head"), scatter_dimension=0, tiled=True),
        lax.psum_scatter(grad_gain2, ("dp", "head"), scatter_dimension=0, tiled=True),
    )
    return (
        result_block,
        grad_input,
        grad_rand,
        grad_value,
        gradient_output_weight,
        shared[4],
        shared[5],
        shared[0],
        shared[2],
        shared[1],
        shared[3],
    )


def solution(mesh):
    in_specs = (
        P("dp", "head", None),
        P("dp"),
        P("dp", "head", None),
        P(),
        P(None, "head"),
        P("head", None, None),
        P("head", None),
        P(),
        P(),
        P(),
        P(),
        P(),
    )
    out_specs = (
        P("dp", "head", None),
        P("dp", "head", None),
        P("head", "dp", None),
        P("dp", "head"),
        P("head", "dp"),
        P(("dp", "head")),
        P(("dp", "head")),
        P(None, ("dp", "head")),
        P(("dp", "head")),
        P(("dp", "head"), None),
        P(("dp", "head")),
    )
    return jax.shard_map(local, mesh=mesh, in_specs=in_specs, out_specs=out_specs, check_vma=False)
```

profile of v0, /device:TPU:0, one launch (start us, length us, event | category | flops | bytes accessed | tf_op | source)
XLA Modules:
  0.0 1075.9 jit_solution(14741107518014677063)
XLA Ops:
  13.5 12.4 %fusion.82 = (bf16[3,1024]{1,0:T(4,128)(2,1)S(1)}, f32[3,1024,1024]{2,1,0:T(8,128)}) fusion(bf16[3,1024,1024]{2,1,0:T(8,128)(2,1)} %param.25), kind=kLoop, calls=%fused_computation.120 | loop fusion | flops 6288384 | bytes 18880512 | tf_op jit(solution)/shard_map/reduce_max | solution.py:28
  28.3 24.6 %fusion.86 = (bf16[3,1024,1024]{2,1,0:T(8,128)(2,1)}, f32[3,1024,1024]{2,1,0:T(8,128)}) fusion(bf16[3,1024,1024]{2,1,0:T(8,128)(2,1)} %param.25, f32[3,1024]{1,0:T(4,128)S(1)} %reduce_max.25), kind=kOutput, calls=%fused_computation.122 | output fusion | flops 18878464 | bytes 25178112 | tf_op jit(solution)/shard_map/div | solution.py:29
  52.9 78.7 %all-gather.3.cloned.1.call-done = bf16[4,1024,768]{2,1,0:T(8,128)(2,1)} async-done(((bf16[4,256,768]{2,1,0:T(8,128)(2,1)}), bf16[4,1024,768]{2,1,0:T(8,128)(2,1)}) %all-gather.3.cloned.1.call-update) | async-done | bytes 6291472 | tf_op jit(solution)/shard_map/all_gather | solution.py:61
  139.0 27.0 %while.24 = (s32[]{:T(128)}, bf16[4,1024,3,64]{1,3,2,0:T(8,128)(2,1)}, pred[4]{0:T(512)(128)(4,1)S(1)}, bf16[4,1024,3,64]{1,3,2,0:T(8,128)(2,1)}, bf16[3,256,256...) while((s32[]{:T(128)}, bf16[4,1024,3,64]{1,3,2,0:T(8,128)(2,1)}, ...), condition=%wide.region_9.10_spmd, body=%wide.region_6.9_spmd.sunk | while | flops 402849792 | bytes 8650896 | solution.py:90
  172.3 113.3 %reduce-scatter.10.cloned.1.call-done = bf16[256,4,768]{2,0,1:T(8,128)(2,1)} async-done(((bf16[1024,4,768]{2,0,1:T(8,128)(2,1)}), bf16[256,4,768]{2,0,1:T(8,128)(2,1)}) %reduce-scatter.10.cloned.1.call-update) | async-done | bytes 1572880 | tf_op jit(solution)/shard_map/reduce_scatter | solution.py:96
  288.5 11.0 %fusion.29 = f32[4,256,3072]{2,1,0:T(8,128)} fusion(bf16[768,3072]{1,0:T(8,128)(2,1)} %param.28, f32[768]{0:T(1024)S(1)} %copy-done.18, f32[4,256]{1,0:T(4,128)S(1)} %add_rsqrt_fusion, f32[4,256]{1,0:T(4,128)S(1)} %broadcast_multiply_fusion.4, bf16[256,4,768]{2,0,1:T(8,128)(2,1)S(1)} %copy-done.3, bf16[4,256,768]{2,1,0:T(8,128)(2,1)S(1)} %copy-done.2), kind=kOutput, calls=%fused_computation.54 | convolution fusion | flops 4837343232 | bytes 20458496 | tf_op jit(solution)/shard_map/nqt,ty->nqy/dot_general | solution.py:111
  299.5 16.8 %convert_reduce_fusion = (f32[3072]{0:T(1024)}, bf16[4,256,3072]{2,1,0:T(8,128)(2,1)}) fusion(f32[4,256,3072]{2,1,0:T(8,128)} %fusion.29, f32[3072]{0:T(1024)S(1)} %copy-done.20, bf16[4,256,768]{2,1,0:T(8,128)(2,1)S(1)} %copy-done.8, bf16[3072,768]{1,0:T(8,128)(2,1)S(1)} %bitcast.148), kind=kOutput, calls=%fused_computation.33 | convolution fusion | flops 4904186880 | bytes 25190400 | tf_op jit(solution)/shard_map/iug,ag->iua/dot_general | solution.py:136
  328.9 115.6 %all-gather.5.cloned.1.call-done = bf16[4,1024,768]{2,1,0:T(8,128)(2,1)} async-done(((bf16[4,256,768]{2,1,0:T(8,128)(2,1)}), bf16[4,1024,768]{2,1,0:T(8,128)(2,1)}) %all-gather.5.cloned.1.call-update) | async-done | bytes 6291472 | tf_op jit(solution)/shard_map/all_gather | solution.py:158
  458.2 58.5 %while.25 = (s32[]{:T(128)}, f32[3,1024,1024]{2,1,0:T(8,128)}, f32[3,256,256]{2,1,0:T(8,128)S(1)}, bf16[4,1024,3,64]{1,3,2,0:T(8,128)(2,1)}, pred[4]{0:T(512)(12...) while((s32[]{:T(128)}, f32[3,1024,1024]{2,1,0:T(8,128)}, ...), condition=%wide.region_18.19_spmd, body=%wide.region_15.18_spmd.sunk | while | flops 808648704 | bytes 35389672 | solution.py:202
  460.6 15.0 %conditional.5 = (f32[3,1024,1024]{2,1,0:T(8,128)}, f32[3,256,256]{2,1,0:T(8,128)S(1)}, bf16[1,1024,3,64]{1,3,2,0:T(8,128)(2,1)S(1)}) conditional(s32[]{:T(128)} %bitcast.136, (bf16[1024,3,64]{0,2,1:T(8,128)(2,1)S(1)}, bf16[1024,3,64]{0,2,1:T(8,128)(2,1)S(1)}, f32[3,256,256]{2,1,0:T(8,128)S(1)}, bf16[3,256,256]{2,1,0:T(8,128)(2,1)S(1)}, ...), branch_computations={%region_16.16_spmd, %region_17.17_spmd} | conditional | flops 808648704 | bytes 33030168 | solution.py:195
  464.6 11.0 %convolution_add_fusion.1 = f32[3,1024,1024]{2,1,0:T(8,128)} fusion(f32[3,1024,1024]{2,1,0:T(8,128)} %get-tuple-element.109, bf16[1024,3,64]{0,2,1:T(8,128)(2,1)S(1)} %get-tuple-element.110, bf16[1024,3,64]{0,2,1:T(8,128)(2,1)S(1)} %get-tuple-element.111), kind=kOutput, calls=%fused_computation.15 | convolution fusion | flops 405798912 | bytes 25952256 | tf_op jit(solution)/shard_map/while/body/eval_jaxpr/cond/branch_1_fun/ihe,jhe->hij/dot_general | solution.py:178
  482.7 15.0 %conditional.5 = (f32[3,1024,1024]{2,1,0:T(8,128)}, f32[3,256,256]{2,1,0:T(8,128)S(1)}, bf16[1,1024,3,64]{1,3,2,0:T(8,128)(2,1)S(1)}) conditional(s32[]{:T(128)} %bitcast.136, (bf16[1024,3,64]{0,2,1:T(8,128)(2,1)S(1)}, bf16[1024,3,64]{0,2,1:T(8,128)(2,1)S(1)}, f32[3,256,256]{2,1,0:T(8,128)S(1)}, bf16[3,256,256]{2,1,0:T(8,128)(2,1)S(1)}, ...), branch_computations={%region_16.16_spmd, %region_17.17_spmd} | conditional | flops 808648704 | bytes 33030168 | solution.py:195
  486.7 11.0 %convolution_add_fusion.1 = f32[3,1024,1024]{2,1,0:T(8,128)} fusion(f32[3,1024,1024]{2,1,0:T(8,128)} %get-tuple-element.109, bf16[1024,3,64]{0,2,1:T(8,128)(2,1)S(1)} %get-tuple-element.110, bf16[1024,3,64]{0,2,1:T(8,128)(2,1)S(1)} %get-tuple-element.111), kind=kOutput, calls=%fused_computation.15 | convolution fusion | flops 405798912 | bytes 25952256 | tf_op jit(solution)/shard_map/while/body/eval_jaxpr/cond/branch_1_fun/ihe,jhe->hij/dot_general | solution.py:178
  500.9 15.0 %conditional.5 = (f32[3,1024,1024]{2,1,0:T(8,128)}, f32[3,256,256]{2,1,0:T(8,128)S(1)}, bf16[1,1024,3,64]{1,3,2,0:T(8,128)(2,1)S(1)}) conditional(s32[]{:T(128)} %bitcast.136, (bf16[1024,3,64]{0,2,1:T(8,128)(2,1)S(1)}, bf16[1024,3,64]{0,2,1:T(8,128)(2,1)S(1)}, f32[3,256,256]{2,1,0:T(8,128)S(1)}, bf16[3,256,256]{2,1,0:T(8,128)(2,1)S(1)}, ...), branch_computations={%region_16.16_spmd, %region_17.17_spmd} | conditional | flops 808648704 | bytes 33030168 | solution.py:195
  504.9 11.0 %convolution_add_fusion.1 = f32[3,1024,1024]{2,1,0:T(8,128)} fusion(f32[3,1024,1024]{2,1,0:T(8,128)} %get-tuple-element.109, bf16[1024,3,64]{0,2,1:T(8,128)(2,1)S(1)} %get-tuple-element.110, bf16[1024,3,64]{0,2,1:T(8,128)(2,1)S(1)} %get-tuple-element.111), kind=kOutput, calls=%fused_computation.15 | convolution fusion | flops 405798912 | bytes 25952256 | tf_op jit(solution)/shard_map/while/body/eval_jaxpr/cond/branch_1_fun/ihe,jhe->hij/dot_general | solution.py:178
  530.7 20.6 %add_convert_fusion = bf16[3,1024,1024]{2,1,0:T(8,128)(2,1)} fusion(f32[3,256,256]{2,1,0:T(8,128)} %subtract_multiply_fusion.1, f32[3,1024,1024]{2,1,0:T(8,128)} %get-tuple-element.195, f32[3,1024,1024]{2,1,0:T(8,128)} %get-tuple-element.144), kind=kOutput, calls=%fused_computation.34 | output fusion | flops 15732735 | bytes 32243712 | tf_op jit(solution)/shard_map/sub | solution.py:33
  558.7 12.9 %convolution_bitcast_fusion = f32[3072,768]{1,0:T(8,128)} fusion(bf16[4,256,768]{2,1,0:T(8,128)(2,1)S(1)} %copy-done.9, f32[4,256,3072]{2,1,0:T(8,128)} %fusion.29, f32[3072]{0:T(1024)S(1)} %copy-done.20), kind=kOutput, calls=%fused_computation.43 | convolution fusion | flops 4863295488 | bytes 23605248 | tf_op jit(solution)/shard_map/bma,bmj->aj/dot_general | solution.py:133
  573.0 13.0 %convolution_bitcast_fusion.1 = f32[768,3072]{0,1:T(8,128)} fusion(bf16[4,256,3072]{2,1,0:T(8,128)(2,1)} %get-tuple-element.198, f32[768]{0:T(1024)S(1)} %copy-done.18, f32[4,256]{1,0:T(4,128)S(1)} %add_rsqrt_fusion, f32[4,256]{1,0:T(4,128)S(1)} %broadcast_multiply_fusion.4, bf16[256,4,768]{2,0,1:T(8,128)(2,1)S(1)} %copy-done.4, ...), kind=kOutput, calls=%fused_computation.44 | convolution fusion | flops 4837343232 | bytes 18885632 | tf_op jit(solution)/shard_map/cqp,cqv->pv/dot_general | solution.py:143
  586.7 13.0 %add_convert_fusion.1 = bf16[4,256,768]{2,1,0:T(8,128)(2,1)} fusion(bf16[256,4,768]{2,0,1:T(8,128)(2,1)S(1)} %copy-done.4, bf16[4,256,768]{2,1,0:T(8,128)(2,1)S(1)} %copy-done.2, bf16[3072,768]{1,0:T(8,128)(2,1)} %param.30, f32[768]{0:T(1024)S(1)} %copy-done.21, f32[4,256,3072]{2,1,0:T(8,128)} %fusion.29, f32[3072]{0:T(1024)S(1)} %copy-done.20), kind=kOutput, calls=%fused_computation.79 | convolution fusion | flops 4868014080 | bytes 22035456 | tf_op jit(solution)/shard_map/uiq,qy->uiy/dot_general | solution.py:122
  607.7 63.5 %reduce-scatter.14.cloned.1.call-done = bf16[3,128,1024]{2,1,0:T(8,128)(2,1)} async-done(((bf16[3,1024,1024]{2,1,0:T(8,128)(2,1)}), bf16[3,128,1024]{2,1,0:T(8,128)(2,1)}) %reduce-scatter.14.cloned.1.call-update) | async-done | bytes 786448 | tf_op jit(solution)/shard_map/reduce_scatter | solution.py:231
  673.7 110.7 %reduce-scatter.12.cloned.1.call-done = bf16[256,4,768]{2,0,1:T(8,128)(2,1)} async-done(((bf16[1024,4,768]{2,0,1:T(8,128)(2,1)}), bf16[256,4,768]{2,0,1:T(8,128)(2,1)}) %reduce-scatter.12.cloned.1.call-update) | async-done | bytes 1572880 | tf_op jit(solution)/shard_map/reduce_scatter | solution.py:212
  793.4 41.1 %all-reduce.7 = (f32[768]{0:T(1024)S(1)}, f32[768]{0:T(1024)S(1)}, f32[3072]{0:T(1024)S(1)}, f32[768]{0:T(1024)S(1)}) all-reduce(f32[768]{0:T(1024)S(1)} %get-tuple-element.148, f32[768]{0:T(1024)S(1)} %get-tuple-element.146, f32[3072]{0:T(1024)S(1)} %copy-done.19, ...), channel_id=7, replica_groups=mesh['dp'=8,'head'=4] {'dp','head'}, use_global_device_ids=true, to_apply=%region_28.29.clone | all-reduce | flops 5376 | bytes 43008
  836.8 91.3 %reduce-scatter.20.cloned.1.call-done = f32[96,768]{1,0:T(8,128)} async-done(((f32[3072,768]{1,0:T(8,128)}), f32[96,768]{1,0:T(8,128)}) %reduce-scatter.20.cloned.1.call-update) | async-done | bytes 294928 | tf_op jit(solution)/shard_map/reduce_scatter | solution.py:243
  928.1 141.1 %reduce-scatter.18.cloned.1.call-done = f32[768,96]{0,1:T(8,128)} async-done(((f32[768,3072]{0,1:T(8,128)}), f32[768,96]{0,1:T(8,128)}) %reduce-scatter.18.cloned.1.call-update) | async-done | bytes 294928 | tf_op jit(solution)/shard_map/reduce_scatter | solution.py:242
  (155 shorter events, 158.8 us)
Async XLA Ops:
  7.2 158.9 %copy-start = (bf16[192,768]{1,0:T(8,128)(2,1)S(1)}, bf16[192,768]{1,0:T(8,128)(2,1)}, u32[]{:S(2)}) copy-start(bf16[192,768]{1,0:T(8,128)(2,1)} %param.26) | copy-start | bytes 884740
  7.2 124.4 %all-gather.3.cloned.1.call-start = ((), (), s32[]{:S(2)}) async-start(), calls=%async_computation.7 | async-start | bytes 7864320 | tf_op jit(solution)/shard_map/all_gather | solution.py:61
  13.4 272.2 %reduce-scatter.10.cloned.1.call-start = ((), (), s32[]{:S(2)}) async-start(), calls=%async_computation.8 | async-start | bytes 7864320 | tf_op jit(solution)/shard_map/reduce_scatter | solution.py:96
  13.4 12.4 %copy-start.22 = (s32[4]{0:T(128)S(1)}, s32[4]{0:T(128)}, u32[]{:S(2)}) copy-start(s32[4]{0:T(128)} %param.21) | copy-start | bytes 52
  28.3 103.3 %copy-start.10 = (bf16[768,192]{0,1:T(8,128)(2,1)S(1)}, bf16[768,192]{0,1:T(8,128)(2,1)}, u32[]{:S(2)}) copy-start(bf16[768,192]{0,1:T(8,128)(2,1)} %param.24) | copy-start | bytes 884740
  172.0 116.4 %copy-start.18 = (f32[768]{0:T(1024)S(1)}, f32[768]{0:T(1024)}, u32[]{:S(2)}) copy-start(f32[768]{0:T(1024)} %param.27) | copy-start | bytes 9220
  172.0 272.4 %all-gather.5.cloned.1.call-start = ((), (), s32[]{:S(2)}) async-start(), calls=%async_computation.9 | async-start | bytes 7864320 | tf_op jit(solution)/shard_map/all_gather | solution.py:158
  287.6 11.8 %slice-start.2 = ((s8[4718592]{0:T(1024)(128)(4,1)}), s8[4194304]{0:T(1024)(128)(4,1)S(1)}, s32[]{:S(2)}) async-start(s8[4718592]{0:T(1024)(128)(4,1)} %bitcast.147), calls=%async_computation.18 | async-start | bytes 8388608
  288.4 11.0 %copy-start.8 = (bf16[4,256,768]{2,1,0:T(8,128)(2,1)S(1)}, bf16[4,256,768]{2,1,0:T(8,128)(2,1)}, u32[]{:S(2)}) copy-start(bf16[4,256,768]{2,1,0:T(8,128)(2,1)} %param.22) | copy-start | bytes 4718596
  288.5 11.0 %slice-start.3 = ((s8[4718592]{0:T(1024)(128)(4,1)}), s8[524288]{0:T(1024)(128)(4,1)S(1)}, s32[]{:S(2)}) async-start(s8[4718592]{0:T(1024)(128)(4,1)} %bitcast.147), calls=%async_computation.19 | async-start | bytes 1048576
  288.5 11.0 %copy-start.20 = (f32[3072]{0:T(1024)S(1)}, f32[3072]{0:T(1024)}, u32[]{:S(2)}) copy-start(f32[3072]{0:T(1024)} %param.29) | copy-start | bytes 36868
  288.5 27.9 %slice-start = ((s8[4718592]{0:T(1024)(128)(4,1)}), s8[4194304]{0:T(1024)(128)(4,1)S(1)}, s32[]{:S(2)}) async-start(s8[4718592]{0:T(1024)(128)(4,1)} %bitcast.145), calls=%async_computation.16 | async-start | bytes 8388608
  299.5 16.9 %slice-start.1 = ((s8[4718592]{0:T(1024)(128)(4,1)}), s8[524288]{0:T(1024)(128)(4,1)S(1)}, s32[]{:S(2)}) async-start(s8[4718592]{0:T(1024)(128)(4,1)} %bitcast.145), calls=%async_computation.17 | async-start | bytes 1048576
  328.4 271.3 %reduce-scatter.22.cloned.1.call-start = ((), (), s32[]{:S(2)}) async-start(), calls=%async_computation.15 | async-start | bytes 442368
  522.3 84.0 %reduce-scatter.16.cloned.1.call-start = ((), (), s32[]{:S(2)}) async-start(), calls=%async_computation.12 | async-start | bytes 442368 | tf_op jit(solution)/shard_map/reduce_scatter | solution.py:234
  530.6 140.6 %reduce-scatter.14.cloned.1.call-start = ((), (), s32[]{:S(2)}) async-start(), calls=%async_computation.11 | async-start | bytes 7077888 | tf_op jit(solution)/shard_map/reduce_scatter | solution.py:231
  551.3 233.1 %reduce-scatter.12.cloned.1.call-start = ((), (), s32[]{:S(2)}) async-start(), calls=%async_computation.10 | async-start | bytes 7864320 | tf_op jit(solution)/shard_map/reduce_scatter | solution.py:212
  557.4 370.7 %reduce-scatter.20.cloned.1.call-start = ((), (), s32[]{:S(2)}) async-start(), calls=%async_computation.14 | async-start | bytes 9732096 | tf_op jit(solution)/shard_map/reduce_scatter | solution.py:243
  571.6 497.6 %reduce-scatter.18.cloned.1.call-start = ((), (), s32[]{:S(2)}) async-start(), calls=%async_computation.13 | async-start | bytes 9732096 | tf_op jit(solution)/shard_map/reduce_scatter | solution.py:242
  586.7 197.7 %copy-start.13 = (f32[4,256]{1,0:T(4,128)S(1)}, f32[4,256]{1,0:T(4,128)}, u32[]{:S(2)}) copy-start(f32[4,256]{1,0:T(4,128)} %copy-done.12) | copy-start | bytes 12292
  586.7 197.7 %copy-start.15 = (f32[4,256]{1,0:T(4,128)S(1)}, f32[4,256]{1,0:T(4,128)}, u32[]{:S(2)}) copy-start(f32[4,256]{1,0:T(4,128)} %copy-done.14) | copy-start | bytes 12292
  586.7 197.7 %copy-start.17 = (f32[768]{0:T(1024)S(1)}, f32[768]{0:T(1024)}, u32[]{:S(2)}) copy-start(f32[768]{0:T(1024)} %param.23) | copy-start | bytes 9220
  787.9 281.3 %copy-start.1 = (bf16[192,768]{1,0:T(8,128)(2,1)S(1)}, bf16[192,768]{1,0:T(8,128)(2,1)}, u32[]{:S(2)}) copy-start(bf16[192,768]{1,0:T(8,128)(2,1)} %param.26) | copy-start | bytes 884740
  788.0 5.4 copy-start.19
  (12 other events, 25.1 us)
Sparse Core Ops, SparseCore 0:
  13.5 118.0 all-gather.2
  172.2 113.4 reduce-scatter.9
  328.5 115.8 all-gather.4
  522.5 46.4 reduce-scatter.21
  572.4 33.8 reduce-scatter.15
  609.5 61.7 reduce-scatter.13
  673.7 110.7 reduce-scatter.11
  791.9 136.1 reduce-scatter.19
  934.6 134.6 reduce-scatter.17
where the time goes:
time: 1090 us; the launch traced here: 1080 us
  waiting for transfers between devices  719 us (66%)
  matrix products  168 us (15%)
  other arithmetic  86.6 us (8%)
  blocking collectives  41.1 us (4%)
  local copies, waits for them, and re-layouts  39.7 us (4%)
  between operations  14.3 us (1%)
    reduce_scatter x1, waiting for transfers between devices, local(): lax.psum_scatter(gradient_up_weight, ('dp', 'head'), scatter_dimension=1,...  141 us
    all_gather x1, waiting for transfers between devices, local(): lax.all_gather(grad_attended, 'head', axis=1, tiled=True)  116 us
    reduce_scatter x1, waiting for transfers between devices, local(): lax.psum_scatter(jnp.einsum('lse,ed->lsd', rows_in, output_projection_wei...  113 us
    reduce_scatter x1, waiting for transfers between devices, local(): lax.psum_scatter(jnp.einsum('lse,de->lsd', rows_in, value_projection_weig...  111 us
    reduce_scatter x1, waiting for transfers between devices, local(): lax.psum_scatter(gradient_down_weight, ('dp', 'head'), scatter_dimension=...  91.3 us
    all_gather x1, waiting for transfers between devices, local(): combined_norm = lax.all_gather(norm1_low, 'head', axis=1, tiled=True)  78.7 us
    reduce_scatter x1, waiting for transfers between devices, local(): lax.psum_scatter(local_rand.astype(jnp.bfloat16), 'dp', scatter_dimension...  63.5 us
    unnamed x1, blocking collectives  41.1 us
  transfers between devices with their start and end apart: 9, of which 8 were waited for; matrix products, arithmetic and copies ran while one was open for 12% of the time, Pallas kernels for 0%

commit v1 on v0

v1 whole, which is shorter than its diff:
```python
import functools

import jax
import jax.numpy as jnp
from jax import lax
from jax.experimental import pallas as pl
from jax.experimental.pallas import tpu as pltpu
from jax.sharding import PartitionSpec as P

SHORT = 256
EPSILON = 1e-05
F32 = jnp.float32
BF16 = jnp.bfloat16
VMEM_LIMIT = 60 * 1024 * 1024
GELU_C = 0.7978845608028654
GELU_A = 0.044715


def dot_nn(a, b):
    return lax.dot_general(a, b, (((1,), (0,)), ((), ())), preferred_element_type=F32)


def dot_nt(a, b):
    return lax.dot_general(a, b, (((1,), (1,)), ((), ())), preferred_element_type=F32)


def dot_tn(a, b):
    return lax.dot_general(a, b, (((0,), (0,)), ((), ())), preferred_element_type=F32)


def norm_of(value):
    centered = value - jnp.mean(value, -1, keepdims=True)
    inverse = lax.rsqrt(jnp.mean(centered * centered, -1, keepdims=True) + EPSILON)
    return centered * inverse, inverse


def norm_back(scaled, hat, inverse):
    return inverse * (
        scaled
        - jnp.mean(scaled, -1, keepdims=True)
        - hat * jnp.mean(scaled * hat, -1, keepdims=True)
    )


def interleave(values, heads, size):
    parts = []
    for head in range(heads):
        for value in values:
            parts.append(value[:, head * size : (head + 1) * size])
    return jnp.concatenate(parts, axis=1)


def separate(piece, seq, count, heads, size):
    parts = []
    for head in range(heads):
        at = (head * count + seq) * size
        parts.append(piece[:, at : at + size])
    return jnp.concatenate(parts, axis=1)


def whole(shape):
    return pl.BlockSpec(shape, lambda *_: (0,) * len(shape))


def cost(flops, moved, special=0):
    return pl.CostEstimate(
        flops=int(flops), bytes_accessed=int(moved), transcendentals=int(special)
    )


def params(grid_dims=1):
    return pltpu.CompilerParams(
        dimension_semantics=("arbitrary",) * grid_dims, vmem_limit_bytes=VMEM_LIMIT
    )


def probs_kernel(logit_ref, long_ref, long_t_ref, short_ref, short_t_ref):
    logits = logit_ref[0].astype(F32)
    raised = jnp.exp(logits - jnp.max(logits, -1, keepdims=True))
    probs = raised / jnp.sum(raised, -1, keepdims=True)
    long_ref[0] = probs.astype(BF16)
    long_t_ref[0] = probs.T.astype(BF16)

    @pl.when(pl.program_id(1) == 0)
    def _():
        corner = logits[:, :SHORT]
        lifted = jnp.exp(corner - jnp.max(corner, -1, keepdims=True))
        part = lifted / jnp.sum(lifted, -1, keepdims=True)
        short_ref[0] = part.astype(BF16)
        short_t_ref[0] = part.T.astype(BF16)


def make_probs(logits):
    heads, rows, _ = logits.shape
    return pl.pallas_call(
        probs_kernel,
        grid=(heads, rows // SHORT),
        in_specs=[pl.BlockSpec((1, SHORT, rows), lambda h, i: (h, i, 0))],
        out_specs=[
            pl.BlockSpec((1, SHORT, rows), lambda h, i: (h, i, 0)),
            pl.BlockSpec((1, rows, SHORT), lambda h, i: (h, 0, i)),
            pl.BlockSpec((1, SHORT, SHORT), lambda h, i: (h, 0, 0)),
            pl.BlockSpec((1, SHORT, SHORT), lambda h, i: (h, 0, 0)),
        ],
        out_shape=[
            jax.ShapeDtypeStruct((heads, rows, rows), BF16),
            jax.ShapeDtypeStruct((heads, rows, rows), BF16),
            jax.ShapeDtypeStruct((heads, SHORT, SHORT), BF16),
            jax.ShapeDtypeStruct((heads, SHORT, SHORT), BF16),
        ],
        compiler_params=params(2),
        cost_estimate=cost(10 * logits.size, 6 * logits.size, logits.size),
        name="probs",
    )(logits)


def values_kernel(zones, heads, size, place_ref, x_ref, gain_ref, both_ref, *rest):
    outs, weight_ref = rest[:zones], rest[zones]
    width = heads * size
    for d in range(zones):
        other = lax.rem(place_ref[0] + d, zones)
        weight_ref[d * width : (d + 1) * width, :] = both_ref[other, :width, :]
    made = []
    for seq in range(x_ref.shape[0]):
        hat, _ = norm_of(x_ref[seq].astype(F32))
        norm = (hat * gain_ref[...]).astype(BF16)
        made.append(dot_nt(norm, weight_ref[...]))
    for d in range(zones):
        mine = [value[:, d * width : (d + 1) * width] for value in made]
        outs[d][...] = interleave(mine, heads, size).astype(BF16)


def make_values(place, x, gain, both, heads):
    count, rows, depth = x.shape
    zones, twice, _ = both.shape
    size = twice // 2 // heads
    wide = heads * count * size
    return pl.pallas_call(
        functools.partial(values_kernel, zones, heads, size),
        grid_spec=pltpu.PrefetchScalarGridSpec(
            num_scalar_prefetch=1,
            grid=(1,),
            in_specs=[whole(x.shape), whole(gain.shape), whole(both.shape)],
            out_specs=[whole((rows, wide))] * zones,
            scratch_shapes=[pltpu.VMEM((zones * heads * size, depth), BF16)],
        ),
        out_shape=[jax.ShapeDtypeStruct((rows, wide), BF16)] * zones,
        compiler_params=params(),
        cost_estimate=cost(2 * count * rows * depth * depth, 2 * x.size * 2 + both.size * 2),
        name="values",
    )(place, x, gain, both)


def mix_kernel(zones, count, size, rows, sign, place_ref, long_flags, *refs):
    pieces = refs[:zones]
    matrix_ref, corner_ref = refs[zones], refs[zones + 1]
    outs = refs[zones + 2 : 2 * zones + 2]
    held = refs[2 * zones + 2]
    place = place_ref[0]
    for d in range(zones):
        source = lax.rem(place + zones - sign * d, zones)
        held[pl.ds(pl.multiple_of(source * rows, rows), rows), :] = pieces[d][...]
    lane = lax.broadcasted_iota(jnp.int32, (1, count * size), 1)
    is_long = jnp.zeros((1, count * size), jnp.bool_)
    for seq in range(count):
        inside = (lane >= seq * size) & (lane < (seq + 1) * size)
        is_long = is_long | (inside & (long_flags[seq] > SHORT))
    corner = dot_nn(corner_ref[0], held[:SHORT, :])
    for d in range(zones):
        target = lax.rem(place + zones + sign * d, zones)
        part = matrix_ref[0, pl.ds(pl.multiple_of(target * rows, rows), rows), :]
        full = dot_nn(part, held[...])
        small = jnp.where(target == 0, corner, jnp.zeros_like(corner))
        outs[d][...] = jnp.where(is_long, full, small).astype(BF16)


def mix(place, lengths, pieces, matrix, corner, count, sign):
    zones = len(pieces)
    heads, full, _ = matrix.shape
    rows, wide = pieces[0].shape
    lanes = wide // heads
    spec = pl.BlockSpec((rows, lanes), lambda h, *_: (0, h))
    return pl.pallas_call(
        functools.partial(mix_kernel, zones, count, lanes // count, rows, sign),
        grid_spec=pltpu.PrefetchScalarGridSpec(
            num_scalar_prefetch=2,
            grid=(heads,),
            in_specs=[spec] * zones
            + [
                pl.BlockSpec((1, full, full), lambda h, *_: (h, 0, 0)),
                pl.BlockSpec((1, SHORT, SHORT), lambda h, *_: (h, 0, 0)),
            ],
            out_specs=[spec] * zones,
            scratch_shapes=[pltpu.VMEM((full, lanes), BF16)],
        ),
        out_shape=[jax.ShapeDtypeStruct((rows, wide), BF16)] * zones,
        compiler_params=params(),
        cost_estimate=cost(
            2 * heads * full * full * lanes, 2 * heads * full * full + 4 * full * wide
        ),
        name="mix",
    )(place, lengths, *pieces, matrix, corner)


def feed_kernel(zones, heads, size, steps, place_ref, *refs):
    pieces = refs[:zones]
    (x_ref, cot_ref, both_ref, gain_ref, up_ref, up_bias_ref, down_ref, down_bias_ref) = refs[
        zones : zones + 8
    ]
    outs = refs[zones + 8 :]
    grads = outs[:zones]
    (
        block_ref,
        resid_grad_ref,
        act_t_ref,
        pre_t_ref,
        norm_ref,
        mixed_ref,
        attended_ref,
        up_sum_ref,
        sums_ref,
        weight_ref,
        resid_ref,
        hat_ref,
        inv_ref,
        forward_ref,
        back_ref,
    ) = outs[zones:]
    count, rows, depth = x_ref.shape
    width = heads * size
    step = pl.program_id(0)

    @pl.when(step == 0)
    def _():
        for d in range(zones):
            other = lax.rem(place_ref[0] + zones - d, zones)
            weight_ref[d * width : (d + 1) * width, :] = both_ref[other, width:, :]
        for seq in range(count):
            at = slice(seq * rows, (seq + 1) * rows)
            mixed = jnp.concatenate(
                [separate(piece[...], seq, count, heads, size) for piece in pieces], axis=1
            )
            mixed_ref[at, :] = mixed
            resid = x_ref[seq].astype(F32) + dot_nn(mixed, weight_ref[...])
            hat, inverse = norm_of(resid)
            resid_ref[at, :] = resid + down_bias_ref[...]
            hat_ref[at, :] = hat
            inv_ref[at, :] = inverse
            norm_ref[at, :] = (hat * gain_ref[...]).astype(BF16)

    up_sum = jnp.zeros((1, up_ref.shape[1]), F32)
    for seq in range(count):
        at = slice(seq * rows, (seq + 1) * rows)
        pre = dot_nn(norm_ref[at, :], up_ref[...]) + up_bias_ref[...]
        grad_act = dot_nt(cot_ref[seq], down_ref[...])
        square = pre * pre
        bent = jnp.tanh(pre * (GELU_C + (GELU_C * GELU_A) * square))
        half = 0.5 + 0.5 * bent
        act = (pre * half).astype(BF16)
        slope = half + (0.5 * pre) * (1.0 - bent * bent) * (
            GELU_C + (3.0 * GELU_C * GELU_A) * square
        )
        grad_pre = (grad_act * slope).astype(BF16)
        up_sum = up_sum + jnp.sum(grad_pre.astype(F32), 0, keepdims=True)
        act_t_ref[:, at] = act.T
        pre_t_ref[:, at] = grad_pre.T
        forward = dot_nn(act, down_ref[...])
        back = dot_nt(grad_pre, up_ref[...])

        @pl.when(step == 0)
        def _():
            forward_ref[at, :] = forward
            back_ref[at, :] = back

        @pl.when(step > 0)
        def _():
            forward_ref[at, :] += forward
            back_ref[at, :] += back

    up_sum_ref[...] = up_sum

    @pl.when(step == steps - 1)
    def _():
        gain_sum = jnp.zeros((1, depth), F32)
        bias_sum = jnp.zeros((1, depth), F32)
        made = []
        for seq in range(count):
            at = slice(seq * rows, (seq + 1) * rows)
            block_ref[seq] = (resid_ref[at, :] + forward_ref[at, :]).astype(BF16)
            cot = cot_ref[seq].astype(F32)
            hat = hat_ref[at, :]
            back = back_ref[at, :]
            gain_sum = gain_sum + jnp.sum(back * hat, 0, keepdims=True)
            bias_sum = bias_sum + jnp.sum(cot, 0, keepdims=True)
            grad = cot + norm_back(back * gain_ref[...], hat, inv_ref[at, :])
            resid_grad_ref[at, :] = grad
            low = grad.astype(BF16)
            attended_ref[at, :] = low
            made.append(dot_nt(low, weight_ref[...]))
        sums_ref[0:1, :] = gain_sum
        sums_ref[1:2, :] = bias_sum
        for d in range(zones):
            mine = [value[:, d * width : (d + 1) * width] for value in made]
            grads[d][...] = interleave(mine, heads, size).astype(BF16)


def feed(place, pieces, x, cot, both, gain, up, up_bias, down, down_bias, heads):
    zones = len(pieces)
    count, rows, depth = x.shape
    size = both.shape[1] // 2 // heads
    hidden = up.shape[1]
    tile = min(512, hidden)
    steps = hidden // tile
    tokens = count * rows
    wide = pieces[0].shape[1]
    shapes = [jax.ShapeDtypeStruct((rows, wide), BF16)] * zones + [
        jax.ShapeDtypeStruct((count, rows, depth), BF16),
        jax.ShapeDtypeStruct((tokens, depth), F32),
        jax.ShapeDtypeStruct((hidden, tokens), BF16),
        jax.ShapeDtypeStruct((hidden, tokens), BF16),
        jax.ShapeDtypeStruct((tokens, depth), BF16),
        jax.ShapeDtypeStruct((tokens, depth), BF16),
        jax.ShapeDtypeStruct((tokens, depth), BF16),
        jax.ShapeDtypeStruct((1, hidden), F32),
        jax.ShapeDtypeStruct((2, depth), F32),
    ]
    return pl.pallas_call(
        functools.partial(feed_kernel, zones, heads, size, steps),
        grid_spec=pltpu.PrefetchScalarGridSpec(
            num_scalar_prefetch=1,
            grid=(steps,),
            in_specs=[whole((rows, wide))] * zones
            + [
                whole(x.shape),
                whole(cot.shape),
                whole(both.shape),
                whole(gain.shape),
                pl.BlockSpec((depth, tile), lambda f, *_: (0, f)),
                pl.BlockSpec((1, tile), lambda f, *_: (0, f)),
                pl.BlockSpec((tile, depth), lambda f, *_: (f, 0)),
                whole(down_bias.shape),
            ],
            out_specs=[whole((rows, wide))] * zones
            + [
                whole((count, rows, depth)),
                whole((tokens, depth)),
                pl.BlockSpec((tile, tokens), lambda f, *_: (f, 0)),
                pl.BlockSpec((tile, tokens), lambda f, *_: (f, 0)),
                whole((tokens, depth)),
                whole((tokens, depth)),
                whole((tokens, depth)),
                pl.BlockSpec((1, tile), lambda f, *_: (0, f)),
                whole((2, depth)),
            ],
            scratch_shapes=[
                pltpu.VMEM((depth, depth), BF16),
                pltpu.VMEM((tokens, depth), F32),
                pltpu.VMEM((tokens, depth), F32),
                pltpu.VMEM((tokens, 1), F32),
                pltpu.VMEM((tokens, depth), F32),
                pltpu.VMEM((tokens, depth), F32),
            ],
        ),
        out_shape=shapes,
        compiler_params=params(),
        cost_estimate=cost(
            8 * tokens * depth * hidden + 4 * tokens * depth * depth,
            4 * depth * hidden + 4 * tokens * hidden + 20 * tokens * depth,
            tokens * hidden,
        ),
        name="feed",
    )(place, *pieces, x, cot, both, gain, up, up_bias, down, down_bias)


def block_order(ranks):
    return [first + 2 * second + 8 * third
            for first in range(2) for second in range(4) for third in range(ranks // 8)]


def relative_block(step, odd, ranks):
    rest = ranks // 8
    return odd + 2 * (step // rest) + 8 * lax.rem(step, rest)


def weights_kernel(zones, chunks, place_ref, *refs):
    acts, pres = refs[:chunks], refs[chunks : 2 * chunks]
    norms, cots = refs[2 * chunks : 3 * chunks], refs[3 * chunks : 4 * chunks]
    out_ref, scratch_ref = refs[4 * chunks], refs[4 * chunks + 1]
    part = scratch_ref.shape[1] // zones
    up = dot_nn(pres[0][...], norms[0][...])
    down = dot_nn(acts[0][...], cots[0][...])
    for c in range(1, chunks):
        up = up + dot_nn(pres[c][...], norms[c][...])
        down = down + dot_nn(acts[c][...], cots[c][...])
    scratch_ref[0] = up
    scratch_ref[1] = down
    for d in range(zones):
        at = pl.multiple_of(lax.rem(place_ref[0] + d, zones) * part, 8)
        for side in range(2):
            out_ref[0, d, side] = scratch_ref[side, pl.ds(at, part), :].astype(BF16)


def weight_grads(place, acts, pres, norms, cots, odd, zones, ranks):
    chunks = len(acts)
    hidden, tokens = acts[0].shape
    depth = norms[0].shape[1]
    tile = hidden // ranks

    def tall(step, place_ref):
        return (lax.bitwise_xor(place_ref[1], relative_block(step, odd, ranks)), 0)

    return pl.pallas_call(
        functools.partial(weights_kernel, zones, chunks),
        grid_spec=pltpu.PrefetchScalarGridSpec(
            num_scalar_prefetch=1,
            grid=(ranks // 2,),
            in_specs=[pl.BlockSpec((tile, tokens), tall)] * (2 * chunks)
            + [whole((tokens, depth))] * (2 * chunks),
            out_specs=pl.BlockSpec(
                (1, zones, 2, tile // zones, depth), lambda s, *_: (s, 0, 0, 0, 0)
            ),
            scratch_shapes=[pltpu.VMEM((2, tile, depth), F32)],
        ),
        out_shape=jax.ShapeDtypeStruct((ranks // 2, zones, 2, tile // zones, depth), BF16),
        compiler_params=params(),
        cost_estimate=cost(
            2 * chunks * hidden * tokens * depth,
            2 * chunks * hidden * tokens + 2 * hidden * depth + 4 * chunks * tokens * depth,
        ),
        name="weights",
    )(place, *acts, *pres, *norms, *cots)


def store_square(place_ref, out_ref, scratch_ref, extra_ref, zones, ranks):
    depth, columns = scratch_ref.shape
    part, width = depth // ranks, columns // zones
    for number, relative in enumerate(block_order(ranks)):
        rank = lax.bitwise_xor(place_ref[1], relative)
        block = scratch_ref[pl.ds(pl.multiple_of(rank * part, 8), part), :]
        for d in range(zones):
            out_ref[number, d, :part, :] = block[:, d * width : (d + 1) * width].astype(BF16)
            zone = lax.rem(place_ref[0] + d, zones)
            line = extra_ref[pl.ds(rank * zones + zone, 1), :]
            out_ref[number, d, part:, :] = jnp.broadcast_to(
                line, (out_ref.shape[2] - part, width)
            ).astype(BF16)


def square_rows(depth, ranks):
    part = depth // ranks
    return -(-part // 16) * 16 + 16 if part % 16 else part + 16


def out_weight_kernel(zones, ranks, chunks, place_ref, *refs):
    grads, mixes = refs[:chunks], refs[chunks : 2 * chunks]
    extra_ref, out_ref, scratch_ref = refs[2 * chunks :]
    total = dot_tn(grads[0][...], mixes[0][...])
    for c in range(1, chunks):
        total = total + dot_tn(grads[c][...], mixes[c][...])
    scratch_ref[...] = total
    store_square(place_ref, out_ref, scratch_ref, extra_ref, zones, ranks)


def out_weight_grads(place, grads, mixes, extra, zones, ranks):
    chunks = len(grads)
    tokens, depth = grads[0].shape
    shape = (ranks, zones, depth // ranks + 16, depth // zones)
    return pl.pallas_call(
        functools.partial(out_weight_kernel, zones, ranks, chunks),
        grid_spec=pltpu.PrefetchScalarGridSpec(
            num_scalar_prefetch=1,
            grid=(1,),
            in_specs=[whole((tokens, depth))] * (2 * chunks) + [whole(extra.shape)],
            out_specs=whole(shape),
            scratch_shapes=[pltpu.VMEM((depth, depth), F32)],
        ),
        out_shape=jax.ShapeDtypeStruct(shape, BF16),
        compiler_params=params(),
        cost_estimate=cost(
            2 * chunks * tokens * depth * depth, 4 * chunks * tokens * depth + 2 * depth * depth
        ),
        name="out_weight",
    )(place, *grads, *mixes, extra)


def logits_kernel(
    zones, chunks, count, heads, size, rows, odd, ranks, place_ref, lengths_ref, *refs
):
    grads = refs[: chunks * zones]
    values = refs[chunks * zones : 2 * chunks * zones]
    logit_ref, out_ref, long_ref, short_ref, value_ref = refs[2 * chunks * zones :]
    place = place_ref[0]
    lanes = count * size
    step = pl.program_id(0)

    @pl.when(step == 0)
    def _():
        lane = lax.broadcasted_iota(jnp.int32, (1, lanes), 1)
        for c in range(chunks):
            is_long = jnp.zeros((1, lanes), jnp.bool_)
            for seq in range(count):
                inside = (lane >= seq * size) & (lane < (seq + 1) * size)
                is_long = is_long | (inside & (lengths_ref[c * count + seq] > SHORT))
            for d in range(zones):
                ahead = lax.rem(place + d, zones)
                behind = lax.rem(place + zones - d, zones)
                to = pl.ds(pl.multiple_of(ahead * rows, rows), rows)
                back = pl.ds(pl.multiple_of(behind * rows, rows), rows)
                for head in range(heads):
                    columns = slice(head * lanes, (head + 1) * lanes)
                    own = slice(c * lanes, (c + 1) * lanes)
                    grad = grads[c * zones + d][:, columns].astype(F32)
                    long_ref[head, to, own] = jnp.where(is_long, grad, 0.0).astype(BF16)
                    value_ref[head, back, own] = values[c * zones + d][:, columns]

                    @pl.when(ahead == 0)
                    def _():
                        short_ref[head, :, own] = jnp.where(is_long, 0.0, grad).astype(BF16)

    rank = lax.bitwise_xor(place_ref[1], relative_block(step, odd, ranks))
    part = out_ref.shape[2]
    start = rank * part
    for head in range(heads):
        logits = logit_ref[head].astype(F32)
        raised = jnp.exp(logits - jnp.max(logits, -1, keepdims=True))
        probs = raised / jnp.sum(raised, -1, keepdims=True)
        at = pl.ds(pl.multiple_of(start, part), part)
        total = dot_nt(long_ref[head, at, :], value_ref[head])
        out = probs * (total - jnp.sum(total * probs, -1, keepdims=True))
        out_ref[0, head] = out.astype(BF16)

        @pl.when(start < SHORT)
        def _():
            corner = logits[:, :SHORT]
            lifted = jnp.exp(corner - jnp.max(corner, -1, keepdims=True))
            small = lifted / jnp.sum(lifted, -1, keepdims=True)
            sums = dot_nt(short_ref[head, at, :], value_ref[head, :SHORT, :])
            more = small * (sums - jnp.sum(sums * small, -1, keepdims=True))
            out_ref[0, head, :, :SHORT] = (out[:, :SHORT] + more).astype(BF16)


def logit_grads(place, lengths, grads, values, logits, odd, ranks, count):
    chunks, zones = len(grads), len(grads[0])
    heads, full, _ = logits.shape
    rows, wide = grads[0][0].shape
    size = wide // heads // count
    part = full // ranks

    def pick(step, place_ref, _):
        return (0, lax.bitwise_xor(place_ref[1], relative_block(step, odd, ranks)), 0)

    flat = [piece for group in grads for piece in group] + [
        piece for group in values for piece in group
    ]
    every = chunks * count * size
    return pl.pallas_call(
        functools.partial(
            logits_kernel, zones, chunks, count, heads, size, rows, odd, ranks
        ),
        grid_spec=pltpu.PrefetchScalarGridSpec(
            num_scalar_prefetch=2,
            grid=(ranks // 2,),
            in_specs=[whole((rows, wide))] * len(flat)
            + [pl.BlockSpec((heads, part, full), pick)],
            out_specs=pl.BlockSpec((1, heads, part, full), lambda s, *_: (s, 0, 0, 0)),
            scratch_shapes=[
                pltpu.VMEM((heads, full, every), BF16),
                pltpu.VMEM((heads, SHORT, every), BF16),
                pltpu.VMEM((heads, full, every), BF16),
            ],
        ),
        out_shape=jax.ShapeDtypeStruct((ranks // 2, heads, part, full), BF16),
        compiler_params=params(),
        cost_estimate=cost(
            heads * full * full * every, 2 * heads * full * full, heads * full * full // 2
        ),
        name="logits",
    )(place, lengths, *flat, logits)


def input_kernel(zones, heads, size, ranks, first, last, place_ref, *refs):
    pieces = refs[:zones]
    x_ref, gain_ref, both_ref, resid_ref = refs[zones : zones + 4]
    refs = refs[zones + 4 :]
    if not first:
        old_ref, old_gain_ref = refs[:2]
        refs = refs[2:]
    grad_ref, total_ref = refs[:2]
    refs = refs[2:]
    if not last:
        gain_out_ref = refs[0]
        refs = refs[1:]
    weight_ref, norm_ref, back_ref = refs[:3]
    count, rows, depth = x_ref.shape
    width = heads * size
    for d in range(zones):
        other = lax.rem(place_ref[0] + d, zones)
        weight_ref[d * width : (d + 1) * width, :] = both_ref[other, :width, :]
    gain_sum = jnp.zeros((1, depth), F32) if first else old_gain_ref[...]
    for seq in range(count):
        at = slice(seq * rows, (seq + 1) * rows)
        hat, inverse = norm_of(x_ref[seq].astype(F32))
        norm_ref[at, :] = (hat * gain_ref[...]).astype(BF16)
        back = jnp.concatenate(
            [separate(piece[...], seq, count, heads, size) for piece in pieces], axis=1
        )
        back_ref[at, :] = back
        grad_norm = dot_nn(back, weight_ref[...])
        gain_sum = gain_sum + jnp.sum(grad_norm * hat, 0, keepdims=True)
        grad = resid_ref[at, :] + norm_back(grad_norm * gain_ref[...], hat, inverse)
        grad_ref[seq] = grad.astype(BF16)
    total = dot_tn(norm_ref[...], back_ref[...])
    if not first:
        total = total + old_ref[...]
    if not last:
        total_ref[...] = total
        gain_out_ref[...] = gain_sum
        return
    scratch_ref, extra_ref = refs[3:]
    scratch_ref[...] = total
    share = depth // ranks // zones
    for index in range(ranks * zones):
        extra_ref[index : index + 1, :share] = gain_sum[:, index * share : (index + 1) * share]
    store_square(place_ref, total_ref, scratch_ref, extra_ref, zones, ranks)


def input_grads(place, pieces, x, gain, both, resid, old, heads, ranks, last):
    zones = len(pieces)
    count, rows, depth = x.shape
    tokens = count * rows
    size = both.shape[1] // 2 // heads
    width = heads * size
    first = old is None
    operands = [*pieces, x, gain, both, resid] + ([] if first else list(old))
    shapes = [jax.ShapeDtypeStruct(x.shape, BF16)]
    scratch = [
        pltpu.VMEM((depth, depth), BF16),
        pltpu.VMEM((tokens, depth), BF16),
        pltpu.VMEM((tokens, depth), BF16),
    ]
    if last:
        shapes.append(
            jax.ShapeDtypeStruct((ranks, zones, depth // ranks + 16, depth // zones), BF16)
        )
        scratch += [pltpu.VMEM((depth, depth), F32), pltpu.VMEM((ranks * zones, width), F32)]
    else:
        shapes += [
            jax.ShapeDtypeStruct((depth, depth), F32),
            jax.ShapeDtypeStruct((1, depth), F32),
        ]
    return pl.pallas_call(
        functools.partial(input_kernel, zones, heads, size, ranks, first, last),
        grid_spec=pltpu.PrefetchScalarGridSpec(
            num_scalar_prefetch=1,
            grid=(1,),
            in_specs=[whole(operand.shape) for operand in operands],
            out_specs=[whole(shape.shape) for shape in shapes],
            scratch_shapes=scratch,
        ),
        out_shape=shapes,
        compiler_params=params(),
        cost_estimate=cost(
            4 * tokens * depth * depth, 12 * tokens * depth + 8 * depth * depth
        ),
        name="input",
    )(place, *operands)


def shift(value, axis, extent, by):
    by = by % extent
    return lax.ppermute(value, axis, [(i, (i + by) % extent) for i in range(extent)])


def flip(value, axis, extent, mask):
    return lax.ppermute(value, axis, [(i, i ^ mask) for i in range(extent)])


def exchange(pieces, axis, extent, sign):
    return [pieces[0]] + [
        shift(pieces[d], axis, extent, sign * d) for d in range(1, extent)
    ]


def widen(value):
    return value.astype(F32)


def reduce_dp(send, keep, ranks):
    rest = ranks // 8
    came = flip(send, "dp", ranks, 1)
    both = [
        widen(keep[q * rest : (q + 1) * rest]) + widen(came[q * rest : (q + 1) * rest])
        for q in range(4)
    ]
    total = both[0]
    for q in range(1, 4):
        total = total + widen(flip(both[q].astype(BF16), "dp", ranks, 2 * q))
    own = total[0]
    for third in range(1, rest):
        own = own + widen(flip(total[third].astype(BF16), "dp", ranks, 8 * third))
    return own


def reduce_head(blocks, zones, sign):
    total = blocks[0]
    for d in range(1, zones):
        total = total + widen(shift(blocks[d].astype(BF16), "head", zones, sign * d))
    return total


def local(
    zones,
    ranks,
    block_input,
    lengths,
    cotangent,
    norm1_gain,
    value_projection_weight,
    rand_logits,
    output_projection_weight,
    norm2_gain,
    up_projection_weight,
    up_bias,
    down_projection_weight,
    down_bias,
):
    seq_count, rows, depth = block_input.shape
    heads, full, _ = rand_logits.shape
    hidden = up_bias.shape[0]
    assert rows == SHORT and full == rows * zones and ranks % 8 == 0
    count = 2
    chunks = seq_count // count
    place = jnp.stack([lax.axis_index("head"), lax.axis_index("dp")]).astype(jnp.int32)
    gain1, gain2 = norm1_gain[None], norm2_gain[None]
    width = value_projection_weight.shape[1]

    shard = jnp.concatenate([value_projection_weight.T, output_projection_weight], 0)
    slot = 2 * width // ranks
    shard = lax.dynamic_slice_in_dim(shard, place[1] * slot, slot, 0)
    both = lax.all_gather(shard, ("head", "dp"), axis=0, tiled=True)
    both = both.reshape(zones, 2 * width, depth)

    probs, probs_t, corner, corner_t = make_probs(rand_logits)

    def part(array, c):
        return array[c * count : (c + 1) * count]

    values, mixed = [], []
    for c in range(chunks):
        made = make_values(place, part(block_input, c), gain1, both, heads)
        values.append(exchange(made, "head", zones, 1))
    for c in range(chunks):
        made = mix(place, part(lengths, c), values[c], probs, corner, count, 1)
        mixed.append(exchange(made, "head", zones, 1))

    fed, grads = [], []
    for c in range(chunks):
        out = feed(
            place,
            mixed[c],
            part(block_input, c),
            part(cotangent, c),
            both,
            gain2,
            up_projection_weight,
            up_bias[None],
            down_projection_weight,
            down_bias[None],
            heads,
        )
        grads.append(exchange(out[:zones], "head", zones, -1))
        fed.append(out[zones:])
    blocks, resids, acts, pres, norms, mixes, attends, up_sums, sums = zip(*fed)

    cots = [part(cotangent, c).reshape(count * rows, depth) for c in range(chunks)]
    halves = [
        weight_grads(place, acts, pres, norms, cots, odd, zones, ranks) for odd in (1, 0)
    ]
    ff = reduce_dp(*halves, ranks)
    ff = reduce_head(ff, zones, 1)

    up_total = sum(up_sums[1:], up_sums[0]).reshape(ranks * zones, -1)
    rest_total = sum(sums[1:], sums[0])
    extra = jnp.concatenate(
        [
            up_total,
            rest_total[0].reshape(ranks * zones, -1),
            rest_total[1].reshape(ranks * zones, -1),
        ],
        1,
    )
    extra = jnp.pad(extra, ((0, 0), (0, width - extra.shape[1])))
    out_blocks = out_weight_grads(place, attends, mixes, extra, zones, ranks)
    half = ranks // 2
    out_total = reduce_dp(out_blocks[half:], out_blocks[:half], ranks)
    out_square = reduce_head(out_total[:, : depth // ranks], zones, -1)
    extra_total = reduce_head(out_total[:, depth // ranks], zones, 1)

    backs = []
    for c in range(chunks):
        made = mix(place, part(lengths, c), grads[c], probs_t, corner_t, count, -1)
        backs.append(exchange(made, "head", zones, -1))

    rand = [
        logit_grads(place, lengths, grads, values, rand_logits, odd, ranks, count)
        for odd in (1, 0)
    ]
    grad_rand = reduce_dp(*rand, ranks)

    inputs, old = [], None
    for c in range(chunks):
        out = input_grads(
            place,
            backs[c],
            part(block_input, c),
            gain1,
            both,
            resids[c],
            old,
            heads,
            ranks,
            c == chunks - 1,
        )
        inputs.append(out[0])
        old = out[1:]
    value_total = reduce_dp(old[0][half:], old[0][:half], ranks)
    value_total = reduce_head(value_total, zones, 1)
    block_rows = depth // ranks

    up_size, gain_size = hidden // ranks // zones, depth // ranks // zones
    return (
        jnp.concatenate(blocks, 0),
        jnp.concatenate(inputs, 0),
        grad_rand,
        value_total[:block_rows],
        out_square.T,
        value_total[block_rows, :gain_size],
        extra_total[up_size : up_size + gain_size],
        ff[0].T,
        extra_total[:up_size],
        ff[1],
        extra_total[up_size + gain_size : up_size + 2 * gain_size],
    )


def solution(mesh):
    in_specs = (
        P("dp", "head", None),
        P("dp"),
        P("dp", "head", None),
        P(),
        P(None, "head"),
        P("head", None, None),
        P("head", None),
        P(),
        P(),
        P(),
        P(),
        P(),
    )
    out_specs = (
        P("dp", "head", None),
        P("dp", "head", None),
        P("head", "dp", None),
        P("dp", "head"),
        P("head", "dp"),
        P(("dp", "head")),
        P(("dp", "head")),
        P(None, ("dp", "head")),
        P(("dp", "head")),
        P(("dp", "head"), None),
        P(("dp", "head")),
    )
    body = functools.partial(local, mesh.shape["head"], mesh.shape["dp"])
    return jax.shard_map(
        body, mesh=mesh, in_specs=in_specs, out_specs=out_specs, check_vma=False
    )
```

time: 1090 us -> 468 us (0.43)
  waiting for transfers between devices: 719 us -> 141 us
  matrix products: 168 us -> 0 us
  Pallas kernels: 0 us -> 163 us
  starting transfers between devices: 1.13 us -> 88.2 us
  other arithmetic: 86.6 us -> 28.9 us
  blocking collectives: 41.1 us -> 0 us
  local copies, waits for them, and re-layouts: 39.7 us -> 25.5 us
    reduce_scatter x6 -> x0, waiting for transfers between devices: 525 us -> none  [the longest x1 141 us: local(): lax.psum_scatter(gradient_up_weight, ('dp', 'head'), scatter_dimension=1,...]
    dot_general x24 -> x0, matrix products: 168 us -> none  [the longest x3 33 us: back_whole(): jnp.einsum('ihe,jhe->hij', seq_grads, seq_values, preferred_element_type=...]
    pallas_call x0 -> x16, Pallas kernels: none -> 163 us  [the longest x2 49.5 us: feed(): pl.pallas_call(functools.partial(feed_kernel, zones, heads, size, steps),...]
    all_gather x2 -> x1, waiting for transfers between devices: 194 us -> 45.6 us  [local(): both = lax.all_gather(shard, ('head', 'dp'), axis=0, tiled=True)]
    ppermute x0 -> x52, waiting for transfers between devices: none -> 95.6 us  [the longest x16 68.5 us: flip(): return lax.ppermute(value, axis, [(i, i ^ mask) for i in range(extent)])]
    ppermute x0 -> x52, starting transfers between devices: none -> 88.1 us  [the longest x36 73.2 us: shift(): lax.ppermute(value, axis, [(i, (i + by) % extent) for i in range(extent)])]
    unnamed x1 -> x0, blocking collectives: 41.1 us -> none
    div x7 -> x0, other arithmetic: 27 us -> none  [the longest x2 27 us: softmax_rows(): return raised / jnp.sum(raised, -1, keepdims=True)]
  transfers between devices with their start and end apart: 9 -> 53, of which waited for: 8 -> 13; matrix products, arithmetic and copies ran while one was open for 12% -> 10% of each run, Pallas kernels for 0% -> 27%
where the time goes in v1:
time: 468 us; the launch traced here: 462 us
  Pallas kernels  163 us (35%)
  waiting for transfers between devices  141 us (30%)
  starting transfers between devices  88.2 us (19%)
  other arithmetic  28.9 us (6%)
  local copies, waits for them, and re-layouts  25.5 us (5%)
  between operations  14.9 us (3%)
    ppermute x36, starting transfers between devices, shift(): lax.ppermute(value, axis, [(i, (i + by) % extent) for i in range(extent)])  73.2 us
    ppermute x16, waiting for transfers between devices, flip(): return lax.ppermute(value, axis, [(i, i ^ mask) for i in range(extent)])  68.5 us
    pallas_call x2, Pallas kernels, feed(): pl.pallas_call(functools.partial(feed_kernel, zones, heads, size, steps),...  49.5 us
    all_gather x1, waiting for transfers between devices, local(): both = lax.all_gather(shard, ('head', 'dp'), axis=0, tiled=True)  45.6 us
    ppermute x36, waiting for transfers between devices, shift(): lax.ppermute(value, axis, [(i, (i + by) % extent) for i in range(extent)])  27.1 us
    pallas_call x4, Pallas kernels, mix(): pl.pallas_call(functools.partial(mix_kernel, zones, count, lanes // count...  25.9 us
    pallas_call x2, Pallas kernels, weight_grads(): pl.pallas_call(functools.partial(weights_kernel, zones, chunks), grid_spe...  22.4 us
    pallas_call x2, Pallas kernels, logit_grads(): pl.pallas_call(functools.partial(logits_kernel, zones, chunks, count, hea...  21 us
  transfers between devices with their start and end apart: 53, of which 13 were waited for; matrix products, arithmetic and copies ran while one was open for 10% of the time, Pallas kernels for 27%

profile of v1, /device:TPU:0, one launch (start us, length us, event | category | flops | bytes accessed | tf_op | source)
XLA Modules:
  0.0 461.6 jit_solution(17816438917369777802)
XLA Ops:
  10.1 13.9 %probs.1 = (bf16[3,1024,1024]{2,1,0:T(8,128)(2,1)}, bf16[3,1024,1024]{2,1,0:T(8,128)(2,1)}, bf16[3,256,256]{2,1,0:T(8,128)(2,1)}, bf16[3,256,256]{2,1,0:T(8,128)(2,1)}) custom-call(bf16[3,1024,1024]{2,1,0:T(8,128)(2,1)} %refs_16_.3), custom_call_target="tpu_custom_call" | custom-call | flops 31457280 | bytes 18874368 | tf_op jit(solution)/shard_map/probs/pallas_call | solution.py:95
  25.9 45.6 %all-gather.2.cloned.1.call-done = bf16[1536,768]{1,0:T(8,128)(2,1)} async-done(((bf16[48,768]{1,0:T(8,128)(2,1)}), bf16[1536,768]{1,0:T(8,128)(2,1)}) %all-gather.2.cloned.1.call-update) | async-done | bytes 2359312 | tf_op jit(solution)/shard_map/all_gather | solution.py:740
  95.1 6.5 %mix.5 = (bf16[256,384]{1,0:T(8,128)(2,1)}, bf16[256,384]{1,0:T(8,128)(2,1)}, bf16[256,384]{1,0:T(8,128)(2,1)}, bf16[256,384]{1,0:T(8,128)(2,1)}) custom-call(s32[2]{0:T(128)} %pad_add_fusion.place_ref, s32[2]{0:T(128)} %get-tuple-element.211.long_flags, bf16[256,384]{1,0:T(8,128)(2,1)} %get-tuple-element.81.refs_0_.refs_12_, bf16[256,384]{1,0:T(8,128)(2,1)} %copy-done.3, ...), custom_call_target="tpu_custom_call" | custom-call | flops 805306368 | bytes 7864320 | tf_op jit(solution)/shard_map/mix/pallas_call | solution.py:183
  101.6 13.1 %collective-permute-start.9 = (bf16[256,384]{1,0:T(8,128)(2,1)}, bf16[256,384]{1,0:T(8,128)(2,1)S(1)}, u32[]{:S(2)}, u32[]{:S(2)}) collective-permute-start(bf16[256,384]{1,0:T(8,128)(2,1)} %get-tuple-element.86), channel_id=1, source_target_pairs={{0,1},{1,2},{2,3},{3,0},{4,5},{5,6},{6,7},{7,4},{8,9},{9,10},{10,1... | collective-permute-start | bytes 589832 | tf_op jit(solution)/shard_map/ppermute | solution.py:671
  121.8 6.5 %mix.4 = (bf16[256,384]{1,0:T(8,128)(2,1)}, bf16[256,384]{1,0:T(8,128)(2,1)}, bf16[256,384]{1,0:T(8,128)(2,1)}, bf16[256,384]{1,0:T(8,128)(2,1)}) custom-call(s32[2]{0:T(128)} %pad_add_fusion.place_ref, s32[2]{0:T(128)} %get-tuple-element.210.long_flags, bf16[256,384]{1,0:T(8,128)(2,1)} %get-tuple-element.70.refs_0_.refs_8_, bf16[256,384]{1,0:T(8,128)(2,1)} %copy-done.6, ...), custom_call_target="tpu_custom_call" | custom-call | flops 805306368 | bytes 7864320 | tf_op jit(solution)/shard_map/mix/pallas_call | solution.py:183
  134.1 24.8 %feed.3 = (bf16[256,384]{1,0:T(8,128)(2,1)}, bf16[256,384]{1,0:T(8,128)(2,1)}, bf16[256,384]{1,0:T(8,128)(2,1)}, bf16[256,384]{1,0:T(8,128)(2,1)}, bf16[2,256,76...) custom-call(s32[2]{0:T(128)} %pad_add_fusion.place_ref, ...), custom_call_target="tpu_custom_call" | custom-call | flops 10871635968 | bytes 23592960 | tf_op jit(solution)/shard_map/feed/pallas_call | solution.py:327
  159.8 24.6 %feed.2 = (bf16[256,384]{1,0:T(8,128)(2,1)}, bf16[256,384]{1,0:T(8,128)(2,1)}, bf16[256,384]{1,0:T(8,128)(2,1)}, bf16[256,384]{1,0:T(8,128)(2,1)}, bf16[2,256,76...) custom-call(s32[2]{0:T(128)} %pad_add_fusion.place_ref, ...), custom_call_target="tpu_custom_call" | custom-call | flops 10871635968 | bytes 23592960 | tf_op jit(solution)/shard_map/feed/pallas_call | solution.py:327
  184.5 11.4 %weights.3 = bf16[4,4,2,96,768]{4,3,2,1,0:T(8,128)(2,1)} custom-call(s32[2]{0:T(128)} %pad_add_fusion.place_ref, bf16[3072,512]{1,0:T(8,128)(2,1)} %get-tuple-element.123.refs_0_, bf16[3072,512]{1,0:T(8,128)(2,1)} %get-tuple-element.124.refs_1_, bf16[3072,512]{1,0:T(8,128)(2,1)} %get-tuple-element.125.refs_2_, bf16[3072,512]{1,0:T(8,128)(2,1)} %get-tuple-element.126.refs_3_, ...), custom_call_target="tpu_custom_call" | custom-call | flops 4831838208 | bytes 14155776 | tf_op jit(solution)/shard_map/weights/pallas_call | solution.py:412
  203.1 8.8 %collective-permute-done.12.refs_1_ = bf16[256,384]{1,0:T(8,128)(2,1)S(1)} collective-permute-done((bf16[256,384]{1,0:T(8,128)(2,1)S(1)}, bf16[256,384]{1,0:T(8,128)(2,1)S(1)}, u32[]{:S(2)}, u32[]{:S(2)}) %collective-permute-start.12) | collective-permute-done | bytes 196640 | tf_op jit(solution)/shard_map/ppermute | solution.py:671
  211.9 17.4 %collective-permute-start.20 = (bf16[256,384]{1,0:T(8,128)(2,1)S(1)}, bf16[256,384]{1,0:T(8,128)(2,1)S(1)}, u32[]{:S(2)}, u32[]{:S(2)}) collective-permute-start(bf16[256,384]{1,0:T(8,128)(2,1)S(1)} %copy-done.31), channel_id=1, source_target_pairs={{0,1},{1,2},{2,3},{3,0},{4,5},{5,6},{6,7},{7,4},{8,9},{9,10},{10,1... | collective-permute-start | bytes 589832 | tf_op jit(solution)/shard_map/ppermute | solution.py:671
  233.1 5.4 %out_weight.1 = bf16[8,4,112,192]{3,2,1,0:T(8,128)(2,1)} custom-call(s32[2]{0:T(128)} %pad_add_fusion.place_ref, bf16[512,768]{1,0:T(8,128)(2,1)} %get-tuple-element.115.refs_0_, bf16[512,768]{1,0:T(8,128)(2,1)} %get-tuple-element.116.refs_1_, bf16[512,768]{1,0:T(8,128)(2,1)} %get-tuple-element.117.refs_2_, bf16[512,768]{1,0:T(8,128)(2,1)} %get-tuple-element.118.refs_3_, ...), custom_call_target="tpu_custom_call" | custom-call | flops 1207959552 | bytes 4325376 | tf_op jit(solution)/shard_map/out_weight/pallas_call | solution.py:468
  241.7 6.5 %mix.6 = (bf16[256,384]{1,0:T(8,128)(2,1)}, bf16[256,384]{1,0:T(8,128)(2,1)}, bf16[256,384]{1,0:T(8,128)(2,1)}, bf16[256,384]{1,0:T(8,128)(2,1)}) custom-call(s32[2]{0:T(128)} %pad_add_fusion.place_ref, s32[2]{0:T(128)} %get-tuple-element.210.long_flags, bf16[256,384]{1,0:T(8,128)(2,1)} %get-tuple-element.90.refs_0_, bf16[256,384]{1,0:T(8,128)(2,1)} %copy-done.11, ...), custom_call_target="tpu_custom_call" | custom-call | flops 805306368 | bytes 7864320 | tf_op jit(solution)/shard_map/mix/pallas_call | solution.py:183
  252.7 11.0 %weights.2 = bf16[4,4,2,96,768]{4,3,2,1,0:T(8,128)(2,1)} custom-call(s32[2]{0:T(128)} %pad_add_fusion.place_ref, bf16[3072,512]{1,0:T(8,128)(2,1)} %get-tuple-element.123.refs_0_, bf16[3072,512]{1,0:T(8,128)(2,1)} %get-tuple-element.124.refs_1_, bf16[3072,512]{1,0:T(8,128)(2,1)} %get-tuple-element.125.refs_2_, bf16[3072,512]{1,0:T(8,128)(2,1)} %get-tuple-element.126.refs_3_, ...), custom_call_target="tpu_custom_call" | custom-call | flops 4831838208 | bytes 14155776 | tf_op jit(solution)/shard_map/weights/pallas_call | solution.py:412
  263.8 6.5 %mix.7 = (bf16[256,384]{1,0:T(8,128)(2,1)}, bf16[256,384]{1,0:T(8,128)(2,1)}, bf16[256,384]{1,0:T(8,128)(2,1)}, bf16[256,384]{1,0:T(8,128)(2,1)}) custom-call(s32[2]{0:T(128)} %pad_add_fusion.place_ref, s32[2]{0:T(128)} %get-tuple-element.211.long_flags, bf16[256,384]{1,0:T(8,128)(2,1)} %get-tuple-element.102.refs_0_.refs_4_, bf16[256,384]{1,0:T(8,128)(2,1)} %copy-done.9, ...), custom_call_target="tpu_custom_call" | custom-call | flops 805306368 | bytes 7864320 | tf_op jit(solution)/shard_map/mix/pallas_call | solution.py:183
  270.3 10.5 %logits.3 = bf16[4,3,128,1024]{3,2,1,0:T(8,128)(2,1)} custom-call(s32[2]{0:T(128)} %pad_add_fusion.place_ref, s32[4]{0:T(128)} %lengths_ref.3, bf16[256,384]{1,0:T(8,128)(2,1)} %get-tuple-element.90.refs_0_, bf16[256,384]{1,0:T(8,128)(2,1)} %copy-done.11, bf16[256,384]{1,0:T(8,128)(2,1)} %copy-done.12, bf16[256,384]{1,0:T(8,128)(2,1)} %copy-done.14, ...), custom_call_target="tpu_custom_call" | custom-call | flops 805306368 | bytes 6291456 | tf_op jit(solution)/shard_map/logits/pallas_call | solution.py:556
  285.8 7.2 %input.2 = (bf16[2,256,768]{2,1,0:T(8,128)(2,1)}, f32[768,768]{1,0:T(8,128)}, f32[1,768]{1,0:T(1,128)}) custom-call(s32[2]{0:T(128)} %pad_add_fusion.place_ref, bf16[256,384]{1,0:T(8,128)(2,1)} %get-tuple-element.96.refs_0_, bf16[256,384]{1,0:T(8,128)(2,1)} %copy-done.19, bf16[256,384]{1,0:T(8,128)(2,1)} %copy-done.20, bf16[256,384]{1,0:T(8,128)(2,1)} %copy-done.21, ...), custom_call_target="tpu_custom_call" | custom-call | flops 1207959552 | bytes 9437184 | tf_op jit(solution)/shard_map/input/pallas_call | solution.py:651
  301.8 8.3 %input.3 = (bf16[2,256,768]{2,1,0:T(8,128)(2,1)}, bf16[8,4,112,192]{3,2,1,0:T(8,128)(2,1)}) custom-call(s32[2]{0:T(128)} %pad_add_fusion.place_ref, bf16[256,384]{1,0:T(8,128)(2,1)} %get-tuple-element.106.refs_0_, bf16[256,384]{1,0:T(8,128)(2,1)} %collective-permute-done.21.refs_1_, bf16[256,384]{1,0:T(8,128)(2,1)} %collective-permute-done.22.refs_2_, ...), custom_call_target="tpu_custom_call" | custom-call | flops 1207959552 | bytes 9437184 | tf_op jit(solution)/shard_map/input/pallas_call | solution.py:651
  317.3 10.5 %logits.2 = bf16[4,3,128,1024]{3,2,1,0:T(8,128)(2,1)} custom-call(s32[2]{0:T(128)} %pad_add_fusion.place_ref, s32[4]{0:T(128)} %lengths_ref.3, bf16[256,384]{1,0:T(8,128)(2,1)} %get-tuple-element.90.refs_0_, bf16[256,384]{1,0:T(8,128)(2,1)} %copy-done.11, bf16[256,384]{1,0:T(8,128)(2,1)} %copy-done.12, bf16[256,384]{1,0:T(8,128)(2,1)} %copy-done.14, ...), custom_call_target="tpu_custom_call" | custom-call | flops 805306368 | bytes 6291456 | tf_op jit(solution)/shard_map/logits/pallas_call | solution.py:556
  340.2 5.3 %collective-permute-done.31 = bf16[1,4,112,192]{3,2,1,0:T(8,128)(2,1)S(1)} collective-permute-done((bf16[1,4,112,192]{3,2,1,0:T(8,128)(2,1)}, bf16[1,4,112,192]{3,2,1,0:T(8,128)(2,1)S(1)}, u32[]{:S(2)}, u32[]{:S(2)}) %collective-permute-start.31) | collective-permute-done | bytes 172064 | tf_op jit(solution)/shard_map/ppermute | solution.py:675
  354.0 5.7 %add_convert_fusion.2 = (bf16[1,4,2,96,768]{4,3,2,1,0:T(8,128)(2,1)}, bf16[1,4,2,96,768]{4,3,2,1,0:T(8,128)(2,1)}, bf16[1,4,2,96,768]{4,3,2,1,0:T(8,128)(2,1)}) fusion(bf16[4,4,2,96,768]{4,3,2,1,0:T(8,128)(2,1)} %collective-permute-done.45, bf16[4,4,2,96,768]{4,3,2,1,0:T(8,128)(2,1)} %weights.2), kind=kLoop, calls=%fused_computation.3 | loop fusion | flops 7077888 | bytes 10616832 | tf_op jit(solution)/shard_map/convert_element_type | solution.py:697
  383.5 10.9 %collective-permute-done.48 = bf16[1,4,2,96,768]{4,3,2,1,0:T(8,128)(2,1)} collective-permute-done((bf16[1,4,2,96,768]{4,3,2,1,0:T(8,128)(2,1)}, bf16[1,4,2,96,768]{4,3,2,1,0:T(8,128)(2,1)}, u32[]{:S(2)}, u32[]{:S(2)}) %collective-permute-start.48) | collective-permute-done | bytes 1179680 | tf_op jit(solution)/shard_map/ppermute | solution.py:675
  397.0 22.7 %collective-permute-done.47 = bf16[1,4,2,96,768]{4,3,2,1,0:T(8,128)(2,1)} collective-permute-done((bf16[1,4,2,96,768]{4,3,2,1,0:T(8,128)(2,1)}, bf16[1,4,2,96,768]{4,3,2,1,0:T(8,128)(2,1)}, u32[]{:S(2)}, u32[]{:S(2)}) %collective-permute-start.47) | collective-permute-done | bytes 1179680 | tf_op jit(solution)/shard_map/ppermute | solution.py:675
  424.8 11.6 %collective-permute-done.27 = bf16[1,3,128,1024]{3,2,1,0:T(8,128)(2,1)S(1)} collective-permute-done((bf16[1,3,128,1024]{3,2,1,0:T(8,128)(2,1)S(1)}, bf16[1,3,128,1024]{3,2,1,0:T(8,128)(2,1)S(1)}, u32[]{:S(2)}, u32[]{:S(2)}) %collective-permute-start.27) | collective-permute-done | bytes 786464 | tf_op jit(solution)/shard_map/ppermute | solution.py:675
  436.5 14.0 %collective-permute-done.26 = bf16[1,3,128,1024]{3,2,1,0:T(8,128)(2,1)S(1)} collective-permute-done((bf16[1,3,128,1024]{3,2,1,0:T(8,128)(2,1)S(1)}, bf16[1,3,128,1024]{3,2,1,0:T(8,128)(2,1)S(1)}, u32[]{:S(2)}, u32[]{:S(2)}) %collective-permute-start.26) | collective-permute-done | bytes 786464 | tf_op jit(solution)/shard_map/ppermute | solution.py:675
  (238 shorter events, 137.9 us)
Async XLA Ops:
  7.2 64.3 %all-gather.2.cloned.1.call-start = ((), (), s32[]{:S(2)}) async-start(), calls=%async_computation | async-start | bytes 2433024 | tf_op jit(solution)/shard_map/all_gather | solution.py:740
  84.6 30.2 %collective-permute-start = (bf16[256,384]{1,0:T(8,128)(2,1)}, bf16[256,384]{1,0:T(8,128)(2,1)S(1)}, u32[]{:S(2)}, u32[]{:S(2)}) collective-permute-start(bf16[256,384]{1,0:T(8,128)(2,1)} %get-tuple-element.71), channel_id=1, source_target_pairs={{0,1},{1,2},{2,3},{3,0},{4,5},{5,6},{6,7},{7,4},{8,9},{9,10},{10,1... | collective-permute-start | bytes 589832 | tf_op jit(solution)/shard_map/ppermute | solution.py:671
  86.1 35.0 %collective-permute-start.1 = (bf16[256,384]{1,0:T(8,128)(2,1)}, bf16[256,384]{1,0:T(8,128)(2,1)S(1)}, u32[]{:S(2)}, u32[]{:S(2)}) collective-permute-start(bf16[256,384]{1,0:T(8,128)(2,1)} %get-tuple-element.72), channel_id=1, source_target_pairs={{0,2},{1,3},{2,0},{3,1},{4,6},{5,7},{6,4},{7,5},{8,10},{9,11},{10,... | collective-permute-start | bytes 589832 | tf_op jit(solution)/shard_map/ppermute | solution.py:671
  87.2 33.9 %collective-permute-start.2 = (bf16[256,384]{1,0:T(8,128)(2,1)}, bf16[256,384]{1,0:T(8,128)(2,1)S(1)}, u32[]{:S(2)}, u32[]{:S(2)}) collective-permute-start(bf16[256,384]{1,0:T(8,128)(2,1)} %get-tuple-element.73), channel_id=1, source_target_pairs={{0,3},{1,0},{2,1},{3,2},{4,7},{5,4},{6,5},{7,6},{8,11},{9,8},{10,9... | collective-permute-start | bytes 589832 | tf_op jit(solution)/shard_map/ppermute | solution.py:671
  101.6 29.3 %collective-permute-start.9 = (bf16[256,384]{1,0:T(8,128)(2,1)}, bf16[256,384]{1,0:T(8,128)(2,1)S(1)}, u32[]{:S(2)}, u32[]{:S(2)}) collective-permute-start(bf16[256,384]{1,0:T(8,128)(2,1)} %get-tuple-element.86), channel_id=1, source_target_pairs={{0,1},{1,2},{2,3},{3,0},{4,5},{5,6},{6,7},{7,4},{8,9},{9,10},{10,1... | collective-permute-start | bytes 589832 | tf_op jit(solution)/shard_map/ppermute | solution.py:671
  128.3 30.6 %collective-permute-start.3 = (bf16[256,384]{1,0:T(8,128)(2,1)}, bf16[256,384]{1,0:T(8,128)(2,1)S(1)}, u32[]{:S(2)}, u32[]{:S(2)}) collective-permute-start(bf16[256,384]{1,0:T(8,128)(2,1)} %get-tuple-element.77), channel_id=1, source_target_pairs={{0,1},{1,2},{2,3},{3,0},{4,5},{5,6},{6,7},{7,4},{8,9},{9,10},{10,1... | collective-permute-start | bytes 589832 | tf_op jit(solution)/shard_map/ppermute | solution.py:671
  195.9 156.0 %collective-permute-start.45 = (bf16[4,4,2,96,768]{4,3,2,1,0:T(8,128)(2,1)}, bf16[4,4,2,96,768]{4,3,2,1,0:T(8,128)(2,1)}, u32[]{:S(2)}, u32[]{:S(2)}) collective-permute-start(bf16[4,4,2,96,768]{4,3,2,1,0:T(8,128)(2,1)} %weights.3), channel_id=1, source_target_pairs={{0,4},{4,0},{8,12},{12,8},{16,20},{20,16},{24,28},{28,24},{1,5},{5... | collective-permute-start | bytes 14155784 | tf_op jit(solution)/shard_map/ppermute | solution.py:675
  196.0 52.2 %collective-permute-start.18 = (bf16[256,384]{1,0:T(8,128)(2,1)}, bf16[256,384]{1,0:T(8,128)(2,1)S(1)}, u32[]{:S(2)}, u32[]{:S(2)}) collective-permute-start(bf16[256,384]{1,0:T(8,128)(2,1)} %get-tuple-element.103), channel_id=1, source_target_pairs={{0,3},{1,0},{2,1},{3,2},{4,7},{5,4},{6,5},{7,6},{8,11},{9,8},{10,9... | collective-permute-start | bytes 589832 | tf_op jit(solution)/shard_map/ppermute | solution.py:671
  198.0 54.1 %collective-permute-start.19 = (bf16[256,384]{1,0:T(8,128)(2,1)S(1)}, bf16[256,384]{1,0:T(8,128)(2,1)S(1)}, u32[]{:S(2)}, u32[]{:S(2)}) collective-permute-start(bf16[256,384]{1,0:T(8,128)(2,1)S(1)} %copy-done.32), channel_id=1, source_target_pairs={{0,2},{1,3},{2,0},{3,1},{4,6},{5,7},{6,4},{7,5},{8,10},{9,11},{10,... | collective-permute-start | bytes 589832 | tf_op jit(solution)/shard_map/ppermute | solution.py:671
  202.7 29.7 %collective-permute-start.13 = (bf16[256,384]{1,0:T(8,128)(2,1)S(1)}, bf16[256,384]{1,0:T(8,128)(2,1)S(1)}, u32[]{:S(2)}, u32[]{:S(2)}) collective-permute-start(bf16[256,384]{1,0:T(8,128)(2,1)S(1)} %copy-done.39), channel_id=1, source_target_pairs={{0,2},{1,3},{2,0},{3,1},{4,6},{5,7},{6,4},{7,5},{8,10},{9,11},{10,... | collective-permute-start | bytes 589832 | tf_op jit(solution)/shard_map/ppermute | solution.py:671
  211.9 40.2 %collective-permute-start.20 = (bf16[256,384]{1,0:T(8,128)(2,1)S(1)}, bf16[256,384]{1,0:T(8,128)(2,1)S(1)}, u32[]{:S(2)}, u32[]{:S(2)}) collective-permute-start(bf16[256,384]{1,0:T(8,128)(2,1)S(1)} %copy-done.31), channel_id=1, source_target_pairs={{0,1},{1,2},{2,3},{3,0},{4,5},{5,6},{6,7},{7,4},{8,9},{9,10},{10,1... | collective-permute-start | bytes 589832 | tf_op jit(solution)/shard_map/ppermute | solution.py:671
  241.0 52.0 %collective-permute-start.35 = (bf16[4,4,112,192]{2,3,1,0:T(8,128)(2,1)}, bf16[4,4,112,192]{2,3,1,0:T(8,128)(2,1)S(1)}, u32[]{:S(2)}, u32[]{:S(2)}) collective-permute-start(bf16[4,4,112,192]{2,3,1,0:T(8,128)(2,1)} %copy.30), channel_id=1, source_target_pairs={{0,4},{4,0},{8,12},{12,8},{16,20},{20,16},{24,28},{28,24},{1,5},{5... | collective-permute-start | bytes 2064392 | tf_op jit(solution)/shard_map/ppermute | solution.py:675
  248.2 32.5 %collective-permute-start.15 = (bf16[256,384]{1,0:T(8,128)(2,1)}, bf16[256,384]{1,0:T(8,128)(2,1)S(1)}, u32[]{:S(2)}, u32[]{:S(2)}) collective-permute-start(bf16[256,384]{1,0:T(8,128)(2,1)} %get-tuple-element.97), channel_id=1, source_target_pairs={{0,3},{1,0},{2,1},{3,2},{4,7},{5,4},{6,5},{7,6},{8,11},{9,8},{10,9... | collective-permute-start | bytes 589832 | tf_op jit(solution)/shard_map/ppermute | solution.py:671
  252.1 32.0 %collective-permute-start.16 = (bf16[256,384]{1,0:T(8,128)(2,1)}, bf16[256,384]{1,0:T(8,128)(2,1)S(1)}, u32[]{:S(2)}, u32[]{:S(2)}) collective-permute-start(bf16[256,384]{1,0:T(8,128)(2,1)} %get-tuple-element.98), channel_id=1, source_target_pairs={{0,2},{1,3},{2,0},{3,1},{4,6},{5,7},{6,4},{7,5},{8,10},{9,11},{10,... | collective-permute-start | bytes 589832 | tf_op jit(solution)/shard_map/ppermute | solution.py:671
  252.1 33.0 %collective-permute-start.17 = (bf16[256,384]{1,0:T(8,128)(2,1)}, bf16[256,384]{1,0:T(8,128)(2,1)S(1)}, u32[]{:S(2)}, u32[]{:S(2)}) collective-permute-start(bf16[256,384]{1,0:T(8,128)(2,1)} %get-tuple-element.99), channel_id=1, source_target_pairs={{0,1},{1,2},{2,3},{3,0},{4,5},{5,6},{6,7},{7,4},{8,9},{9,10},{10,1... | collective-permute-start | bytes 589832 | tf_op jit(solution)/shard_map/ppermute | solution.py:671
  293.0 84.8 %collective-permute-start.24 = (bf16[4,3,128,1024]{3,2,1,0:T(8,128)(2,1)}, bf16[4,3,128,1024]{3,2,1,0:T(8,128)(2,1)}, u32[]{:S(2)}, u32[]{:S(2)}) collective-permute-start(bf16[4,3,128,1024]{3,2,1,0:T(8,128)(2,1)} %logits.3), channel_id=1, source_target_pairs={{0,4},{4,0},{8,12},{12,8},{16,20},{20,16},{24,28},{28,24},{1,5},{5... | collective-permute-start | bytes 9437192 | tf_op jit(solution)/shard_map/ppermute | solution.py:675
  364.2 30.1 %collective-permute-start.48 = (bf16[1,4,2,96,768]{4,3,2,1,0:T(8,128)(2,1)}, bf16[1,4,2,96,768]{4,3,2,1,0:T(8,128)(2,1)}, u32[]{:S(2)}, u32[]{:S(2)}) collective-permute-start(bf16[1,4,2,96,768]{4,3,2,1,0:T(8,128)(2,1)} %get-tuple-element.174), channel_id=1, source_target_pairs={{0,24},{4,28},{8,16},{12,20},{16,8},{20,12},{24,0},{28,4},{1,25},{... | collective-permute-start | bytes 3538952 | tf_op jit(solution)/shard_map/ppermute | solution.py:675
  366.3 53.4 %collective-permute-start.47 = (bf16[1,4,2,96,768]{4,3,2,1,0:T(8,128)(2,1)}, bf16[1,4,2,96,768]{4,3,2,1,0:T(8,128)(2,1)}, u32[]{:S(2)}, u32[]{:S(2)}) collective-permute-start(bf16[1,4,2,96,768]{4,3,2,1,0:T(8,128)(2,1)} %get-tuple-element.175), channel_id=1, source_target_pairs={{0,16},{4,20},{8,24},{12,28},{16,0},{20,4},{24,8},{28,12},{1,17},{... | collective-permute-start | bytes 3538952 | tf_op jit(solution)/shard_map/ppermute | solution.py:675
  367.7 52.0 %collective-permute-start.46 = (bf16[1,4,2,96,768]{4,3,2,1,0:T(8,128)(2,1)}, bf16[1,4,2,96,768]{4,3,2,1,0:T(8,128)(2,1)}, u32[]{:S(2)}, u32[]{:S(2)}) collective-permute-start(bf16[1,4,2,96,768]{4,3,2,1,0:T(8,128)(2,1)} %get-tuple-element.173), channel_id=1, source_target_pairs={{0,8},{4,12},{8,0},{12,4},{16,24},{20,28},{24,16},{28,20},{1,9},{5... | collective-permute-start | bytes 3538952 | tf_op jit(solution)/shard_map/ppermute | solution.py:675
  380.6 55.9 %collective-permute-start.27 = (bf16[1,3,128,1024]{3,2,1,0:T(8,128)(2,1)S(1)}, bf16[1,3,128,1024]{3,2,1,0:T(8,128)(2,1)S(1)}, u32[]{:S(2)}, u32[]{:S(2)}) collective-permute-start(bf16[1,3,128,1024]{3,2,1,0:T(8,128)(2,1)S(1)} %get-tuple-element.177), channel_id=1, source_target_pairs={{0,24},{4,28},{8,16},{12,20},{16,8},{20,12},{24,0},{28,4},{1,25},{... | collective-permute-start | bytes 2359304 | tf_op jit(solution)/shard_map/ppermute | solution.py:675
  382.1 68.4 %collective-permute-start.26 = (bf16[1,3,128,1024]{3,2,1,0:T(8,128)(2,1)S(1)}, bf16[1,3,128,1024]{3,2,1,0:T(8,128)(2,1)S(1)}, u32[]{:S(2)}, u32[]{:S(2)}) collective-permute-start(bf16[1,3,128,1024]{3,2,1,0:T(8,128)(2,1)S(1)} %get-tuple-element.178), channel_id=1, source_target_pairs={{0,16},{4,20},{8,24},{12,28},{16,0},{20,4},{24,8},{28,12},{1,17},{... | collective-permute-start | bytes 2359304 | tf_op jit(solution)/shard_map/ppermute | solution.py:675
  394.4 56.2 %collective-permute-start.25 = (bf16[1,3,128,1024]{3,2,1,0:T(8,128)(2,1)S(1)}, bf16[1,3,128,1024]{3,2,1,0:T(8,128)(2,1)S(1)}, u32[]{:S(2)}, u32[]{:S(2)}) collective-permute-start(bf16[1,3,128,1024]{3,2,1,0:T(8,128)(2,1)S(1)} %get-tuple-element.176), channel_id=1, source_target_pairs={{0,8},{4,12},{8,0},{12,4},{16,24},{20,28},{24,16},{28,20},{1,9},{5... | collective-permute-start | bytes 2359304 | tf_op jit(solution)/shard_map/ppermute | solution.py:675
  423.2 30.4 %collective-permute-start.51 = (bf16[2,96,768]{2,1,0:T(8,128)(2,1)S(1)}, bf16[2,96,768]{2,1,0:T(8,128)(2,1)S(1)}, u32[]{:S(2)}, u32[]{:S(2)}) collective-permute-start(bf16[2,96,768]{2,1,0:T(8,128)(2,1)S(1)} %get-tuple-element.190), channel_id=1, source_target_pairs={{0,3},{1,0},{2,1},{3,2},{4,7},{5,4},{6,5},{7,6},{8,11},{9,8},{10,9... | collective-permute-start | bytes 884744 | tf_op jit(solution)/shard_map/ppermute | solution.py:671
  424.2 29.4 %collective-permute-start.50 = (bf16[2,96,768]{2,1,0:T(8,128)(2,1)S(1)}, bf16[2,96,768]{2,1,0:T(8,128)(2,1)S(1)}, u32[]{:S(2)}, u32[]{:S(2)}) collective-permute-start(bf16[2,96,768]{2,1,0:T(8,128)(2,1)S(1)} %get-tuple-element.191), channel_id=1, source_target_pairs={{0,2},{1,3},{2,0},{3,1},{4,6},{5,7},{6,4},{7,5},{8,10},{9,11},{10,... | collective-permute-start | bytes 884744 | tf_op jit(solution)/shard_map/ppermute | solution.py:671
  (72 other events, 795.7 us)
Sparse Core Ops, SparseCore 0:
  11.5 59.9 all-gather.1

commit v2 on v1

v2 whole, which is shorter than its diff:
```python
import functools

import jax
import jax.numpy as jnp
from jax import lax
from jax.experimental import pallas as pl
from jax.experimental.pallas import tpu as pltpu
from jax.sharding import PartitionSpec as P

SHORT = 256
EPSILON = 1e-05
F32 = jnp.float32
BF16 = jnp.bfloat16
GELU_C = 0.7978845608028654
GELU_A = 0.044715
SHARE = 1.0


def dot_nn(a, b):
    return lax.dot_general(a, b, (((1,), (0,)), ((), ())), preferred_element_type=F32)


def dot_nt(a, b):
    return lax.dot_general(a, b, (((1,), (1,)), ((), ())), preferred_element_type=F32)


def dot_tn(a, b):
    return lax.dot_general(a, b, (((0,), (0,)), ((), ())), preferred_element_type=F32)


def norm_of(value):
    centered = value - jnp.mean(value, -1, keepdims=True)
    inverse = lax.rsqrt(jnp.mean(centered * centered, -1, keepdims=True) + EPSILON)
    return centered * inverse, inverse


def norm_back(scaled, hat, inverse):
    return inverse * (
        scaled
        - jnp.mean(scaled, -1, keepdims=True)
        - hat * jnp.mean(scaled * hat, -1, keepdims=True)
    )


def interleave(values, heads, size):
    parts = []
    for head in range(heads):
        for value in values:
            parts.append(value[:, head * size : (head + 1) * size])
    return jnp.concatenate(parts, axis=1)


def separate(piece, seq, count, heads, size):
    parts = []
    for head in range(heads):
        at = (head * count + seq) * size
        parts.append(piece[:, at : at + size])
    return jnp.concatenate(parts, axis=1)


def far(shape, dtype):
    return pltpu.HBM(shape, dtype)


def kept(value):
    return pltpu.with_memory_space_constraint(value, pltpu.HBM)


def whole(shape):
    return pl.BlockSpec(
        shape, lambda *_: (0,) * len(shape), pipeline_mode=pl.Buffered(buffer_count=1)
    )


def resident():
    return pl.BlockSpec(memory_space=pltpu.VMEM)


def cost(flops, moved, special=0):
    return pl.CostEstimate(
        flops=int(flops * SHARE), bytes_accessed=int(moved * SHARE), transcendentals=0
    )


def params(megabytes, grid_dims=1):
    return pltpu.CompilerParams(
        dimension_semantics=("arbitrary",) * grid_dims, vmem_limit_bytes=megabytes << 20
    )


def probs_kernel(logit_ref, long_ref, long_t_ref, short_ref, short_t_ref):
    logits = logit_ref[0].astype(F32)
    raised = jnp.exp(logits - jnp.max(logits, -1, keepdims=True))
    probs = raised / jnp.sum(raised, -1, keepdims=True)
    long_ref[0] = probs.astype(BF16)
    long_t_ref[0] = probs.T.astype(BF16)

    @pl.when(pl.program_id(1) == 0)
    def _():
        corner = logits[:, :SHORT]
        lifted = jnp.exp(corner - jnp.max(corner, -1, keepdims=True))
        part = lifted / jnp.sum(lifted, -1, keepdims=True)
        short_ref[0] = part.astype(BF16)
        short_t_ref[0] = part.T.astype(BF16)


def make_probs(logits):
    heads, rows, _ = logits.shape
    return pl.pallas_call(
        probs_kernel,
        grid=(heads, rows // SHORT),
        in_specs=[pl.BlockSpec((1, SHORT, rows), lambda h, i: (h, i, 0))],
        out_specs=[
            pl.BlockSpec((1, SHORT, rows), lambda h, i: (h, i, 0)),
            pl.BlockSpec((1, rows, SHORT), lambda h, i: (h, 0, i)),
            pl.BlockSpec((1, SHORT, SHORT), lambda h, i: (h, 0, 0)),
            pl.BlockSpec((1, SHORT, SHORT), lambda h, i: (h, 0, 0)),
        ],
        out_shape=[
            far((heads, rows, rows), BF16),
            far((heads, rows, rows), BF16),
            jax.ShapeDtypeStruct((heads, SHORT, SHORT), BF16),
            jax.ShapeDtypeStruct((heads, SHORT, SHORT), BF16),
        ],
        compiler_params=params(20, 2),
        cost_estimate=cost(10 * logits.size, 6 * logits.size, logits.size),
        name="probs",
    )(kept(logits))


def values_kernel(zones, heads, size, first, place_ref, x_ref, gain_ref, *rest):
    width = heads * size
    if first:
        own_ref, others_ref = rest[0], rest[zones]
        mine = rest[1:zones]
        outs, weight_ref = rest[zones + 1 : 2 * zones + 1], rest[2 * zones + 1]
        half = width // 2
        parity = lax.rem(place_ref[1], 2)
        weight_ref[:width, :] = own_ref[...]
        for d in range(1, zones):
            at = pl.multiple_of(d * width + parity * half, 16)
            weight_ref[pl.ds(at, half), :] = mine[d - 1][...]
            at = pl.multiple_of(d * width + (1 - parity) * half, 16)
            weight_ref[pl.ds(at, half), :] = others_ref[d - 1]
    else:
        weight_ref, outs = rest[0], rest[1:]
    made = []
    for seq in range(x_ref.shape[0]):
        hat, _ = norm_of(x_ref[seq].astype(F32))
        norm = (hat * gain_ref[...]).astype(BF16)
        made.append(dot_nt(norm, weight_ref[...]))
    for d in range(zones):
        own = [value[:, d * width : (d + 1) * width] for value in made]
        outs[d][...] = interleave(own, heads, size).astype(BF16)


def make_values(place, x, gain, weights, zones, heads, first):
    count, rows, depth = x.shape
    wide = count * depth // zones
    operands = [x, gain, *weights]
    shapes = [jax.ShapeDtypeStruct((rows, wide), BF16)] * zones
    if first:
        shapes.append(jax.ShapeDtypeStruct((depth, depth), BF16))
    return pl.pallas_call(
        functools.partial(values_kernel, zones, heads, depth // zones // heads, first),
        grid_spec=pltpu.PrefetchScalarGridSpec(
            num_scalar_prefetch=1,
            grid=(1,),
            in_specs=[whole(operand.shape) for operand in operands],
            out_specs=[whole(shape.shape) for shape in shapes],
        ),
        out_shape=shapes,
        compiler_params=params(12),
        cost_estimate=cost(
            2 * count * rows * depth * depth, 2 * x.size * 2 + 4 * depth * depth
        ),
        name="values",
    )(place, *operands)


def mix_kernel(zones, chunks, count, size, rows, sign, place_ref, long_flags, *refs):
    pieces = refs[: chunks * zones]
    matrix_ref, corner_ref = refs[chunks * zones : chunks * zones + 2]
    outs, held = refs[chunks * zones + 2 : -1], refs[-1]
    place = place_ref[0]
    wide = count * size
    for c in range(chunks):
        for d in range(zones):
            source = lax.rem(place + zones - sign * d, zones)
            at = pl.ds(pl.multiple_of(source * rows, rows), rows)
            held[at, c * wide : (c + 1) * wide] = pieces[c * zones + d][...]
    lane = lax.broadcasted_iota(jnp.int32, (1, chunks * wide), 1)
    is_long = jnp.zeros((1, chunks * wide), jnp.bool_)
    for seq in range(chunks * count):
        inside = (lane >= seq * size) & (lane < (seq + 1) * size)
        is_long = is_long | (inside & (long_flags[seq] > SHORT))
    corner = dot_nn(corner_ref[0], held[:SHORT, :])
    for d in range(zones):
        target = lax.rem(place + zones + sign * d, zones)
        part = matrix_ref[0, pl.ds(pl.multiple_of(target * rows, rows), rows), :]
        full = dot_nn(part, held[...])
        small = jnp.where(target == 0, corner, jnp.zeros_like(corner))
        outs[d][...] = jnp.where(is_long, full, small).astype(BF16)


def mix(place, lengths, groups, matrix, corner, count, sign):
    chunks, zones = len(groups), len(groups[0])
    heads, full, _ = matrix.shape
    rows, wide = groups[0][0].shape
    lanes = wide // heads
    spec = pl.BlockSpec((rows, lanes), lambda h, *_: (0, h))
    out_spec = pl.BlockSpec((rows, chunks * lanes), lambda h, *_: (0, h))
    return pl.pallas_call(
        functools.partial(mix_kernel, zones, chunks, count, lanes // count, rows, sign),
        grid_spec=pltpu.PrefetchScalarGridSpec(
            num_scalar_prefetch=2,
            grid=(heads,),
            in_specs=[spec] * (chunks * zones)
            + [
                pl.BlockSpec((1, full, full), lambda h, *_: (h, 0, 0)),
                pl.BlockSpec((1, SHORT, SHORT), lambda h, *_: (h, 0, 0)),
            ],
            out_specs=[out_spec] * zones,
            scratch_shapes=[pltpu.VMEM((full, chunks * lanes), BF16)],
        ),
        out_shape=[jax.ShapeDtypeStruct((rows, chunks * wide), BF16)] * zones,
        compiler_params=params(16),
        cost_estimate=cost(
            2 * heads * full * full * lanes * chunks,
            2 * heads * full * full + 4 * full * wide * chunks,
        ),
        name="mix",
    )(place, lengths, *(piece for group in groups for piece in group), kept(matrix), corner)


def feed_kernel(zones, heads, size, steps, place_ref, *refs):
    pieces = refs[:zones]
    (x_ref, cot_ref, project_ref, gain_ref, up_ref, up_bias_ref, down_ref, down_bias_ref) = refs[
        zones : zones + 8
    ]
    outs = refs[zones + 8 :]
    grads = outs[:zones]
    (
        block_ref,
        resid_grad_ref,
        act_t_ref,
        pre_t_ref,
        norm_ref,
        mixed_ref,
        attended_ref,
        up_sum_ref,
        sums_ref,
        weight_ref,
        resid_ref,
        hat_ref,
        inv_ref,
        forward_ref,
        back_ref,
    ) = outs[zones:]
    count, rows, depth = x_ref.shape
    width = heads * size
    step = pl.program_id(0)

    @pl.when(step == 0)
    def _():
        for d in range(zones):
            other = lax.rem(place_ref[0] + zones - d, zones)
            at = pl.multiple_of(other * width, 16)
            weight_ref[d * width : (d + 1) * width, :] = project_ref[pl.ds(at, width), :]
        for seq in range(count):
            at = slice(seq * rows, (seq + 1) * rows)
            mixed = jnp.concatenate(
                [separate(piece[...], seq, count, heads, size) for piece in pieces], axis=1
            )
            mixed_ref[at, :] = mixed
            resid = x_ref[seq].astype(F32) + dot_nn(mixed, weight_ref[...])
            hat, inverse = norm_of(resid)
            resid_ref[at, :] = resid + down_bias_ref[...]
            hat_ref[at, :] = hat
            inv_ref[at, :] = inverse
            norm_ref[at, :] = (hat * gain_ref[...]).astype(BF16)
        forward_ref[...] = jnp.zeros_like(forward_ref)
        back_ref[...] = jnp.zeros_like(back_ref)

    up_sum = jnp.zeros((1, up_ref.shape[1]), F32)
    for seq in range(count):
        at = slice(seq * rows, (seq + 1) * rows)
        pre = dot_nn(norm_ref[at, :], up_ref[...]) + up_bias_ref[...]
        grad_act = dot_nt(cot_ref[seq], down_ref[...])
        square = pre * pre
        bent = jnp.tanh(pre * (GELU_C + (GELU_C * GELU_A) * square))
        half = 0.5 + 0.5 * bent
        act = (pre * half).astype(BF16)
        slope = half + (0.5 * pre) * (1.0 - bent * bent) * (
            GELU_C + (3.0 * GELU_C * GELU_A) * square
        )
        grad_pre = (grad_act * slope).astype(BF16)
        up_sum = up_sum + jnp.sum(grad_pre.astype(F32), 0, keepdims=True)
        act_t_ref[:, at] = act.T
        pre_t_ref[:, at] = grad_pre.T
        forward = dot_nn(act, down_ref[...])
        back = dot_nt(grad_pre, up_ref[...])

        forward_ref[at, :] += forward
        back_ref[at, :] += back

    up_sum_ref[...] = up_sum

    @pl.when(step == steps - 1)
    def _():
        gain_sum = jnp.zeros((1, depth), F32)
        bias_sum = jnp.zeros((1, depth), F32)
        made = []
        for seq in range(count):
            at = slice(seq * rows, (seq + 1) * rows)
            block_ref[seq] = (resid_ref[at, :] + forward_ref[at, :]).astype(BF16)
            cot = cot_ref[seq].astype(F32)
            hat = hat_ref[at, :]
            back = back_ref[at, :]
            gain_sum = gain_sum + jnp.sum(back * hat, 0, keepdims=True)
            bias_sum = bias_sum + jnp.sum(cot, 0, keepdims=True)
            grad = cot + norm_back(back * gain_ref[...], hat, inv_ref[at, :])
            resid_grad_ref[at, :] = grad
            low = grad.astype(BF16)
            attended_ref[:, at] = low.T
            made.append(dot_nt(low, weight_ref[...]))
        sums_ref[0:1, :] = gain_sum
        sums_ref[1:2, :] = bias_sum
        for d in range(zones):
            mine = [value[:, d * width : (d + 1) * width] for value in made]
            grads[d][...] = interleave(mine, heads, size).astype(BF16)


def feed(place, pieces, x, cot, project, gain, up, up_bias, down, down_bias, heads):
    zones = len(pieces)
    count, rows, depth = x.shape
    size = depth // zones // heads
    hidden = up.shape[1]
    tile = min(512, hidden)
    steps = hidden // tile
    tokens = count * rows
    wide = pieces[0].shape[1]
    shapes = [jax.ShapeDtypeStruct((rows, wide), BF16)] * zones + [
        far((count, rows, depth), BF16),
        far((tokens, depth), F32),
        far((hidden, tokens), BF16),
        far((hidden, tokens), BF16),
        far((tokens, depth), BF16),
        far((tokens, depth), BF16),
        far((depth, tokens), BF16),
        jax.ShapeDtypeStruct((1, hidden), F32),
        jax.ShapeDtypeStruct((2, depth), F32),
    ]
    return pl.pallas_call(
        functools.partial(feed_kernel, zones, heads, size, steps),
        grid_spec=pltpu.PrefetchScalarGridSpec(
            num_scalar_prefetch=1,
            grid=(steps,),
            in_specs=[whole((rows, wide))] * zones
            + [
                whole(x.shape),
                whole(cot.shape),
                whole(project.shape),
                whole(gain.shape),
                pl.BlockSpec((depth, tile), lambda f, *_: (0, f)),
                pl.BlockSpec((1, tile), lambda f, *_: (0, f)),
                pl.BlockSpec((tile, depth), lambda f, *_: (f, 0)),
                whole(down_bias.shape),
            ],
            out_specs=[whole((rows, wide))] * zones
            + [
                whole((count, rows, depth)),
                whole((tokens, depth)),
                pl.BlockSpec((tile, tokens), lambda f, *_: (f, 0)),
                pl.BlockSpec((tile, tokens), lambda f, *_: (f, 0)),
                whole((tokens, depth)),
                whole((tokens, depth)),
                whole((depth, tokens)),
                pl.BlockSpec((1, tile), lambda f, *_: (0, f)),
                whole((2, depth)),
            ],
            scratch_shapes=[
                pltpu.VMEM((depth, depth), BF16),
                pltpu.VMEM((tokens, depth), F32),
                pltpu.VMEM((tokens, depth), F32),
                pltpu.VMEM((tokens, 1), F32),
                pltpu.VMEM((tokens, depth), F32),
                pltpu.VMEM((tokens, depth), F32),
            ],
        ),
        out_shape=shapes,
        compiler_params=params(28),
        cost_estimate=cost(
            8 * tokens * depth * hidden + 4 * tokens * depth * depth,
            4 * depth * hidden + 4 * tokens * hidden + 20 * tokens * depth,
            tokens * hidden,
        ),
        name="feed",
    )(
        place,
        *map(kept, pieces),
        kept(x),
        kept(cot),
        kept(project),
        gain,
        kept(up),
        up_bias,
        kept(down),
        down_bias,
    )


def relative_block(step, odd, ranks):
    rest = ranks // 8
    return odd + 2 * (step // rest) + 8 * lax.rem(step, rest)


def group_rows(rows, zones):
    return -(-rows // (8 * zones)) * 8


def pack(block, d, zones):
    rows, depth = block.shape
    width, group = depth // zones, group_rows(rows, zones)
    parts = []
    for k in range(zones):
        if k * group < rows:
            parts.append(block[k * group : (k + 1) * group, d * width : (d + 1) * width])
        else:
            parts.append(jnp.zeros((group, width), block.dtype))
    return jnp.concatenate(parts, axis=1)


def unpack(packed, rows, zones):
    group, depth = packed.shape
    spread = packed.reshape(group, zones, depth // zones).swapaxes(0, 1)
    return spread.reshape(group * zones, depth // zones)[:rows]


def place_first(second):
    return second // 2 + 2 * (1 - lax.rem(second, 2))


def place_second(second):
    return lax.rem(second + 2, 4)


def weights_kernel(zones, chunks, place_ref, *refs):
    acts, pres = refs[:chunks], refs[chunks : 2 * chunks]
    attends = refs[2 * chunks : 3 * chunks]
    norms, cots = refs[3 * chunks : 4 * chunks], refs[4 * chunks : 5 * chunks]
    mixes = refs[5 * chunks : 6 * chunks]
    first_ref, second_ref, scratch_ref = refs[6 * chunks :]
    part = scratch_ref.shape[1] // zones

    def total(lefts, rights):
        result = dot_nn(lefts[0][...], rights[0][...])
        for left, right in zip(lefts[1:], rights[1:]):
            result = result + dot_nn(left[...], right[...])
        return result

    scratch_ref[0] = total(pres, norms)
    scratch_ref[1] = total(acts, cots)
    square = total(attends, mixes)
    for d in range(zones):
        at = pl.ds(pl.multiple_of(lax.rem(place_ref[0] + d, zones) * part, 8), part)
        parts = [scratch_ref[0, at, :], scratch_ref[1, at, :], pack(square, -d % zones, zones)]
        used = sum(value.shape[0] for value in parts)
        parts.append(jnp.zeros((first_ref.shape[2] - used, first_ref.shape[3]), F32))
        side, number = (first_ref, d) if d < zones // 2 else (second_ref, d - zones // 2)
        side[0, number] = jnp.concatenate(parts, axis=0).astype(BF16)


def weight_grads(place, acts, pres, attends, norms, cots, mixes, odd, zones, ranks):
    chunks = len(acts)
    hidden, tokens = acts[0].shape
    depth = norms[0].shape[1]
    tile, square = hidden // ranks, depth // ranks
    rows = 2 * tile // zones + group_rows(square, zones)
    rows = -(-rows // 16) * 16
    rest = ranks // 8

    def tall(step, place_ref):
        return (lax.bitwise_xor(place_ref[1], relative_block(step, odd, ranks)), 0)

    def first(step, _):
        return (place_first(step // rest) * rest + lax.rem(step, rest), 0, 0, 0)

    def second(step, _):
        return (place_second(step // rest) * rest + lax.rem(step, rest), 0, 0, 0)

    shape = (ranks // 2, zones // 2, rows, depth)
    return pl.pallas_call(
        functools.partial(weights_kernel, zones, chunks),
        grid_spec=pltpu.PrefetchScalarGridSpec(
            num_scalar_prefetch=1,
            grid=(ranks // 2,),
            in_specs=[pl.BlockSpec((tile, tokens), tall)] * (2 * chunks)
            + [pl.BlockSpec((square, tokens), tall)] * chunks
            + [whole((tokens, depth))] * (3 * chunks),
            out_specs=[pl.BlockSpec((1, *shape[1:]), first), pl.BlockSpec((1, *shape[1:]), second)],
            scratch_shapes=[pltpu.VMEM((2, tile, depth), F32)],
        ),
        out_shape=[far(shape, BF16)] * 2,
        compiler_params=params(24),
        cost_estimate=cost(
            2 * chunks * hidden * tokens * depth,
            2 * chunks * hidden * tokens + 2 * hidden * depth + 4 * chunks * tokens * depth,
        ),
        name="weights",
    )(
        place,
        *map(kept, acts),
        *map(kept, pres),
        *map(kept, attends),
        *map(kept, norms),
        *map(kept, cots),
        *map(kept, mixes),
    )


def store_square(place_ref, outs, scratch_ref, extra_ref, zones, ranks):
    depth = scratch_ref.shape[0]
    part = depth // ranks
    for odd, out_ref in zip((1, 0), outs):
        for step in range(ranks // 2):
            rest = ranks // 8
            relative = odd + 2 * (step // rest) + 8 * (step % rest)
            rank = lax.bitwise_xor(place_ref[1], relative)
            block = scratch_ref[pl.ds(pl.multiple_of(rank * part, 8), part), :]
            for d in range(zones):
                zone = lax.rem(place_ref[0] + d, zones)
                line = extra_ref[pl.ds(rank * zones + zone, 1), :]
                packed = pack(block, d, zones)
                below = jnp.broadcast_to(line, (out_ref.shape[2] - packed.shape[0], depth))
                out_ref[step, d] = jnp.concatenate([packed, below], axis=0).astype(BF16)


def logits_kernel(
    zones, chunks, count, heads, size, rows, ranks, place_ref, lengths_ref, *refs
):
    grads = refs[: chunks * zones]
    values = refs[chunks * zones : 2 * chunks * zones]
    refs = refs[2 * chunks * zones :]
    logit_ref, sends, keeps = refs[0], refs[1:3], refs[3:5]
    long_ref, short_ref, value_ref, out_ref = refs[5:]
    place = place_ref[0]
    lanes = count * size
    step = pl.program_id(0)

    @pl.when(step == 0)
    def _():
        lane = lax.broadcasted_iota(jnp.int32, (1, lanes), 1)
        for c in range(chunks):
            is_long = jnp.zeros((1, lanes), jnp.bool_)
            for seq in range(count):
                inside = (lane >= seq * size) & (lane < (seq + 1) * size)
                is_long = is_long | (inside & (lengths_ref[c * count + seq] > SHORT))
            for d in range(zones):
                ahead = lax.rem(place + d, zones)
                behind = lax.rem(place + zones - d, zones)
                to = pl.ds(pl.multiple_of(ahead * rows, rows), rows)
                back = pl.ds(pl.multiple_of(behind * rows, rows), rows)
                for head in range(heads):
                    columns = slice(head * lanes, (head + 1) * lanes)
                    own = slice(c * lanes, (c + 1) * lanes)
                    grad = grads[c * zones + d][:, columns].astype(F32)
                    long_ref[head, to, own] = jnp.where(is_long, grad, 0.0).astype(BF16)
                    value_ref[head, back, own] = values[c * zones + d][:, columns]

                    @pl.when(ahead == 0)
                    def _():
                        short_ref[head, :, own] = jnp.where(is_long, 0.0, grad).astype(BF16)

    odd = jnp.where(step < ranks // 2, 1, 0)
    rank = lax.bitwise_xor(
        place_ref[1], relative_block(lax.rem(step, ranks // 2), odd, ranks)
    )
    part = logit_ref.shape[1]
    middle = part // 2
    start = rank * part
    for head in range(heads):
        logits = logit_ref[head].astype(F32)
        raised = jnp.exp(logits - jnp.max(logits, -1, keepdims=True))
        probs = raised / jnp.sum(raised, -1, keepdims=True)
        at = pl.ds(pl.multiple_of(start, part), part)
        total = dot_nt(long_ref[head, at, :], value_ref[head])
        out_ref[head] = probs * (total - jnp.sum(total * probs, -1, keepdims=True))

        @pl.when(start < SHORT)
        def _():
            corner = logits[:, :SHORT]
            lifted = jnp.exp(corner - jnp.max(corner, -1, keepdims=True))
            small = lifted / jnp.sum(lifted, -1, keepdims=True)
            sums = dot_nt(short_ref[head, at, :], value_ref[head, :SHORT, :])
            more = small * (sums - jnp.sum(sums * small, -1, keepdims=True))
            out_ref[head, :, :SHORT] += more

    @pl.when(step < ranks // 2)
    def _():
        sends[0][0] = out_ref[:, :middle, :].astype(BF16)
        sends[1][0] = out_ref[:, middle:, :].astype(BF16)

    @pl.when(step >= ranks // 2)
    def _():
        keeps[0][0] = out_ref[:, :middle, :].astype(BF16)
        keeps[1][0] = out_ref[:, middle:, :].astype(BF16)


def logit_grads(place, lengths, grads, values, logits, ranks, count):
    chunks, zones = len(grads), len(grads[0])
    heads, full, _ = logits.shape
    rows, wide = grads[0][0].shape
    size = wide // heads // count
    part = full // ranks
    half, rest = ranks // 2, ranks // 8

    def pick(step, place_ref, _):
        odd = jnp.where(step < half, 1, 0)
        block = relative_block(lax.rem(step, half), odd, ranks)
        return (0, lax.bitwise_xor(place_ref[1], block), 0)

    def spec(order, keep):
        def number(step, *_):
            at = jnp.maximum(step - half, 0) if keep else jnp.minimum(step, half - 1)
            return (order(at // rest) * rest + lax.rem(at, rest), 0, 0, 0)

        return pl.BlockSpec((1, heads, part // 2, full), number)

    flat = [piece for group in grads for piece in group] + [
        piece for group in values for piece in group
    ]
    every = chunks * count * size
    shape = (half, heads, part // 2, full)
    return pl.pallas_call(
        functools.partial(logits_kernel, zones, chunks, count, heads, size, rows, ranks),
        grid_spec=pltpu.PrefetchScalarGridSpec(
            num_scalar_prefetch=2,
            grid=(ranks,),
            in_specs=[whole((rows, wide))] * len(flat)
            + [pl.BlockSpec((heads, part, full), pick)],
            out_specs=[
                spec(order, keep) for keep in (False, True) for order in (place_first, place_second)
            ],
            scratch_shapes=[
                pltpu.VMEM((heads, full, every), BF16),
                pltpu.VMEM((heads, SHORT, every), BF16),
                pltpu.VMEM((heads, full, every), BF16),
                pltpu.VMEM((heads, part, full), F32),
            ],
        ),
        out_shape=[far(shape, BF16)] * 4,
        compiler_params=params(24),
        cost_estimate=cost(
            2 * heads * full * full * every, 4 * heads * full * full, heads * full * full
        ),
        name="logits",
    )(place, lengths, *map(kept, flat), kept(logits))


def input_kernel(zones, heads, size, ranks, count, place_ref, *refs):
    pieces = refs[:zones]
    x_ref, gain_ref, weight_ref, resid_ref, extra_in_ref = refs[zones : zones + 5]
    grad_ref, send_ref, keep_ref, total_ref, gain_sum_ref, extra_ref = refs[zones + 5 :]
    depth = x_ref.shape[2]
    seq = pl.program_id(0)

    @pl.when(seq == 0)
    def _():
        total_ref[...] = jnp.zeros_like(total_ref)
        gain_sum_ref[...] = jnp.zeros_like(gain_sum_ref)

    hat, inverse = norm_of(x_ref[0].astype(F32))
    norm = (hat * gain_ref[...]).astype(BF16)
    pair = 128 // size
    parts = []
    lane = lax.broadcasted_iota(jnp.int32, (1, 128), 1)
    for piece in pieces:
        for head in range(heads):
            at = pl.multiple_of((head * count + seq // pair * pair) * size, 128)
            both = piece[:, pl.ds(at, 128)].astype(F32)
            moved = pltpu.roll(both, shift=size, axis=1)
            parts.append(jnp.where(lax.rem(seq, pair) == 0, both, moved)[:, :size])
    back = jnp.concatenate(parts, axis=1).astype(BF16)
    grad_norm = dot_nn(back, weight_ref[...])
    gain_sum_ref[...] += jnp.sum(grad_norm * hat, 0, keepdims=True)
    grad = resid_ref[...] + norm_back(grad_norm * gain_ref[...], hat, inverse)
    grad_ref[0] = grad.astype(BF16)
    total_ref[...] += dot_tn(norm, back)

    @pl.when(seq == count - 1)
    def _():
        extra_ref[...] = extra_in_ref[...]
        share = depth // ranks // zones
        for index in range(ranks * zones):
            extra_ref[index : index + 1, :share] = gain_sum_ref[
                :, index * share : (index + 1) * share
            ]
        store_square(place_ref, (send_ref, keep_ref), total_ref, extra_ref, zones, ranks)


def input_grads(place, pieces, x, gain, weight, resid, extra, heads, ranks):
    zones = len(pieces)
    count, rows, depth = x.shape
    size = depth // zones // heads
    assert 2 * size == 128 and count % 2 == 0
    height = -(-(group_rows(depth // ranks, zones) + 1) // 16) * 16
    shape = (ranks // 2, zones, height, depth)
    return pl.pallas_call(
        functools.partial(input_kernel, zones, heads, size, ranks, count),
        grid_spec=pltpu.PrefetchScalarGridSpec(
            num_scalar_prefetch=1,
            grid=(count,),
            in_specs=[whole(pieces[0].shape)] * zones
            + [
                pl.BlockSpec((1, rows, depth), lambda s, *_: (s, 0, 0)),
                whole(gain.shape),
                whole(weight.shape),
                pl.BlockSpec((rows, depth), lambda s, *_: (s, 0)),
                whole(extra.shape),
            ],
            out_specs=[
                pl.BlockSpec((1, rows, depth), lambda s, *_: (s, 0, 0)),
                whole(shape),
                whole(shape),
            ],
            scratch_shapes=[
                pltpu.VMEM((depth, depth), F32),
                pltpu.VMEM((1, depth), F32),
                pltpu.VMEM(extra.shape, F32),
            ],
        ),
        out_shape=[
            far(x.shape, BF16),
            jax.ShapeDtypeStruct(shape, BF16),
            jax.ShapeDtypeStruct(shape, BF16),
        ],
        compiler_params=params(24),
        cost_estimate=cost(
            4 * count * rows * depth * depth, 12 * count * rows * depth + 8 * depth * depth
        ),
        name="input",
    )(place, *map(kept, pieces), kept(x), gain, kept(weight), kept(resid), extra)


def shift(value, axis, extent, by):
    by = by % extent
    return lax.ppermute(value, axis, [(i, (i + by) % extent) for i in range(extent)])


def flip(value, axis, extent, mask):
    return lax.ppermute(value, axis, [(i, i ^ mask) for i in range(extent)])


def widen(value):
    return value.astype(F32)


def after(value, *results):
    return lax.optimization_barrier((value, *results))[0]


def exchange(pieces, extent, sign, *results):
    sent = pieces[1:]
    if results:
        sent = lax.optimization_barrier((*sent, *results))[: extent - 1]
    return [pieces[0]] + [
        shift(piece, "head", extent, sign * (d + 1)) for d, piece in enumerate(sent)
    ]


def exchange_some(pieces, numbers, extent, sign, *results):
    sent = [pieces[d] for d in numbers]
    if results:
        sent = lax.optimization_barrier((*sent, *results))[: len(sent)]
    return [shift(piece, "head", extent, sign * d) for d, piece in zip(numbers, sent)]


class Reduce:
    masks = ((2, 4), (4, 2))

    def __init__(self, ranks):
        self.ranks = ranks

    def core(self, sends):
        self.came = [flip(send, "dp", self.ranks, 1) for send in sends]

    def first(self, keeps, *results):
        half = self.ranks // 4
        sent = [
            (widen(keep[:half]) + widen(came[:half])).astype(BF16)
            for keep, came in zip(keeps, self.came)
        ]
        if results:
            sent = lax.optimization_barrier((*sent, *results))[:2]
        self.keeps = keeps
        self.went = [
            flip(value, "dp", self.ranks, masks[0]) for value, masks in zip(sent, self.masks)
        ]

    def second(self, *results):
        half, rest = self.ranks // 4, self.ranks // 8
        rests = [
            widen(keep[half:]) + widen(came[half:]) + widen(went)
            for keep, came, went in zip(self.keeps, self.came, self.went)
        ]
        self.own = [value[:rest] for value in rests]
        sent = [value[rest:].astype(BF16) for value in rests]
        if results:
            sent = lax.optimization_barrier((*sent, *results))[:2]
        self.last = [
            flip(value, "dp", self.ranks, masks[1]) for value, masks in zip(sent, self.masks)
        ]

    def finish(self):
        sides = []
        for own, last in zip(self.own, self.last):
            total = own + widen(last)
            side = total[0]
            for third in range(1, self.ranks // 8):
                side = side + widen(flip(total[third].astype(BF16), "dp", self.ranks, 8 * third))
            sides.append(side)
        return sides


def reduce_direct(send, keep, ranks, *results):
    rest = ranks // 8
    came = flip(send, "dp", ranks, 1)
    both = [
        widen(keep[q * rest : (q + 1) * rest]) + widen(came[q * rest : (q + 1) * rest])
        for q in range(4)
    ]
    sent = lax.optimization_barrier((*(part.astype(BF16) for part in both[1:]), *results))
    total = both[0]
    for q in range(1, 4):
        total = total + widen(flip(sent[q - 1], "dp", ranks, 2 * q))
    own = total[0]
    for third in range(1, rest):
        own = own + widen(flip(total[third].astype(BF16), "dp", ranks, 8 * third))
    return own


def reduce_head(blocks, zones, *results):
    sent = [block.astype(BF16) for block in blocks[1:]]
    if results:
        sent = lax.optimization_barrier((*sent, *results))[: zones - 1]
    total = blocks[0]
    for d in range(1, zones):
        total = total + widen(shift(sent[d - 1], "head", zones, d))
    return total


def local(
    zones,
    ranks,
    block_input,
    lengths,
    cotangent,
    norm1_gain,
    value_projection_weight,
    rand_logits,
    output_projection_weight,
    norm2_gain,
    up_projection_weight,
    up_bias,
    down_projection_weight,
    down_bias,
):
    seq_count, rows, depth = block_input.shape
    heads, full, _ = rand_logits.shape
    hidden = up_bias.shape[0]
    assert rows == SHORT and full == rows * zones and ranks % 8 == 0
    count = seq_count // 2
    assert seq_count == 2 * count
    place = jnp.stack([lax.axis_index("head"), lax.axis_index("dp")]).astype(jnp.int32)
    gain1, gain2 = norm1_gain[None], norm2_gain[None]
    width = value_projection_weight.shape[1]

    slot = width // ranks
    project = lax.dynamic_slice_in_dim(output_projection_weight, place[1] * slot, slot, 0)
    project = lax.all_gather(project, ("head", "dp"), axis=0, tiled=True)

    own = value_projection_weight.T
    half = width // 2
    parity = lax.rem(place[1], 2)
    part_rows = lax.dynamic_slice_in_dim(own, parity * half, half, 0)
    mine = [shift(part_rows, "head", zones, -d) for d in range(1, zones)]
    probs, probs_t, corner, corner_t = make_probs(rand_logits)
    others = flip(after(jnp.stack(mine), corner), "dp", ranks, 1)
    place = after(place, corner)

    def part(array, c):
        return array[c * count : (c + 1) * count]

    def call_values(place, c, weights):
        return make_values(place, part(block_input, c), gain1, weights, zones, heads, c == 0)

    def call_feed(place, c, pieces):
        return feed(
            place,
            pieces,
            part(block_input, c),
            part(cotangent, c),
            project,
            gain2,
            up_projection_weight,
            up_bias[None],
            down_projection_weight,
            down_bias[None],
            heads,
        )

    made = call_values(place, 0, [own, *mine, others])
    weight = made[zones]
    place = after(place, weight)
    values0 = exchange(made[:zones], zones, 1)
    made = call_values(place, 1, [weight])
    place = after(place, made[0])
    values1 = exchange(made, zones, 1, *values0)

    made = mix(place, part(lengths, 0), [values0], probs, corner, count, 1)
    place = after(place, made[0])
    mixed0 = exchange(made, zones, 1, *values1)
    made = mix(place, part(lengths, 1), [values1], probs, corner, count, 1)
    place = after(place, made[0])
    mixed1 = exchange(made, zones, 1, *mixed0)

    feed0 = call_feed(place, 0, mixed0)
    place = after(place, feed0[0])
    grads0 = exchange(feed0[:zones], zones, -1, *mixed1)
    feed1 = call_feed(place, 1, mixed1)
    place = after(place, feed1[0], *grads0)
    blocks, resids, acts, pres, norms, mixes, attends, up_sums, sums = zip(
        feed0[zones:], feed1[zones:]
    )
    cots = [part(cotangent, c).reshape(count * rows, depth) for c in range(2)]

    weight_sum, rand_sum = Reduce(ranks), Reduce(ranks)

    def call_weights(place, odd):
        return weight_grads(
            place, acts, pres, attends, norms, cots, mixes, odd, zones, ranks
        )

    grads1 = exchange(feed1[:zones], zones, -1, *grads0)
    sends = call_weights(place, 1)
    place = after(place, sends[0], *grads1)
    weight_sum.core([after(value, *grads1) for value in sends])
    made = mix(place, lengths, [grads0, grads1], probs_t, corner_t, count, -1)
    place = after(place, made[0])
    evens = exchange_some(made, range(2, zones, 2), zones, -1)
    keeps = call_weights(place, 0)
    place = after(place, keeps[0], *evens, *weight_sum.came)
    odds = exchange_some(made, range(1, zones, 2), zones, -1, *evens)
    backs = [made[0]] + [(odds if d % 2 else evens)[(d - 1) // 2] for d in range(1, zones)]
    weight_sum.first(keeps, *evens)
    rand = logit_grads(
        place, lengths, (grads0, grads1), (values0, values1), rand_logits, ranks, count
    )
    place = after(place, rand[0], *weight_sum.went, *odds)

    rand_sum.core([after(value, *weight_sum.went, *odds) for value in rand[:2]])
    weight_sum.second(rand[0], *odds)
    place = after(place, *rand_sum.came)

    up_total = (up_sums[0] + up_sums[1]).reshape(ranks * zones, -1)
    rest_total = sums[0] + sums[1]
    gain_total, bias_total = (
        rest_total[i].reshape(ranks * zones, -1) for i in range(2)
    )
    up_size, gain_size = hidden // ranks // zones, depth // ranks // zones
    extra = jnp.concatenate([jnp.zeros_like(gain_total), gain_total, bias_total, up_total], 1)
    extra = jnp.pad(extra, ((0, 0), (0, depth - extra.shape[1])))

    rand_sum.first(rand[2:], *backs)
    resid = jnp.concatenate(resids, 0)
    grad_x, value_send, value_keep = input_grads(
        place, backs, block_input, gain1, weight, resid, extra, heads, ranks
    )
    sides = weight_sum.finish()
    blocks_ff = [side[d] for side in sides for d in range(zones // 2)]
    ff = reduce_head(blocks_ff, zones)
    rand_sum.second(value_send)
    value_own = reduce_direct(value_send, value_keep, ranks, *rand_sum.went)
    value_total = reduce_head([value_own[d] for d in range(zones)], zones)
    grad_rand = jnp.concatenate(rand_sum.finish(), 1)

    tile, square = hidden // ranks // zones, depth // ranks
    group = group_rows(square, zones)
    line = value_total[group]
    return (
        jnp.concatenate(blocks, 0),
        grad_x,
        grad_rand,
        unpack(value_total[:group], square, zones),
        unpack(ff[2 * tile : 2 * tile + group], square, zones).T,
        line[:gain_size],
        line[gain_size : 2 * gain_size],
        ff[:tile].T,
        line[3 * gain_size : 3 * gain_size + up_size],
        ff[tile : 2 * tile],
        line[2 * gain_size : 3 * gain_size],
    )


def solution(mesh):
    in_specs = (
        P("dp", "head", None),
        P("dp"),
        P("dp", "head", None),
        P(),
        P(None, "head"),
        P("head", None, None),
        P("head", None),
        P(),
        P(),
        P(),
        P(),
        P(),
    )
    out_specs = (
        P("dp", "head", None),
        P("dp", "head", None),
        P("head", "dp", None),
        P("dp", "head"),
        P("head", "dp"),
        P(("dp", "head")),
        P(("dp", "head")),
        P(None, ("dp", "head")),
        P(("dp", "head")),
        P(("dp", "head"), None),
        P(("dp", "head")),
    )
    body = functools.partial(local, mesh.shape["head"], mesh.shape["dp"])
    return jax.shard_map(
        body, mesh=mesh, in_specs=in_specs, out_specs=out_specs, check_vma=False
    )
```

time: 468 us -> 328 us (0.70); the launches traced: 462 us -> 327 us
  waiting for transfers between devices: 141 us -> 78 us
  Pallas kernels: 163 us -> 132 us
  starting transfers between devices: 88.2 us -> 64.6 us
  local copies, waits for them, and re-layouts: 25.5 us -> 13.9 us
  other arithmetic: 28.9 us -> 23.5 us
    all_gather x1, waiting for transfers between devices: 45.6 us -> 0.01 us  [local(): project = lax.all_gather(project, ('head', 'dp'), axis=0, tiled=True)]
    ppermute x16 -> x17, waiting for transfers between devices: 68.5 us -> 41.6 us  [flip(): return lax.ppermute(value, axis, [(i, i ^ mask) for i in range(extent)])]
    ppermute x36 -> x30, starting transfers between devices: 73.2 us -> 48.4 us  [shift(): lax.ppermute(value, axis, [(i, (i + by) % extent) for i in range(extent)])]
    pallas_call x7 -> x5, Pallas kernels: 40.6 us -> 21.3 us  [the longest x3 16.8 us: mix(): pl.pallas_call(functools.partial(mix_kernel, zones, chunks, count, lanes...]
    ppermute x36 -> x30, waiting for transfers between devices: 27.1 us -> 36.3 us  [shift(): lax.ppermute(value, axis, [(i, (i + by) % extent) for i in range(extent)])]
    pallas_call x2, Pallas kernels: 49.5 us -> 42.8 us  [feed(): pl.pallas_call(functools.partial(feed_kernel, zones, heads, size, steps),...]
    pallas_call x2 -> x1, Pallas kernels: 15.5 us -> 9.75 us  [input_grads(): pl.pallas_call(functools.partial(input_kernel, zones, heads, size, ranks,...]
    convert_element_type x4 -> x5, other arithmetic: 10.2 us -> 7.25 us  [the longest x4 7.1 us: first(): (widen(keep[:half]) + widen(came[:half])).astype(BF16)]
  transfers between devices with their start and end apart: 53 -> 48, of which waited for: 13 -> 17; matrix products, arithmetic and copies ran while one was open for 10% -> 9% of each run, Pallas kernels for 27% -> 40%
where the time goes in v2:
time: 328 us; the launch traced here: 327 us
  Pallas kernels  132 us (40%)
  waiting for transfers between devices  78 us (24%)
  starting transfers between devices  64.6 us (20%)
  other arithmetic  23.5 us (7%)
  between operations  14.9 us (5%)
  local copies, waits for them, and re-layouts  13.9 us (4%)
    ppermute x30, starting transfers between devices, shift(): lax.ppermute(value, axis, [(i, (i + by) % extent) for i in range(extent)])  48.4 us
    pallas_call x2, Pallas kernels, feed(): pl.pallas_call(functools.partial(feed_kernel, zones, heads, size, steps),...  42.8 us
    ppermute x17, waiting for transfers between devices, flip(): return lax.ppermute(value, axis, [(i, i ^ mask) for i in range(extent)])  41.6 us
    ppermute x30, waiting for transfers between devices, shift(): lax.ppermute(value, axis, [(i, (i + by) % extent) for i in range(extent)])  36.3 us
    pallas_call x2, Pallas kernels, weight_grads(): pl.pallas_call(functools.partial(weights_kernel, zones, chunks), grid_spe...  26.6 us
    pallas_call x1, Pallas kernels, logit_grads(): pl.pallas_call(functools.partial(logits_kernel, zones, chunks, count, hea...  18.1 us
    pallas_call x3, Pallas kernels, mix(): pl.pallas_call(functools.partial(mix_kernel, zones, chunks, count, lanes...  16.8 us
    ppermute x17, starting transfers between devices, flip(): return lax.ppermute(value, axis, [(i, i ^ mask) for i in range(extent)])  16.1 us
  transfers between devices with their start and end apart: 48, of which 17 were waited for; matrix products, arithmetic and copies ran while one was open for 9% of the time, Pallas kernels for 40%

profile of v2, /device:TPU:0, one launch (start us, length us, event | category | flops | bytes accessed | tf_op | source)
XLA Modules:
  0.0 327.3 jit_solution(3084613976287501068)
XLA Ops:
  9.7 5.1 %collective-permute-start = (bf16[96,768]{1,0:T(8,128)(2,1)S(1)}, bf16[96,768]{1,0:T(8,128)(2,1)S(1)}, u32[]{:S(2)}, u32[]{:S(2)}) collective-permute-start(bf16[96,768]{1,0:T(8,128)(2,1)S(1)} %dynamic-slice_bitcast_fusion), channel_id=1, source_target_pairs={{0,3},{1,0},{2,1},{3,2},{4,7},{5,4},{6,5},{7,6},{8,11},{9,8},{10,9... | collective-permute-start | bytes 442376 | tf_op jit(solution)/shard_map/ppermute | solution.py:748
  15.9 14.0 %probs.1 = (bf16[3,1024,1024]{2,1,0:T(8,128)(2,1)}, bf16[3,1024,1024]{2,1,0:T(8,128)(2,1)}, bf16[3,256,256]{2,1,0:T(8,128)(2,1)S(1)}, bf16[3,256,256]{2,1,0:T(8,128)(2,1)S(1)}) custom-call(bf16[3,1024,1024]{2,1,0:T(8,128)(2,1)} %refs_16_.1), custom_call_target="tpu_custom_call" | custom-call | flops 31457280 | bytes 18874368 | tf_op jit(solution)/shard_map/probs/pallas_call | solution.py:109
  45.0 8.5 %collective-permute-done.5.refs_2_.refs_10_ = bf16[256,384]{1,0:T(8,128)(2,1)S(1)} collective-permute-done((bf16[256,384]{1,0:T(8,128)(2,1)S(1)}, bf16[256,384]{1,0:T(8,128)(2,1)S(1)}, u32[]{:S(2)}, u32[]{:S(2)}) %collective-permute-start.5) | collective-permute-done | bytes 196640 | tf_op jit(solution)/shard_map/ppermute | solution.py:748
  53.5 4.9 %collective-permute-start.7 = (bf16[256,384]{1,0:T(8,128)(2,1)S(1)}, bf16[256,384]{1,0:T(8,128)(2,1)S(1)}, u32[]{:S(2)}, u32[]{:S(2)}) collective-permute-start(bf16[256,384]{1,0:T(8,128)(2,1)S(1)} %get-tuple-element.135), channel_id=1, source_target_pairs={{0,1},{1,2},{2,3},{3,0},{4,5},{5,6},{6,7},{7,4},{8,9},{9,10},{10,1... | collective-permute-start | bytes 589832 | tf_op jit(solution)/shard_map/ppermute | solution.py:748
  60.9 5.6 %mix.3 = (bf16[256,384]{1,0:T(8,128)(2,1)S(1)}, bf16[256,384]{1,0:T(8,128)(2,1)S(1)}, bf16[256,384]{1,0:T(8,128)(2,1)S(1)}, bf16[256,384]{1,0:T(8,128)(2,1)S(1)}) custom-call(s32[2]{0:T(128)S(1)} %pad_add_fusion.place_ref, s32[2]{0:T(128)S(1)} %get-tuple-element.258.long_flags, bf16[256,384]{1,0:T(8,128)(2,1)S(1)} %get-tuple-element.125.refs_0_.refs_8_, ...), custom_call_target="tpu_custom_call" | custom-call | flops 805306368 | bytes 7864320 | tf_op jit(solution)/shard_map/mix/pallas_call | solution.py:213
  67.1 7.7 %collective-permute-done.8.refs_2_.refs_14_ = bf16[256,384]{1,0:T(8,128)(2,1)S(1)} collective-permute-done((bf16[256,384]{1,0:T(8,128)(2,1)S(1)}, bf16[256,384]{1,0:T(8,128)(2,1)S(1)}, u32[]{:S(2)}, u32[]{:S(2)}) %collective-permute-start.8) | collective-permute-done | bytes 196640 | tf_op jit(solution)/shard_map/ppermute | solution.py:748
  74.8 5.3 %collective-permute-start.10 = (bf16[256,384]{1,0:T(8,128)(2,1)S(1)}, bf16[256,384]{1,0:T(8,128)(2,1)S(1)}, u32[]{:S(2)}, u32[]{:S(2)}) collective-permute-start(bf16[256,384]{1,0:T(8,128)(2,1)S(1)} %get-tuple-element.143), channel_id=1, source_target_pairs={{0,1},{1,2},{2,3},{3,0},{4,5},{5,6},{6,7},{7,4},{8,9},{9,10},{10,1... | collective-permute-start | bytes 589832 | tf_op jit(solution)/shard_map/ppermute | solution.py:748
  84.0 5.5 %mix.4 = (bf16[256,384]{1,0:T(8,128)(2,1)S(1)}, bf16[256,384]{1,0:T(8,128)(2,1)S(1)}, bf16[256,384]{1,0:T(8,128)(2,1)S(1)}, bf16[256,384]{1,0:T(8,128)(2,1)S(1)}) custom-call(s32[2]{0:T(128)S(1)} %pad_add_fusion.place_ref, s32[2]{0:T(128)S(1)} %get-tuple-element.257.long_flags, bf16[256,384]{1,0:T(8,128)(2,1)S(1)} %get-tuple-element.123.refs_0_.refs_12_, ...), custom_call_target="tpu_custom_call" | custom-call | flops 805306368 | bytes 7864320 | tf_op jit(solution)/shard_map/mix/pallas_call | solution.py:213
  90.2 4.6 %collective-permute-done.11.refs_2_ = bf16[256,384]{1,0:T(8,128)(2,1)S(1)} collective-permute-done((bf16[256,384]{1,0:T(8,128)(2,1)S(1)}, bf16[256,384]{1,0:T(8,128)(2,1)S(1)}, u32[]{:S(2)}, u32[]{:S(2)}) %collective-permute-start.11) | collective-permute-done | bytes 196640 | tf_op jit(solution)/shard_map/ppermute | solution.py:748
  94.8 4.7 %collective-permute-start.13 = (bf16[256,384]{1,0:T(8,128)(2,1)S(1)}, bf16[256,384]{1,0:T(8,128)(2,1)S(1)}, u32[]{:S(2)}, u32[]{:S(2)}) collective-permute-start(bf16[256,384]{1,0:T(8,128)(2,1)S(1)} %get-tuple-element.152), channel_id=1, source_target_pairs={{0,1},{1,2},{2,3},{3,0},{4,5},{5,6},{6,7},{7,4},{8,9},{9,10},{10,1... | collective-permute-start | bytes 589832 | tf_op jit(solution)/shard_map/ppermute | solution.py:748
  101.9 21.4 %feed.2 = (bf16[256,384]{1,0:T(8,128)(2,1)S(1)}, bf16[256,384]{1,0:T(8,128)(2,1)S(1)}, bf16[256,384]{1,0:T(8,128)(2,1)S(1)}, bf16[256,384]{1,0:T(8,128)(2,1)S(1)...) custom-call(s32[2]{0:T(128)S(1)} %pad_add_fusion.place_ref, ...), custom_call_target="tpu_custom_call" | custom-call | flops 10871635968 | bytes 23592960 | tf_op jit(solution)/shard_map/feed/pallas_call | solution.py:354
  126.1 21.4 %feed.3 = (bf16[256,384]{1,0:T(8,128)(2,1)S(1)}, bf16[256,384]{1,0:T(8,128)(2,1)S(1)}, bf16[256,384]{1,0:T(8,128)(2,1)S(1)}, bf16[256,384]{1,0:T(8,128)(2,1)S(1)...) custom-call(s32[2]{0:T(128)S(1)} %pad_add_fusion.place_ref, ...), custom_call_target="tpu_custom_call" | custom-call | flops 10871635968 | bytes 23592960 | tf_op jit(solution)/shard_map/feed/pallas_call | solution.py:354
  147.5 3.7 %collective-permute-start.19 = (bf16[256,384]{1,0:T(8,128)(2,1)S(1)}, bf16[256,384]{1,0:T(8,128)(2,1)S(1)}, u32[]{:S(2)}, u32[]{:S(2)}) collective-permute-start(bf16[256,384]{1,0:T(8,128)(2,1)S(1)} %get-tuple-element.178), channel_id=1, source_target_pairs={{0,3},{1,0},{2,1},{3,2},{4,7},{5,4},{6,5},{7,6},{8,11},{9,8},{10,9... | collective-permute-start | bytes 589832 | tf_op jit(solution)/shard_map/ppermute | solution.py:748
  151.9 13.3 %weights.2 = (bf16[4,2,224,768]{3,2,1,0:T(8,128)(2,1)}, bf16[4,2,224,768]{3,2,1,0:T(8,128)(2,1)}) custom-call(s32[2]{0:T(128)S(1)} %pad_add_fusion.place_ref, bf16[3072,512]{1,0:T(8,128)(2,1)} %get-tuple-element.164.refs_0_, bf16[3072,512]{1,0:T(8,128)(2,1)} %get-tuple-element.165.refs_1_, bf16[3072,512]{1,0:T(8,128)(2,1)} %get-tuple-element.166.refs_2_, ...), custom_call_target="tpu_custom_call" | custom-call | flops 4831838208 | bytes 14155776 | tf_op jit(solution)/shard_map/weights/pallas_call | solution.py:493
  168.2 5.8 %mix.5 = (bf16[256,768]{1,0:T(8,128)(2,1)S(1)}, bf16[256,768]{1,0:T(8,128)(2,1)S(1)}, bf16[256,768]{1,0:T(8,128)(2,1)S(1)}, bf16[256,768]{1,0:T(8,128)(2,1)S(1)}) custom-call(s32[2]{0:T(128)S(1)} %pad_add_fusion.place_ref, s32[4]{0:T(128)S(1)} %copy-done.21, bf16[256,384]{1,0:T(8,128)(2,1)S(1)} %get-tuple-element.147.refs_0_, ...), custom_call_target="tpu_custom_call" | custom-call | flops 1610612736 | bytes 9437184 | tf_op jit(solution)/shard_map/mix/pallas_call | solution.py:213
  176.3 13.3 %weights.3 = (bf16[4,2,224,768]{3,2,1,0:T(8,128)(2,1)}, bf16[4,2,224,768]{3,2,1,0:T(8,128)(2,1)}) custom-call(s32[2]{0:T(128)S(1)} %pad_add_fusion.place_ref, bf16[3072,512]{1,0:T(8,128)(2,1)} %get-tuple-element.164.refs_0_, bf16[3072,512]{1,0:T(8,128)(2,1)} %get-tuple-element.165.refs_1_, bf16[3072,512]{1,0:T(8,128)(2,1)} %get-tuple-element.166.refs_2_, ...), custom_call_target="tpu_custom_call" | custom-call | flops 4831838208 | bytes 14155776 | tf_op jit(solution)/shard_map/weights/pallas_call | solution.py:493
  200.1 18.1 %logits.1 = (bf16[4,3,64,1024]{3,2,1,0:T(8,128)(2,1)}, bf16[4,3,64,1024]{3,2,1,0:T(8,128)(2,1)}, bf16[4,3,64,1024]{3,2,1,0:T(8,128)(2,1)}, bf16[4,3,64,1024]{3,2,1,0:T(8,128)(2,1)}) custom-call(s32[2]{0:T(128)S(1)} %pad_add_fusion.place_ref, s32[4]{0:T(128)S(1)} %copy-done.21, bf16[256,384]{1,0:T(8,128)(2,1)} %copy-done.12, bf16[256,384]{1,0:T(8,128)(2,1)} %copy-done.13, ...), custom_call_target="tpu_custom_call" | custom-call | flops 1610612736 | bytes 12582912 | tf_op jit(solution)/shard_map/logits/pallas_call | solution.py:635
  218.2 9.0 %collective-permute-done.25 = bf16[2,2,224,768]{3,2,1,0:T(8,128)(2,1)S(1)} collective-permute-done((bf16[2,2,224,768]{3,2,1,0:T(8,128)(2,1)S(1)}, bf16[2,2,224,768]{3,2,1,0:T(8,128)(2,1)S(1)}, u32[]{:S(2)}, u32[]{:S(2)}) %collective-permute-start.25) | collective-permute-done | bytes 1376288 | tf_op jit(solution)/shard_map/ppermute | solution.py:752
  234.3 3.9 %pad_maximum_fusion.refs_7_ = f32[1024,768]{1,0:T(8,128)} fusion(f32[512,768]{1,0:T(8,128)} %get-tuple-element.206, f32[512,768]{1,0:T(8,128)} %get-tuple-element.205), kind=kLoop, calls=%fused_computation | loop fusion | flops 786432 | bytes 6291456 | tf_op jit(solution)/shard_map/concatenate | solution.py:976
  238.2 8.8 %collective-permute-done.44 = bf16[1,2,224,768]{3,2,1,0:T(8,128)(2,1)} collective-permute-done((bf16[1,2,224,768]{3,2,1,0:T(8,128)(2,1)}, bf16[1,2,224,768]{3,2,1,0:T(8,128)(2,1)}, u32[]{:S(2)}, u32[]{:S(2)}) %collective-permute-start.44) | collective-permute-done | bytes 688160 | tf_op jit(solution)/shard_map/ppermute | solution.py:752
  251.0 9.8 %input.1 = (bf16[4,256,768]{2,1,0:T(8,128)(2,1)}, bf16[4,4,32,768]{3,2,1,0:T(8,128)(2,1)S(1)}, bf16[4,4,32,768]{3,2,1,0:T(8,128)(2,1)S(1)}) custom-call(s32[2]{0:T(128)S(1)} %pad_add_fusion.place_ref, bf16[256,768]{1,0:T(8,128)(2,1)} %copy-done.22, bf16[256,768]{1,0:T(8,128)(2,1)} %copy-done.45, bf16[256,768]{1,0:T(8,128)(2,1)} %copy-done.44, ...), custom_call_target="tpu_custom_call" | custom-call | flops 2415919104 | bytes 14155776 | tf_op jit(solution)/shard_map/input/pallas_call | solution.py:709
  269.9 6.6 %collective-permute-done.45 = bf16[224,768]{1,0:T(8,128)(2,1)S(1)} collective-permute-done((bf16[224,768]{1,0:T(8,128)(2,1)S(1)}, bf16[224,768]{1,0:T(8,128)(2,1)S(1)}, u32[]{:S(2)}, u32[]{:S(2)}) %collective-permute-start.45) | collective-permute-done | bytes 344096 | tf_op jit(solution)/shard_map/ppermute | solution.py:748
  278.7 7.1 %collective-permute-done.32 = bf16[2,3,64,1024]{3,2,1,0:T(8,128)(2,1)} collective-permute-done((bf16[2,3,64,1024]{3,2,1,0:T(8,128)(2,1)}, bf16[2,3,64,1024]{3,2,1,0:T(8,128)(2,1)}, u32[]{:S(2)}, u32[]{:S(2)}) %collective-permute-start.32) | collective-permute-done | bytes 786464 | tf_op jit(solution)/shard_map/ppermute | solution.py:752
  310.8 5.7 %collective-permute-done.34 = bf16[1,3,64,1024]{3,2,1,0:T(8,128)(2,1)} collective-permute-done((bf16[1,3,64,1024]{3,2,1,0:T(8,128)(2,1)S(1)}, bf16[1,3,64,1024]{3,2,1,0:T(8,128)(2,1)}, u32[]{:S(2)}, u32[]{:S(2)}) %collective-permute-start.34) | collective-permute-done | bytes 393248 | tf_op jit(solution)/shard_map/ppermute | solution.py:752
  (247 shorter events, 98.7 us)
Async XLA Ops:
  7.2 94.7 %all-gather.2.cloned.1.call-start = ((), (), s32[]{:S(2)}) async-start(), calls=%async_computation | async-start | bytes 1216512 | tf_op jit(solution)/shard_map/all_gather | solution.py:881
  9.7 20.1 %collective-permute-start = (bf16[96,768]{1,0:T(8,128)(2,1)S(1)}, bf16[96,768]{1,0:T(8,128)(2,1)S(1)}, u32[]{:S(2)}, u32[]{:S(2)}) collective-permute-start(bf16[96,768]{1,0:T(8,128)(2,1)S(1)} %dynamic-slice_bitcast_fusion), channel_id=1, source_target_pairs={{0,3},{1,0},{2,1},{3,2},{4,7},{5,4},{6,5},{7,6},{8,11},{9,8},{10,9... | collective-permute-start | bytes 442376 | tf_op jit(solution)/shard_map/ppermute | solution.py:748
  94.8 28.5 %collective-permute-start.13 = (bf16[256,384]{1,0:T(8,128)(2,1)S(1)}, bf16[256,384]{1,0:T(8,128)(2,1)S(1)}, u32[]{:S(2)}, u32[]{:S(2)}) collective-permute-start(bf16[256,384]{1,0:T(8,128)(2,1)S(1)} %get-tuple-element.152), channel_id=1, source_target_pairs={{0,1},{1,2},{2,3},{3,0},{4,5},{5,6},{6,7},{7,4},{8,9},{9,10},{10,1... | collective-permute-start | bytes 589832 | tf_op jit(solution)/shard_map/ppermute | solution.py:748
  99.5 23.8 %collective-permute-start.14 = (bf16[256,384]{1,0:T(8,128)(2,1)S(1)}, bf16[256,384]{1,0:T(8,128)(2,1)S(1)}, u32[]{:S(2)}, u32[]{:S(2)}) collective-permute-start(bf16[256,384]{1,0:T(8,128)(2,1)S(1)} %get-tuple-element.153), channel_id=1, source_target_pairs={{0,2},{1,3},{2,0},{3,1},{4,6},{5,7},{6,4},{7,5},{8,10},{9,11},{10,... | collective-permute-start | bytes 589832 | tf_op jit(solution)/shard_map/ppermute | solution.py:748
  100.9 22.5 %collective-permute-start.15 = (bf16[256,384]{1,0:T(8,128)(2,1)S(1)}, bf16[256,384]{1,0:T(8,128)(2,1)S(1)}, u32[]{:S(2)}, u32[]{:S(2)}) collective-permute-start(bf16[256,384]{1,0:T(8,128)(2,1)S(1)} %get-tuple-element.154), channel_id=1, source_target_pairs={{0,3},{1,0},{2,1},{3,2},{4,7},{5,4},{6,5},{7,6},{8,11},{9,8},{10,9... | collective-permute-start | bytes 589832 | tf_op jit(solution)/shard_map/ppermute | solution.py:748
  123.3 24.1 %collective-permute-start.16 = (bf16[256,384]{1,0:T(8,128)(2,1)S(1)}, bf16[256,384]{1,0:T(8,128)(2,1)S(1)}, u32[]{:S(2)}, u32[]{:S(2)}) collective-permute-start(bf16[256,384]{1,0:T(8,128)(2,1)S(1)} %get-tuple-element.160), channel_id=1, source_target_pairs={{0,3},{1,0},{2,1},{3,2},{4,7},{5,4},{6,5},{7,6},{8,11},{9,8},{10,9... | collective-permute-start | bytes 589832 | tf_op jit(solution)/shard_map/ppermute | solution.py:748
  125.4 22.1 %collective-permute-start.17 = (bf16[256,384]{1,0:T(8,128)(2,1)S(1)}, bf16[256,384]{1,0:T(8,128)(2,1)S(1)}, u32[]{:S(2)}, u32[]{:S(2)}) collective-permute-start(bf16[256,384]{1,0:T(8,128)(2,1)S(1)} %get-tuple-element.161), channel_id=1, source_target_pairs={{0,2},{1,3},{2,0},{3,1},{4,6},{5,7},{6,4},{7,5},{8,10},{9,11},{10,... | collective-permute-start | bytes 589832 | tf_op jit(solution)/shard_map/ppermute | solution.py:748
  125.9 21.6 %collective-permute-start.18 = (bf16[256,384]{1,0:T(8,128)(2,1)S(1)}, bf16[256,384]{1,0:T(8,128)(2,1)S(1)}, u32[]{:S(2)}, u32[]{:S(2)}) collective-permute-start(bf16[256,384]{1,0:T(8,128)(2,1)S(1)} %get-tuple-element.162), channel_id=1, source_target_pairs={{0,1},{1,2},{2,3},{3,0},{4,5},{5,6},{6,7},{7,4},{8,9},{9,10},{10,1... | collective-permute-start | bytes 589832 | tf_op jit(solution)/shard_map/ppermute | solution.py:748
  167.6 21.9 %collective-permute-start.23 = (bf16[4,2,224,768]{3,2,1,0:T(8,128)(2,1)}, bf16[4,2,224,768]{3,2,1,0:T(8,128)(2,1)S(1)}, u32[]{:S(2)}, u32[]{:S(2)}) collective-permute-start(bf16[4,2,224,768]{3,2,1,0:T(8,128)(2,1)} %get-tuple-element.188), channel_id=1, source_target_pairs={{0,4},{4,0},{8,12},{12,8},{16,20},{20,16},{24,28},{28,24},{1,5},{5... | collective-permute-start | bytes 8257544 | tf_op jit(solution)/shard_map/ppermute | solution.py:752
  167.7 23.7 %collective-permute-start.24 = (bf16[4,2,224,768]{3,2,1,0:T(8,128)(2,1)}, bf16[4,2,224,768]{3,2,1,0:T(8,128)(2,1)S(1)}, u32[]{:S(2)}, u32[]{:S(2)}) collective-permute-start(bf16[4,2,224,768]{3,2,1,0:T(8,128)(2,1)} %get-tuple-element.190), channel_id=1, source_target_pairs={{0,4},{4,0},{8,12},{12,8},{16,20},{20,16},{24,28},{28,24},{1,5},{5... | collective-permute-start | bytes 8257544 | tf_op jit(solution)/shard_map/ppermute | solution.py:752
  174.8 20.3 %collective-permute-start.22 = (bf16[256,768]{1,0:T(8,128)(2,1)S(1)}, bf16[256,768]{1,0:T(8,128)(2,1)S(1)}, u32[]{:S(2)}, u32[]{:S(2)}) collective-permute-start(bf16[256,768]{1,0:T(8,128)(2,1)S(1)} %get-tuple-element.187), channel_id=1, source_target_pairs={{0,2},{1,3},{2,0},{3,1},{4,6},{5,7},{6,4},{7,5},{8,10},{9,11},{10,... | collective-permute-start | bytes 1179656 | tf_op jit(solution)/shard_map/ppermute | solution.py:748
  195.1 32.1 %collective-permute-start.25 = (bf16[2,2,224,768]{3,2,1,0:T(8,128)(2,1)S(1)}, bf16[2,2,224,768]{3,2,1,0:T(8,128)(2,1)S(1)}, u32[]{:S(2)}, u32[]{:S(2)}) collective-permute-start(bf16[2,2,224,768]{3,2,1,0:T(8,128)(2,1)S(1)} %add_convert_fusion.1), channel_id=1, source_target_pairs={{0,8},{4,12},{8,0},{12,4},{16,24},{20,28},{24,16},{28,20},{1,9},{5... | collective-permute-start | bytes 4128776 | tf_op jit(solution)/shard_map/ppermute | solution.py:752
  196.6 32.0 %collective-permute-start.26 = (bf16[2,2,224,768]{3,2,1,0:T(8,128)(2,1)S(1)}, bf16[2,2,224,768]{3,2,1,0:T(8,128)(2,1)S(1)}, u32[]{:S(2)}, u32[]{:S(2)}) collective-permute-start(bf16[2,2,224,768]{3,2,1,0:T(8,128)(2,1)S(1)} %add_convert_fusion), channel_id=1, source_target_pairs={{0,16},{4,20},{8,24},{12,28},{16,0},{20,4},{24,8},{28,12},{1,17},{... | collective-permute-start | bytes 4128776 | tf_op jit(solution)/shard_map/ppermute | solution.py:752
  198.1 32.0 %collective-permute-start.27 = (bf16[256,768]{1,0:T(8,128)(2,1)S(1)}, bf16[256,768]{1,0:T(8,128)(2,1)S(1)}, u32[]{:S(2)}, u32[]{:S(2)}) collective-permute-start(bf16[256,768]{1,0:T(8,128)(2,1)S(1)} %get-tuple-element.198), channel_id=1, source_target_pairs={{0,3},{1,0},{2,1},{3,2},{4,7},{5,4},{6,5},{7,6},{8,11},{9,8},{10,9... | collective-permute-start | bytes 1179656 | tf_op jit(solution)/shard_map/ppermute | solution.py:748
  199.6 30.5 %collective-permute-start.28 = (bf16[256,768]{1,0:T(8,128)(2,1)S(1)}, bf16[256,768]{1,0:T(8,128)(2,1)S(1)}, u32[]{:S(2)}, u32[]{:S(2)}) collective-permute-start(bf16[256,768]{1,0:T(8,128)(2,1)S(1)} %get-tuple-element.199), channel_id=1, source_target_pairs={{0,1},{1,2},{2,3},{3,0},{4,5},{5,6},{6,7},{7,4},{8,9},{9,10},{10,1... | collective-permute-start | bytes 1179656 | tf_op jit(solution)/shard_map/ppermute | solution.py:748
  231.7 19.2 %collective-permute-start.29 = (bf16[4,3,64,1024]{3,2,1,0:T(8,128)(2,1)}, bf16[4,3,64,1024]{3,2,1,0:T(8,128)(2,1)}, u32[]{:S(2)}, u32[]{:S(2)}) collective-permute-start(bf16[4,3,64,1024]{3,2,1,0:T(8,128)(2,1)} %get-tuple-element.201), channel_id=1, source_target_pairs={{0,4},{4,0},{8,12},{12,8},{16,20},{20,16},{24,28},{28,24},{1,5},{5... | collective-permute-start | bytes 4718600 | tf_op jit(solution)/shard_map/ppermute | solution.py:752
  231.8 19.1 %collective-permute-start.30 = (bf16[4,3,64,1024]{3,2,1,0:T(8,128)(2,1)}, bf16[4,3,64,1024]{3,2,1,0:T(8,128)(2,1)}, u32[]{:S(2)}, u32[]{:S(2)}) collective-permute-start(bf16[4,3,64,1024]{3,2,1,0:T(8,128)(2,1)} %get-tuple-element.203), channel_id=1, source_target_pairs={{0,4},{4,0},{8,12},{12,8},{16,20},{20,16},{24,28},{28,24},{1,5},{5... | collective-permute-start | bytes 4718600 | tf_op jit(solution)/shard_map/ppermute | solution.py:752
  232.7 17.7 %collective-permute-start.42 = (bf16[1,2,224,768]{3,2,1,0:T(8,128)(2,1)}, bf16[1,2,224,768]{3,2,1,0:T(8,128)(2,1)S(1)}, u32[]{:S(2)}, u32[]{:S(2)}) collective-permute-start(bf16[1,2,224,768]{3,2,1,0:T(8,128)(2,1)} %slice.373), channel_id=1, source_target_pairs={{0,16},{4,20},{8,24},{12,28},{16,0},{20,4},{24,8},{28,12},{1,17},{... | collective-permute-start | bytes 2064392 | tf_op jit(solution)/shard_map/ppermute | solution.py:752
  248.3 18.8 %collective-permute-start.46 = (bf16[224,768]{1,0:T(8,128)(2,1)S(1)}, bf16[224,768]{1,0:T(8,128)(2,1)S(1)}, u32[]{:S(2)}, u32[]{:S(2)}) collective-permute-start(bf16[224,768]{1,0:T(8,128)(2,1)S(1)} %get-tuple-element.250), channel_id=1, source_target_pairs={{0,3},{1,0},{2,1},{3,2},{4,7},{5,4},{6,5},{7,6},{8,11},{9,8},{10,9... | collective-permute-start | bytes 1032200 | tf_op jit(solution)/shard_map/ppermute | solution.py:748
  248.4 28.1 %collective-permute-start.45 = (bf16[224,768]{1,0:T(8,128)(2,1)S(1)}, bf16[224,768]{1,0:T(8,128)(2,1)S(1)}, u32[]{:S(2)}, u32[]{:S(2)}) collective-permute-start(bf16[224,768]{1,0:T(8,128)(2,1)S(1)} %get-tuple-element.249), channel_id=1, source_target_pairs={{0,2},{1,3},{2,0},{3,1},{4,6},{5,7},{6,4},{7,5},{8,10},{9,11},{10,... | collective-permute-start | bytes 1032200 | tf_op jit(solution)/shard_map/ppermute | solution.py:748
  250.6 25.9 %collective-permute-start.43 = (bf16[224,768]{1,0:T(8,128)(2,1)S(1)}, bf16[224,768]{1,0:T(8,128)(2,1)S(1)}, u32[]{:S(2)}, u32[]{:S(2)}) collective-permute-start(bf16[224,768]{1,0:T(8,128)(2,1)S(1)} %fusion.6), channel_id=1, source_target_pairs={{0,1},{1,2},{2,3},{3,0},{4,5},{5,6},{6,7},{7,4},{8,9},{9,10},{10,1... | collective-permute-start | bytes 1032200 | tf_op jit(solution)/shard_map/ppermute | solution.py:748
  260.7 17.8 %collective-permute-start.35 = (bf16[4,4,32,768]{3,2,1,0:T(8,128)(2,1)S(1)}, bf16[4,4,32,768]{3,2,1,0:T(8,128)(2,1)S(1)}, u32[]{:S(2)}, u32[]{:S(2)}) collective-permute-start(bf16[4,4,32,768]{3,2,1,0:T(8,128)(2,1)S(1)} %get-tuple-element.216), channel_id=1, source_target_pairs={{0,4},{4,0},{8,12},{12,8},{16,20},{20,16},{24,28},{28,24},{1,5},{5... | collective-permute-start | bytes 2359304 | tf_op jit(solution)/shard_map/ppermute | solution.py:752
  265.6 20.1 %collective-permute-start.32 = (bf16[2,3,64,1024]{3,2,1,0:T(8,128)(2,1)}, bf16[2,3,64,1024]{3,2,1,0:T(8,128)(2,1)}, u32[]{:S(2)}, u32[]{:S(2)}) collective-permute-start(bf16[2,3,64,1024]{3,2,1,0:T(8,128)(2,1)} %add_convert_fusion.2), channel_id=1, source_target_pairs={{0,16},{4,20},{8,24},{12,28},{16,0},{20,4},{24,8},{28,12},{1,17},{... | collective-permute-start | bytes 2359304 | tf_op jit(solution)/shard_map/ppermute | solution.py:752
  267.2 19.8 %collective-permute-start.31 = (bf16[2,3,64,1024]{3,2,1,0:T(8,128)(2,1)}, bf16[2,3,64,1024]{3,2,1,0:T(8,128)(2,1)}, u32[]{:S(2)}, u32[]{:S(2)}) collective-permute-start(bf16[2,3,64,1024]{3,2,1,0:T(8,128)(2,1)} %add_convert_fusion.3), channel_id=1, source_target_pairs={{0,8},{4,12},{8,0},{12,4},{16,24},{20,28},{24,16},{28,20},{1,9},{5... | collective-permute-start | bytes 2359304 | tf_op jit(solution)/shard_map/ppermute | solution.py:752
  (77 other events, 946.3 us)
Sparse Core Ops, SparseCore 0:
  11.5 66.4 all-gather.1

commit v3 on v2

--- a/solution.py
+++ b/solution.py
@@ -233,23 +233,22 @@
     )(place, lengths, *(piece for group in groups for piece in group), kept(matrix), corner)
 
 
-def feed_kernel(zones, heads, size, steps, place_ref, *refs):
+def feed_kernel(zones, heads, size, steps, earlier, place_ref, *refs):
     pieces = refs[:zones]
     (x_ref, cot_ref, project_ref, gain_ref, up_ref, up_bias_ref, down_ref, down_bias_ref) = refs[
         zones : zones + 8
     ]
-    outs = refs[zones + 8 :]
+    outs = refs[zones + 8 + earlier :]
     grads = outs[:zones]
     (
         block_ref,
-        resid_grad_ref,
         act_t_ref,
         pre_t_ref,
-        norm_ref,
-        mixed_ref,
+        norm_out_ref,
         attended_ref,
         up_sum_ref,
         sums_ref,
+        norm_ref,
         weight_ref,
         resid_ref,
         hat_ref,
@@ -272,7 +271,6 @@
             mixed = jnp.concatenate(
                 [separate(piece[...], seq, count, heads, size) for piece in pieces], axis=1
             )
-            mixed_ref[at, :] = mixed
             resid = x_ref[seq].astype(F32) + dot_nn(mixed, weight_ref[...])
             hat, inverse = norm_of(resid)
             resid_ref[at, :] = resid + down_bias_ref[...]
@@ -305,6 +303,8 @@
         back_ref[at, :] += back
 
     up_sum_ref[...] = up_sum
+    share = norm_out_ref.shape[1]
+    norm_out_ref[...] = norm_ref[:, pl.ds(pl.multiple_of(step * share, share), share)]
 
     @pl.when(step == steps - 1)
     def _():
@@ -320,7 +320,6 @@
             gain_sum = gain_sum + jnp.sum(back * hat, 0, keepdims=True)
             bias_sum = bias_sum + jnp.sum(cot, 0, keepdims=True)
             grad = cot + norm_back(back * gain_ref[...], hat, inv_ref[at, :])
-            resid_grad_ref[at, :] = grad
             low = grad.astype(BF16)
             attended_ref[:, at] = low.T
             made.append(dot_nt(low, weight_ref[...]))
@@ -331,7 +330,7 @@
             grads[d][...] = interleave(mine, heads, size).astype(BF16)
 
 
-def feed(place, pieces, x, cot, project, gain, up, up_bias, down, down_bias, heads):
+def feed(place, pieces, x, cot, project, gain, up, up_bias, down, down_bias, heads, c, blocks):
     zones = len(pieces)
     count, rows, depth = x.shape
     size = depth // zones // heads
@@ -340,19 +339,18 @@
     steps = hidden // tile
     tokens = count * rows
     wide = pieces[0].shape[1]
+    earlier = [] if blocks is None else [blocks]
     shapes = [jax.ShapeDtypeStruct((rows, wide), BF16)] * zones + [
-        far((count, rows, depth), BF16),
-        far((tokens, depth), F32),
+        far((2 * count, rows, depth), BF16),
         far((hidden, tokens), BF16),
         far((hidden, tokens), BF16),
-        far((tokens, depth), BF16),
         far((tokens, depth), BF16),
         far((depth, tokens), BF16),
         jax.ShapeDtypeStruct((1, hidden), F32),
         jax.ShapeDtypeStruct((2, depth), F32),
     ]
     return pl.pallas_call(
-        functools.partial(feed_kernel, zones, heads, size, steps),
+        functools.partial(feed_kernel, zones, heads, size, steps, len(earlier)),
         grid_spec=pltpu.PrefetchScalarGridSpec(
             num_scalar_prefetch=1,
             grid=(steps,),
@@ -366,20 +364,24 @@
                 pl.BlockSpec((1, tile), lambda f, *_: (0, f)),
                 pl.BlockSpec((tile, depth), lambda f, *_: (f, 0)),
                 whole(down_bias.shape),
-            ],
+            ]
+            + [pl.BlockSpec(memory_space=pltpu.HBM)] * len(earlier),
             out_specs=[whole((rows, wide))] * zones
             + [
-                whole((count, rows, depth)),
-                whole((tokens, depth)),
+                pl.BlockSpec(
+                    (count, rows, depth),
+                    lambda *_: (c, 0, 0),
+                    pipeline_mode=pl.Buffered(buffer_count=1),
+                ),
                 pl.BlockSpec((tile, tokens), lambda f, *_: (f, 0)),
                 pl.BlockSpec((tile, tokens), lambda f, *_: (f, 0)),
-                whole((tokens, depth)),
-                whole((tokens, depth)),
+                pl.BlockSpec((tokens, depth // steps), lambda f, *_: (0, f)),
                 whole((depth, tokens)),
                 pl.BlockSpec((1, tile), lambda f, *_: (0, f)),
                 whole((2, depth)),
             ],
             scratch_shapes=[
+                pltpu.VMEM((tokens, depth), BF16),
                 pltpu.VMEM((depth, depth), BF16),
                 pltpu.VMEM((tokens, depth), F32),
                 pltpu.VMEM((tokens, depth), F32),
@@ -395,6 +397,7 @@
             4 * depth * hidden + 4 * tokens * hidden + 20 * tokens * depth,
             tokens * hidden,
         ),
+        input_output_aliases={zones + 9: zones} if earlier else {},
         name="feed",
     )(
         place,
@@ -407,6 +410,7 @@
         up_bias,
         kept(down),
         down_bias,
+        *earlier,
     )
 
 
@@ -431,12 +435,6 @@
     return jnp.concatenate(parts, axis=1)
 
 
-def unpack(packed, rows, zones):
-    group, depth = packed.shape
-    spread = packed.reshape(group, zones, depth // zones).swapaxes(0, 1)
-    return spread.reshape(group * zones, depth // zones)[:rows]
-
-
 def place_first(second):
     return second // 2 + 2 * (1 - lax.rem(second, 2))
 
@@ -445,12 +443,26 @@
     return lax.rem(second + 2, 4)
 
 
-def weights_kernel(zones, chunks, place_ref, *refs):
+def weights_kernel(zones, chunks, heads, place_ref, *refs):
     acts, pres = refs[:chunks], refs[chunks : 2 * chunks]
     attends = refs[2 * chunks : 3 * chunks]
     norms, cots = refs[3 * chunks : 4 * chunks], refs[4 * chunks : 5 * chunks]
-    mixes = refs[5 * chunks : 6 * chunks]
-    first_ref, second_ref, scratch_ref = refs[6 * chunks :]
+    pieces = refs[5 * chunks : (5 + zones) * chunks]
+    first_ref, second_ref, scratch_ref, mixed_ref = refs[(5 + zones) * chunks :]
+    mixes = [mixed_ref.at[c] for c in range(chunks)]
+    rows, wide = pieces[0].shape
+    count = norms[0].shape[0] // rows
+
+    @pl.when(pl.program_id(0) == 0)
+    def _():
+        for c in range(chunks):
+            group = pieces[c * zones : (c + 1) * zones]
+            for seq in range(count):
+                parts = [
+                    separate(piece[...], seq, count, heads, wide // heads // count)
+                    for piece in group
+                ]
+                mixed_ref[c, seq * rows : (seq + 1) * rows, :] = jnp.concatenate(parts, axis=1)
     part = scratch_ref.shape[1] // zones
 
     def total(lefts, rights):
@@ -471,7 +483,7 @@
         side[0, number] = jnp.concatenate(parts, axis=0).astype(BF16)
 
 
-def weight_grads(place, acts, pres, attends, norms, cots, mixes, odd, zones, ranks):
+def weight_grads(place, acts, pres, attends, norms, cots, pieces, heads, odd, zones, ranks):
     chunks = len(acts)
     hidden, tokens = acts[0].shape
     depth = norms[0].shape[1]
@@ -491,15 +503,19 @@
 
     shape = (ranks // 2, zones // 2, rows, depth)
     return pl.pallas_call(
-        functools.partial(weights_kernel, zones, chunks),
+        functools.partial(weights_kernel, zones, chunks, heads),
         grid_spec=pltpu.PrefetchScalarGridSpec(
             num_scalar_prefetch=1,
             grid=(ranks // 2,),
             in_specs=[pl.BlockSpec((tile, tokens), tall)] * (2 * chunks)
             + [pl.BlockSpec((square, tokens), tall)] * chunks
-            + [whole((tokens, depth))] * (3 * chunks),
+            + [whole((tokens, depth))] * (2 * chunks)
+            + [whole(pieces[0][0].shape)] * (zones * chunks),
             out_specs=[pl.BlockSpec((1, *shape[1:]), first), pl.BlockSpec((1, *shape[1:]), second)],
-            scratch_shapes=[pltpu.VMEM((2, tile, depth), F32)],
+            scratch_shapes=[
+                pltpu.VMEM((2, tile, depth), F32),
+                pltpu.VMEM((chunks, tokens, depth), BF16),
+            ],
         ),
         out_shape=[far(shape, BF16)] * 2,
         compiler_params=params(24),
@@ -515,7 +531,7 @@
         *map(kept, attends),
         *map(kept, norms),
         *map(kept, cots),
-        *map(kept, mixes),
+        *(kept(piece) for group in pieces for piece in group),
     )
 
 
@@ -660,8 +676,9 @@
 
 def input_kernel(zones, heads, size, ranks, count, place_ref, *refs):
     pieces = refs[:zones]
-    x_ref, gain_ref, weight_ref, resid_ref, extra_in_ref = refs[zones : zones + 5]
-    grad_ref, send_ref, keep_ref, total_ref, gain_sum_ref, extra_ref = refs[zones + 5 :]
+    x_ref, gain_ref, weight_ref, extra_in_ref = refs[zones : zones + 4]
+    resids = refs[zones + 4 : zones + 6]
+    grad_ref, send_ref, keep_ref, total_ref, gain_sum_ref, extra_ref = refs[zones + 6 :]
     depth = x_ref.shape[2]
     seq = pl.program_id(0)
 
@@ -684,7 +701,8 @@
     back = jnp.concatenate(parts, axis=1).astype(BF16)
     grad_norm = dot_nn(back, weight_ref[...])
     gain_sum_ref[...] += jnp.sum(grad_norm * hat, 0, keepdims=True)
-    grad = resid_ref[...] + norm_back(grad_norm * gain_ref[...], hat, inverse)
+    resid = jnp.where(seq < count // 2, resids[0][...], resids[1][...]).astype(F32).T
+    grad = resid + norm_back(grad_norm * gain_ref[...], hat, inverse)
     grad_ref[0] = grad.astype(BF16)
     total_ref[...] += dot_tn(norm, back)
 
@@ -699,7 +717,7 @@
         store_square(place_ref, (send_ref, keep_ref), total_ref, extra_ref, zones, ranks)
 
 
-def input_grads(place, pieces, x, gain, weight, resid, extra, heads, ranks):
+def input_grads(place, pieces, x, gain, weight, resids, extra, heads, ranks):
     zones = len(pieces)
     count, rows, depth = x.shape
     size = depth // zones // heads
@@ -716,8 +734,9 @@
                 pl.BlockSpec((1, rows, depth), lambda s, *_: (s, 0, 0)),
                 whole(gain.shape),
                 whole(weight.shape),
-                pl.BlockSpec((rows, depth), lambda s, *_: (s, 0)),
                 whole(extra.shape),
+                pl.BlockSpec((depth, rows), lambda s, *_: (0, jnp.minimum(s, count // 2 - 1))),
+                pl.BlockSpec((depth, rows), lambda s, *_: (0, jnp.maximum(s - count // 2, 0))),
             ],
             out_specs=[
                 pl.BlockSpec((1, rows, depth), lambda s, *_: (s, 0, 0)),
@@ -740,7 +759,67 @@
             4 * count * rows * depth * depth, 12 * count * rows * depth + 8 * depth * depth
         ),
         name="input",
-    )(place, *map(kept, pieces), kept(x), gain, kept(weight), kept(resid), extra)
+    )(place, *map(kept, pieces), kept(x), gain, kept(weight), extra, *map(kept, resids))
+
+
+def total_of(terms):
+    total = terms[0][...]
+    for term in terms[1:]:
+        total = total + term[...].astype(F32)
+    return total
+
+
+def unpack(packed, rows, zones):
+    width = packed.shape[1] // zones
+    parts = [packed[:, k * width : (k + 1) * width] for k in range(zones)]
+    return jnp.concatenate(parts, axis=0)[:rows]
+
+
+def feed_sums_kernel(zones, tile, square, *refs):
+    up_ref, down_ref, square_ref = refs[zones:]
+    total = total_of(refs[:zones])
+    up_ref[...] = total[:tile].T
+    down_ref[...] = total[tile : 2 * tile]
+    packed = total[2 * tile : 2 * tile + group_rows(square, zones)]
+    square_ref[...] = unpack(packed, square, zones).T
+
+
+def feed_sums(terms, tile, square, zones):
+    depth = terms[0].shape[1]
+    return pl.pallas_call(
+        functools.partial(feed_sums_kernel, zones, tile, square),
+        grid=(1,),
+        in_specs=[whole(term.shape) for term in terms],
+        out_specs=[whole((depth, tile)), whole((tile, depth)), whole((depth // zones, square))],
+        out_shape=[
+            far((depth, tile), F32),
+            far((tile, depth), F32),
+            far((depth // zones, square), F32),
+        ],
+        compiler_params=params(12),
+        name="feed_sums",
+    )(*map(kept, terms))
+
+
+def value_sums_kernel(zones, square, *refs):
+    square_ref, line_ref = refs[zones:]
+    total = total_of(refs[:zones])
+    group = group_rows(square, zones)
+    square_ref[...] = unpack(total[:group], square, zones)
+    line_ref[...] = total[group : group + 1]
+
+
+def value_sums(terms, square, zones):
+    depth = terms[0].shape[1]
+    return pl.pallas_call(
+        functools.partial(value_sums_kernel, zones, square),
+        grid=(1,),
+        in_specs=[whole(term.shape) for term in terms],
+        out_specs=[whole((square, depth // zones)), whole((1, depth))],
+        out_shape=[far((square, depth // zones), F32), jax.ShapeDtypeStruct((1, depth), F32)],
+        compiler_params=params(12),
+        name="value_sums",
+    )(*terms)
 
 
 def shift(value, axis, extent, by):
@@ -793,28 +872,34 @@
         ]
         if results:
             sent = lax.optimization_barrier((*sent, *results))[:2]
-        self.keeps = keeps
+        self.keeps, self.sent = keeps, sent
         self.went = [
             flip(value, "dp", self.ranks, masks[0]) for value, masks in zip(sent, self.masks)
         ]
 
-    def second(self, *results):
-        half, rest = self.ranks // 4, self.ranks // 8
-        rests = [
-            widen(keep[half:]) + widen(came[half:]) + widen(went)
+    def rest(self, start, stop):
+        half = self.ranks // 4
+        return [
+            widen(keep[half + start : half + stop])
+            + widen(came[half + start : half + stop])
+            + widen(went[start:stop])
             for keep, came, went in zip(self.keeps, self.came, self.went)
         ]
-        self.own = [value[:rest] for value in rests]
-        sent = [value[rest:].astype(BF16) for value in rests]
+
+    def second(self, *results):
+        sent = [value.astype(BF16) for value in self.rest(self.ranks // 8, self.ranks // 4)]
         if results:
             sent = lax.optimization_barrier((*sent, *results))[:2]
         self.last = [
             flip(value, "dp", self.ranks, masks[1]) for value, masks in zip(sent, self.masks)
         ]
 
-    def finish(self):
+    def finish(self, *results):
+        lasts = self.last
+        if results:
+            lasts = lax.optimization_barrier((*lasts, *results))[:2]
         sides = []
-        for own, last in zip(self.own, self.last):
+        for own, last in zip(self.rest(0, self.ranks // 8), lasts):
             total = own + widen(last)
             side = total[0]
             for third in range(1, self.ranks // 8):
@@ -825,29 +910,24 @@
 
 def reduce_direct(send, keep, ranks, *results):
     rest = ranks // 8
-    came = flip(send, "dp", ranks, 1)
+    came = flip(after(send, *results), "dp", ranks, 1)
     both = [
         widen(keep[q * rest : (q + 1) * rest]) + widen(came[q * rest : (q + 1) * rest])
         for q in range(4)
     ]
-    sent = lax.optimization_barrier((*(part.astype(BF16) for part in both[1:]), *results))
     total = both[0]
     for q in range(1, 4):
-        total = total + widen(flip(sent[q - 1], "dp", ranks, 2 * q))
+        total = total + widen(flip(both[q].astype(BF16), "dp", ranks, 2 * q))
     own = total[0]
     for third in range(1, rest):
         own = own + widen(flip(total[third].astype(BF16), "dp", ranks, 8 * third))
     return own
 
 
-def reduce_head(blocks, zones, *results):
-    sent = [block.astype(BF16) for block in blocks[1:]]
-    if results:
-        sent = lax.optimization_barrier((*sent, *results))[: zones - 1]
-    total = blocks[0]
-    for d in range(1, zones):
-        total = total + widen(shift(sent[d - 1], "head", zones, d))
-    return total
+def spread_head(blocks, zones):
+    return [blocks[0]] + [
+        shift(blocks[d].astype(BF16), "head", zones, d) for d in range(1, zones)
+    ]
 
 
 def local(
@@ -895,7 +975,7 @@
     def call_values(place, c, weights):
         return make_values(place, part(block_input, c), gain1, weights, zones, heads, c == 0)
 
-    def call_feed(place, c, pieces):
+    def call_feed(place, c, pieces, blocks):
         return feed(
             place,
             pieces,
@@ -908,6 +988,8 @@
             down_projection_weight,
             down_bias[None],
             heads,
+            c,
+            blocks,
         )
 
     made = call_values(place, 0, [own, *mine, others])
@@ -925,21 +1007,29 @@
     place = after(place, made[0])
     mixed1 = exchange(made, zones, 1, *mixed0)
 
-    feed0 = call_feed(place, 0, mixed0)
+    feed0 = call_feed(place, 0, mixed0, None)
     place = after(place, feed0[0])
     grads0 = exchange(feed0[:zones], zones, -1, *mixed1)
-    feed1 = call_feed(place, 1, mixed1)
+    feed1 = call_feed(place, 1, mixed1, feed0[zones])
     place = after(place, feed1[0], *grads0)
-    blocks, resids, acts, pres, norms, mixes, attends, up_sums, sums = zip(
-        feed0[zones:], feed1[zones:]
-    )
+    acts, pres, norms, attends, up_sums, sums = zip(feed0[zones + 1 :], feed1[zones + 1 :])
     cots = [part(cotangent, c).reshape(count * rows, depth) for c in range(2)]
 
     weight_sum, rand_sum = Reduce(ranks), Reduce(ranks)
 
     def call_weights(place, odd):
         return weight_grads(
-            place, acts, pres, attends, norms, cots, mixes, odd, zones, ranks
+            place,
+            acts,
+            pres,
+            attends,
+            norms,
+            cots,
+            (mixed0, mixed1),
+            heads,
+            odd,
+            zones,
+            ranks,
         )
 
     grads1 = exchange(feed1[:zones], zones, -1, *grads0)
@@ -973,32 +1063,37 @@
     extra = jnp.pad(extra, ((0, 0), (0, depth - extra.shape[1])))
 
     rand_sum.first(rand[2:], *backs)
-    resid = jnp.concatenate(resids, 0)
     grad_x, value_send, value_keep = input_grads(
-        place, backs, block_input, gain1, weight, resid, extra, heads, ranks
-    )
-    sides = weight_sum.finish()
-    blocks_ff = [side[d] for side in sides for d in range(zones // 2)]
-    ff = reduce_head(blocks_ff, zones)
-    rand_sum.second(value_send)
+        place, backs, block_input, gain1, weight, attends, extra, heads, ranks
+    )
+    sides = weight_sum.finish(*rand_sum.sent)
+    terms = [side[d] for side in sides for d in range(zones // 2)]
+    far_apart = zones // 2
+    for d in (far_apart, *(d for d in range(1, zones) if d != far_apart)):
+        sent = terms[d].astype(BF16)
+        if d != far_apart:
+            sent = after(sent, terms[far_apart])
+        terms[d] = shift(sent, "head", zones, d)
+    rand_sum.second(value_send, terms[far_apart])
     value_own = reduce_direct(value_send, value_keep, ranks, *rand_sum.went)
-    value_total = reduce_head([value_own[d] for d in range(zones)], zones)
+    tile, square = hidden // ranks // zones, depth // ranks
+    terms = lax.optimization_barrier((*terms, *rand_sum.last))[:zones]
+    grad_up, grad_down, grad_out = feed_sums(terms, tile, square, zones)
+    value_terms = spread_head([value_own[d] for d in range(zones)], zones)
+    grad_value, line = value_sums(value_terms, square, zones)
+    line = line[0]
     grad_rand = jnp.concatenate(rand_sum.finish(), 1)
-
-    tile, square = hidden // ranks // zones, depth // ranks
-    group = group_rows(square, zones)
-    line = value_total[group]
     return (
-        jnp.concatenate(blocks, 0),
+        feed1[zones],
         grad_x,
         grad_rand,
-        unpack(value_total[:group], square, zones),
-        unpack(ff[2 * tile : 2 * tile + group], square, zones).T,
+        grad_value,
+        grad_out,
         line[:gain_size],
         line[gain_size : 2 * gain_size],
-        ff[:tile].T,
+        grad_up,
         line[3 * gain_size : 3 * gain_size + up_size],
-        ff[tile : 2 * tile],
+        grad_down,
         line[2 * gain_size : 3 * gain_size],
     )
 

time: 328 us -> 317 us (0.966)
  waiting for transfers between devices: 78 us -> 64.5 us
  Pallas kernels: 132 us -> 136 us
    ppermute x17, waiting for transfers between devices: 41.6 us -> 34.7 us  [flip(): return lax.ppermute(value, axis, [(i, i ^ mask) for i in range(extent)])]
    convert_element_type x1 -> x5, other arithmetic: 0.15 us -> 6.74 us  [the longest x4 5.82 us: second(): value.astype(BF16)]
    ppermute x30, waiting for transfers between devices: 36.3 us -> 29.8 us  [shift(): lax.ppermute(value, axis, [(i, (i + by) % extent) for i in range(extent)])]
    concatenate x2 -> x0, other arithmetic: 5.16 us -> none  [the longest x1 3.88 us: local(): resid = jnp.concatenate(resids, 0)]
    ppermute x30, starting transfers between devices: 48.4 us -> 53.2 us  [shift(): lax.ppermute(value, axis, [(i, (i + by) % extent) for i in range(extent)])]
    add x6 -> x0, other arithmetic: 4.64 us -> none  [the longest x4 4.43 us: second(): widen(keep[half:]) + widen(came[half:]) + widen(went)]
    pallas_call x4 -> x6, Pallas kernels: 69.3 us -> 72.3 us  [the longest x2 40.8 us: feed(): pl.pallas_call(functools.partial(feed_kernel, zones, heads, size, steps,...]
    unnamed x107 -> x105, local copies, waits for them, and re-layouts: 5.4 us -> 7.02 us
  transfers between devices with their start and end apart: 48 -> 48, of which waited for: 17 -> 16; matrix products, arithmetic and copies ran while one was open for 9% -> 8% of each run, Pallas kernels for 40% -> 43%
where the time goes in v3:
time: 317 us; the launch traced here: 316 us
  Pallas kernels  136 us (43%)
  starting transfers between devices  67.1 us (21%)
  waiting for transfers between devices  64.5 us (20%)
  other arithmetic  21.2 us (7%)
  between operations  15 us (5%)
  local copies, waits for them, and re-layouts  12.4 us (4%)
    ppermute x30, starting transfers between devices, shift(): lax.ppermute(value, axis, [(i, (i + by) % extent) for i in range(extent)])  53.2 us
    pallas_call x2, Pallas kernels, feed(): pl.pallas_call(functools.partial(feed_kernel, zones, heads, size, steps,...  40.8 us
    ppermute x17, waiting for transfers between devices, flip(): return lax.ppermute(value, axis, [(i, i ^ mask) for i in range(extent)])  34.7 us
    ppermute x30, waiting for transfers between devices, shift(): lax.ppermute(value, axis, [(i, (i + by) % extent) for i in range(extent)])  29.8 us
    pallas_call x2, Pallas kernels, weight_grads(): pl.pallas_call(functools.partial(weights_kernel, zones, chunks, heads), g...  28.3 us
    pallas_call x1, Pallas kernels, logit_grads(): pl.pallas_call(functools.partial(logits_kernel, zones, chunks, count, hea...  18.1 us
    pallas_call x3, Pallas kernels, mix(): pl.pallas_call(functools.partial(mix_kernel, zones, chunks, count, lanes...  16.8 us
    pallas_call x1, Pallas kernels, make_probs(): pl.pallas_call(probs_kernel, grid=(heads, rows // SHORT), in_specs=[pl.Bl...  14 us
  transfers between devices with their start and end apart: 48, of which 16 were waited for; matrix products, arithmetic and copies ran while one was open for 8% of the time, Pallas kernels for 43%

profile of v3, /device:TPU:0, one launch (start us, length us, event | category | flops | bytes accessed | tf_op | source)
XLA Modules:
  0.0 316.2 jit_solution(8571902489178285266)
XLA Ops:
  9.7 5.1 %collective-permute-start = (bf16[96,768]{1,0:T(8,128)(2,1)S(1)}, bf16[96,768]{1,0:T(8,128)(2,1)S(1)}, u32[]{:S(2)}, u32[]{:S(2)}) collective-permute-start(bf16[96,768]{1,0:T(8,128)(2,1)S(1)} %dynamic-slice_bitcast_fusion), channel_id=1, source_target_pairs={{0,3},{1,0},{2,1},{3,2},{4,7},{5,4},{6,5},{7,6},{8,11},{9,8},{10,9... | collective-permute-start | bytes 442376 | tf_op jit(solution)/shard_map/ppermute | solution.py:827
  15.9 14.0 %probs.1 = (bf16[3,1024,1024]{2,1,0:T(8,128)(2,1)}, bf16[3,1024,1024]{2,1,0:T(8,128)(2,1)}, bf16[3,256,256]{2,1,0:T(8,128)(2,1)S(1)}, bf16[3,256,256]{2,1,0:T(8,128)(2,1)S(1)}) custom-call(bf16[3,1024,1024]{2,1,0:T(8,128)(2,1)} %refs_16_.1), custom_call_target="tpu_custom_call" | custom-call | flops 31457280 | bytes 18874368 | tf_op jit(solution)/shard_map/probs/pallas_call | solution.py:109
  41.5 3.5 %collective-permute-done.4.refs_1_.refs_9_ = bf16[256,384]{1,0:T(8,128)(2,1)S(1)} collective-permute-done((bf16[256,384]{1,0:T(8,128)(2,1)S(1)}, bf16[256,384]{1,0:T(8,128)(2,1)S(1)}, u32[]{:S(2)}, u32[]{:S(2)}) %collective-permute-start.4) | collective-permute-done | bytes 196640 | tf_op jit(solution)/shard_map/ppermute | solution.py:827
  45.0 8.5 %collective-permute-done.5.refs_2_.refs_10_ = bf16[256,384]{1,0:T(8,128)(2,1)S(1)} collective-permute-done((bf16[256,384]{1,0:T(8,128)(2,1)S(1)}, bf16[256,384]{1,0:T(8,128)(2,1)S(1)}, u32[]{:S(2)}, u32[]{:S(2)}) %collective-permute-start.5) | collective-permute-done | bytes 196640 | tf_op jit(solution)/shard_map/ppermute | solution.py:827
  53.5 4.9 %collective-permute-start.7 = (bf16[256,384]{1,0:T(8,128)(2,1)S(1)}, bf16[256,384]{1,0:T(8,128)(2,1)S(1)}, u32[]{:S(2)}, u32[]{:S(2)}) collective-permute-start(bf16[256,384]{1,0:T(8,128)(2,1)S(1)} %get-tuple-element.142), channel_id=1, source_target_pairs={{0,1},{1,2},{2,3},{3,0},{4,5},{5,6},{6,7},{7,4},{8,9},{9,10},{10,1... | collective-permute-start | bytes 589832 | tf_op jit(solution)/shard_map/ppermute | solution.py:827
  60.9 5.6 %mix.3 = (bf16[256,384]{1,0:T(8,128)(2,1)S(1)}, bf16[256,384]{1,0:T(8,128)(2,1)S(1)}, bf16[256,384]{1,0:T(8,128)(2,1)S(1)}, bf16[256,384]{1,0:T(8,128)(2,1)S(1)}) custom-call(s32[2]{0:T(128)S(1)} %pad_add_fusion.place_ref, s32[2]{0:T(128)S(1)} %get-tuple-element.281.long_flags, bf16[256,384]{1,0:T(8,128)(2,1)S(1)} %get-tuple-element.132.refs_0_.refs_8_, ...), custom_call_target="tpu_custom_call" | custom-call | flops 805306368 | bytes 7864320 | tf_op jit(solution)/shard_map/mix/pallas_call | solution.py:213
  66.5 8.3 %collective-permute-done.8.refs_2_.refs_14_ = bf16[256,384]{1,0:T(8,128)(2,1)S(1)} collective-permute-done((bf16[256,384]{1,0:T(8,128)(2,1)S(1)}, bf16[256,384]{1,0:T(8,128)(2,1)S(1)}, u32[]{:S(2)}, u32[]{:S(2)}) %collective-permute-start.8) | collective-permute-done | bytes 196640 | tf_op jit(solution)/shard_map/ppermute | solution.py:827
  74.8 5.3 %collective-permute-start.10 = (bf16[256,384]{1,0:T(8,128)(2,1)S(1)}, bf16[256,384]{1,0:T(8,128)(2,1)S(1)}, u32[]{:S(2)}, u32[]{:S(2)}) collective-permute-start(bf16[256,384]{1,0:T(8,128)(2,1)S(1)} %get-tuple-element.150), channel_id=1, source_target_pairs={{0,1},{1,2},{2,3},{3,0},{4,5},{5,6},{6,7},{7,4},{8,9},{9,10},{10,1... | collective-permute-start | bytes 589832 | tf_op jit(solution)/shard_map/ppermute | solution.py:827
  83.9 5.5 %mix.4 = (bf16[256,384]{1,0:T(8,128)(2,1)S(1)}, bf16[256,384]{1,0:T(8,128)(2,1)S(1)}, bf16[256,384]{1,0:T(8,128)(2,1)S(1)}, bf16[256,384]{1,0:T(8,128)(2,1)S(1)}) custom-call(s32[2]{0:T(128)S(1)} %pad_add_fusion.place_ref, s32[2]{0:T(128)S(1)} %get-tuple-element.280.long_flags, bf16[256,384]{1,0:T(8,128)(2,1)S(1)} %get-tuple-element.130.refs_0_.refs_12_, ...), custom_call_target="tpu_custom_call" | custom-call | flops 805306368 | bytes 7864320 | tf_op jit(solution)/shard_map/mix/pallas_call | solution.py:213
  90.1 4.7 %collective-permute-done.11.refs_2_.refs_12_ = bf16[256,384]{1,0:T(8,128)(2,1)S(1)} collective-permute-done((bf16[256,384]{1,0:T(8,128)(2,1)S(1)}, bf16[256,384]{1,0:T(8,128)(2,1)S(1)}, u32[]{:S(2)}, u32[]{:S(2)}) %collective-permute-start.11) | collective-permute-done | bytes 196640 | tf_op jit(solution)/shard_map/ppermute | solution.py:827
  94.8 4.7 %collective-permute-start.13 = (bf16[256,384]{1,0:T(8,128)(2,1)S(1)}, bf16[256,384]{1,0:T(8,128)(2,1)S(1)}, u32[]{:S(2)}, u32[]{:S(2)}) collective-permute-start(bf16[256,384]{1,0:T(8,128)(2,1)S(1)} %get-tuple-element.158), channel_id=1, source_target_pairs={{0,1},{1,2},{2,3},{3,0},{4,5},{5,6},{6,7},{7,4},{8,9},{9,10},{10,1... | collective-permute-start | bytes 589832 | tf_op jit(solution)/shard_map/ppermute | solution.py:827
  101.9 20.4 %feed.2 = (bf16[256,384]{1,0:T(8,128)(2,1)S(1)}, bf16[256,384]{1,0:T(8,128)(2,1)S(1)}, bf16[256,384]{1,0:T(8,128)(2,1)S(1)}, bf16[256,384]{1,0:T(8,128)(2,1)S(1)...) custom-call(s32[2]{0:T(128)S(1)} %pad_add_fusion.place_ref, ...), custom_call_target="tpu_custom_call" | custom-call | flops 10871635968 | bytes 23592960 | tf_op jit(solution)/shard_map/feed/pallas_call | solution.py:352
  125.1 20.4 %feed.3 = (bf16[256,384]{1,0:T(8,128)(2,1)S(1)}, bf16[256,384]{1,0:T(8,128)(2,1)S(1)}, bf16[256,384]{1,0:T(8,128)(2,1)S(1)}, bf16[256,384]{1,0:T(8,128)(2,1)S(1)...) custom-call(s32[2]{0:T(128)S(1)} %pad_add_fusion.place_ref, ...), custom_call_target="tpu_custom_call", output_to_operand_aliasing={{4}: (13, {})} | custom-call | flops 10871635968 | bytes 23592960 | tf_op jit(solution)/shard_map/feed/pallas_call | solution.py:352
  145.6 3.7 %collective-permute-start.19 = (bf16[256,384]{1,0:T(8,128)(2,1)S(1)}, bf16[256,384]{1,0:T(8,128)(2,1)S(1)}, u32[]{:S(2)}, u32[]{:S(2)}) collective-permute-start(bf16[256,384]{1,0:T(8,128)(2,1)S(1)} %get-tuple-element.183), channel_id=1, source_target_pairs={{0,3},{1,0},{2,1},{3,2},{4,7},{5,4},{6,5},{7,6},{8,11},{9,8},{10,9... | collective-permute-start | bytes 589832 | tf_op jit(solution)/shard_map/ppermute | solution.py:827
  149.9 14.1 %weights.2 = (bf16[4,2,224,768]{3,2,1,0:T(8,128)(2,1)}, bf16[4,2,224,768]{3,2,1,0:T(8,128)(2,1)}) custom-call(s32[2]{0:T(128)S(1)} %pad_add_fusion.place_ref, bf16[3072,512]{1,0:T(8,128)(2,1)} %get-tuple-element.171.refs_0_, bf16[3072,512]{1,0:T(8,128)(2,1)} %get-tuple-element.172.refs_1_, bf16[3072,512]{1,0:T(8,128)(2,1)} %get-tuple-element.173.refs_2_, ...), custom_call_target="tpu_custom_call" | custom-call | flops 4831838208 | bytes 14155776 | tf_op jit(solution)/shard_map/weights/pallas_call | solution.py:505
  166.3 5.8 %mix.5 = (bf16[256,768]{1,0:T(8,128)(2,1)S(1)}, bf16[256,768]{1,0:T(8,128)(2,1)S(1)}, bf16[256,768]{1,0:T(8,128)(2,1)S(1)}, bf16[256,768]{1,0:T(8,128)(2,1)S(1)}) custom-call(s32[2]{0:T(128)S(1)} %pad_add_fusion.place_ref, s32[4]{0:T(128)S(1)} %copy-done.23, bf16[256,384]{1,0:T(8,128)(2,1)S(1)} %get-tuple-element.153.refs_0_, ...), custom_call_target="tpu_custom_call" | custom-call | flops 1610612736 | bytes 9437184 | tf_op jit(solution)/shard_map/mix/pallas_call | solution.py:213
  174.4 14.2 %weights.3 = (bf16[4,2,224,768]{3,2,1,0:T(8,128)(2,1)}, bf16[4,2,224,768]{3,2,1,0:T(8,128)(2,1)}) custom-call(s32[2]{0:T(128)S(1)} %pad_add_fusion.place_ref, bf16[3072,512]{1,0:T(8,128)(2,1)} %get-tuple-element.171.refs_0_, bf16[3072,512]{1,0:T(8,128)(2,1)} %get-tuple-element.172.refs_1_, bf16[3072,512]{1,0:T(8,128)(2,1)} %get-tuple-element.173.refs_2_, ...), custom_call_target="tpu_custom_call" | custom-call | flops 4831838208 | bytes 14155776 | tf_op jit(solution)/shard_map/weights/pallas_call | solution.py:505
  198.6 18.1 %logits.1 = (bf16[4,3,64,1024]{3,2,1,0:T(8,128)(2,1)}, bf16[4,3,64,1024]{3,2,1,0:T(8,128)(2,1)}, bf16[4,3,64,1024]{3,2,1,0:T(8,128)(2,1)}, bf16[4,3,64,1024]{3,2,1,0:T(8,128)(2,1)}) custom-call(s32[2]{0:T(128)S(1)} %pad_add_fusion.place_ref, s32[4]{0:T(128)S(1)} %copy-done.23, bf16[256,384]{1,0:T(8,128)(2,1)} %copy-done.14, bf16[256,384]{1,0:T(8,128)(2,1)} %copy-done.15, ...), custom_call_target="tpu_custom_call" | custom-call | flops 1610612736 | bytes 12582912 | tf_op jit(solution)/shard_map/logits/pallas_call | solution.py:651
  216.7 8.0 %collective-permute-done.25 = bf16[2,2,224,768]{3,2,1,0:T(8,128)(2,1)S(1)} collective-permute-done((bf16[2,2,224,768]{3,2,1,0:T(8,128)(2,1)S(1)}, bf16[2,2,224,768]{3,2,1,0:T(8,128)(2,1)S(1)}, u32[]{:S(2)}, u32[]{:S(2)}) %collective-permute-start.25) | collective-permute-done | bytes 1376288 | tf_op jit(solution)/shard_map/ppermute | solution.py:831
  237.8 10.9 %collective-permute-done.33 = bf16[1,2,224,768]{3,2,1,0:T(8,128)(2,1)S(1)} collective-permute-done((bf16[1,2,224,768]{3,2,1,0:T(8,128)(2,1)S(1)}, bf16[1,2,224,768]{3,2,1,0:T(8,128)(2,1)S(1)}, u32[]{:S(2)}, u32[]{:S(2)}) %collective-permute-start.33) | collective-permute-done | bytes 688160 | tf_op jit(solution)/shard_map/ppermute | solution.py:831
  253.5 10.3 %input.1 = (bf16[4,256,768]{2,1,0:T(8,128)(2,1)}, bf16[4,4,32,768]{3,2,1,0:T(8,128)(2,1)S(1)}, bf16[4,4,32,768]{3,2,1,0:T(8,128)(2,1)S(1)}) custom-call(s32[2]{0:T(128)S(1)} %pad_add_fusion.place_ref, bf16[256,768]{1,0:T(8,128)(2,1)} %copy-done.24, bf16[256,768]{1,0:T(8,128)(2,1)} %copy-done.50, bf16[256,768]{1,0:T(8,128)(2,1)} %copy-done.49, ...), custom_call_target="tpu_custom_call" | custom-call | flops 2415919104 | bytes 14155776 | tf_op jit(solution)/shard_map/input/pallas_call | solution.py:727
  274.9 3.3 %collective-permute-done.37 = bf16[1,3,64,1024]{3,2,1,0:T(8,128)(2,1)S(1)} collective-permute-done((bf16[1,3,64,1024]{3,2,1,0:T(8,128)(2,1)S(1)}, bf16[1,3,64,1024]{3,2,1,0:T(8,128)(2,1)S(1)}, u32[]{:S(2)}, u32[]{:S(2)}) %collective-permute-start.37) | collective-permute-done | bytes 393248 | tf_op jit(solution)/shard_map/ppermute | solution.py:831
  283.1 7.5 %collective-permute-done.36 = bf16[1,3,64,1024]{3,2,1,0:T(8,128)(2,1)S(1)} collective-permute-done((bf16[1,3,64,1024]{3,2,1,0:T(8,128)(2,1)S(1)}, bf16[1,3,64,1024]{3,2,1,0:T(8,128)(2,1)S(1)}, u32[]{:S(2)}, u32[]{:S(2)}) %collective-permute-start.36) | collective-permute-done | bytes 393248 | tf_op jit(solution)/shard_map/ppermute | solution.py:831
  301.4 3.4 %collective-permute-start.44 = (bf16[32,768]{1,0:T(8,128)(2,1)S(1)}, bf16[32,768]{1,0:T(8,128)(2,1)S(1)}, u32[]{:S(2)}, u32[]{:S(2)}) collective-permute-start(bf16[32,768]{1,0:T(8,128)(2,1)S(1)} %get-tuple-element.274), channel_id=1, source_target_pairs={{0,3},{1,0},{2,1},{3,2},{4,7},{5,4},{6,5},{7,6},{8,11},{9,8},{10,9... | collective-permute-start | bytes 147464 | tf_op jit(solution)/shard_map/ppermute | solution.py:827
  (234 shorter events, 91.2 us)
Async XLA Ops:
  7.2 94.7 %all-gather.2.cloned.1.call-start = ((), (), s32[]{:S(2)}) async-start(), calls=%async_computation | async-start | bytes 1216512 | tf_op jit(solution)/shard_map/all_gather | solution.py:961
  9.7 20.1 %collective-permute-start = (bf16[96,768]{1,0:T(8,128)(2,1)S(1)}, bf16[96,768]{1,0:T(8,128)(2,1)S(1)}, u32[]{:S(2)}, u32[]{:S(2)}) collective-permute-start(bf16[96,768]{1,0:T(8,128)(2,1)S(1)} %dynamic-slice_bitcast_fusion), channel_id=1, source_target_pairs={{0,3},{1,0},{2,1},{3,2},{4,7},{5,4},{6,5},{7,6},{8,11},{9,8},{10,9... | collective-permute-start | bytes 442376 | tf_op jit(solution)/shard_map/ppermute | solution.py:827
  94.8 27.5 %collective-permute-start.13 = (bf16[256,384]{1,0:T(8,128)(2,1)S(1)}, bf16[256,384]{1,0:T(8,128)(2,1)S(1)}, u32[]{:S(2)}, u32[]{:S(2)}) collective-permute-start(bf16[256,384]{1,0:T(8,128)(2,1)S(1)} %get-tuple-element.158), channel_id=1, source_target_pairs={{0,1},{1,2},{2,3},{3,0},{4,5},{5,6},{6,7},{7,4},{8,9},{9,10},{10,1... | collective-permute-start | bytes 589832 | tf_op jit(solution)/shard_map/ppermute | solution.py:827
  99.5 22.8 %collective-permute-start.14 = (bf16[256,384]{1,0:T(8,128)(2,1)S(1)}, bf16[256,384]{1,0:T(8,128)(2,1)S(1)}, u32[]{:S(2)}, u32[]{:S(2)}) collective-permute-start(bf16[256,384]{1,0:T(8,128)(2,1)S(1)} %get-tuple-element.159), channel_id=1, source_target_pairs={{0,2},{1,3},{2,0},{3,1},{4,6},{5,7},{6,4},{7,5},{8,10},{9,11},{10,... | collective-permute-start | bytes 589832 | tf_op jit(solution)/shard_map/ppermute | solution.py:827
  100.9 21.5 %collective-permute-start.15 = (bf16[256,384]{1,0:T(8,128)(2,1)S(1)}, bf16[256,384]{1,0:T(8,128)(2,1)S(1)}, u32[]{:S(2)}, u32[]{:S(2)}) collective-permute-start(bf16[256,384]{1,0:T(8,128)(2,1)S(1)} %get-tuple-element.160), channel_id=1, source_target_pairs={{0,3},{1,0},{2,1},{3,2},{4,7},{5,4},{6,5},{7,6},{8,11},{9,8},{10,9... | collective-permute-start | bytes 589832 | tf_op jit(solution)/shard_map/ppermute | solution.py:827
  122.4 23.1 %collective-permute-start.16 = (bf16[256,384]{1,0:T(8,128)(2,1)S(1)}, bf16[256,384]{1,0:T(8,128)(2,1)S(1)}, u32[]{:S(2)}, u32[]{:S(2)}) collective-permute-start(bf16[256,384]{1,0:T(8,128)(2,1)S(1)} %get-tuple-element.167), channel_id=1, source_target_pairs={{0,3},{1,0},{2,1},{3,2},{4,7},{5,4},{6,5},{7,6},{8,11},{9,8},{10,9... | collective-permute-start | bytes 589832 | tf_op jit(solution)/shard_map/ppermute | solution.py:827
  124.4 21.1 %collective-permute-start.17 = (bf16[256,384]{1,0:T(8,128)(2,1)S(1)}, bf16[256,384]{1,0:T(8,128)(2,1)S(1)}, u32[]{:S(2)}, u32[]{:S(2)}) collective-permute-start(bf16[256,384]{1,0:T(8,128)(2,1)S(1)} %get-tuple-element.168), channel_id=1, source_target_pairs={{0,2},{1,3},{2,0},{3,1},{4,6},{5,7},{6,4},{7,5},{8,10},{9,11},{10,... | collective-permute-start | bytes 589832 | tf_op jit(solution)/shard_map/ppermute | solution.py:827
  124.9 20.6 %collective-permute-start.18 = (bf16[256,384]{1,0:T(8,128)(2,1)S(1)}, bf16[256,384]{1,0:T(8,128)(2,1)S(1)}, u32[]{:S(2)}, u32[]{:S(2)}) collective-permute-start(bf16[256,384]{1,0:T(8,128)(2,1)S(1)} %get-tuple-element.169), channel_id=1, source_target_pairs={{0,1},{1,2},{2,3},{3,0},{4,5},{5,6},{6,7},{7,4},{8,9},{9,10},{10,1... | collective-permute-start | bytes 589832 | tf_op jit(solution)/shard_map/ppermute | solution.py:827
  145.6 18.5 %collective-permute-start.19 = (bf16[256,384]{1,0:T(8,128)(2,1)S(1)}, bf16[256,384]{1,0:T(8,128)(2,1)S(1)}, u32[]{:S(2)}, u32[]{:S(2)}) collective-permute-start(bf16[256,384]{1,0:T(8,128)(2,1)S(1)} %get-tuple-element.183), channel_id=1, source_target_pairs={{0,3},{1,0},{2,1},{3,2},{4,7},{5,4},{6,5},{7,6},{8,11},{9,8},{10,9... | collective-permute-start | bytes 589832 | tf_op jit(solution)/shard_map/ppermute | solution.py:827
  165.7 22.9 %collective-permute-start.23 = (bf16[4,2,224,768]{3,2,1,0:T(8,128)(2,1)}, bf16[4,2,224,768]{3,2,1,0:T(8,128)(2,1)S(1)}, u32[]{:S(2)}, u32[]{:S(2)}) collective-permute-start(bf16[4,2,224,768]{3,2,1,0:T(8,128)(2,1)} %get-tuple-element.193), channel_id=1, source_target_pairs={{0,4},{4,0},{8,12},{12,8},{16,20},{20,16},{24,28},{28,24},{1,5},{5... | collective-permute-start | bytes 8257544 | tf_op jit(solution)/shard_map/ppermute | solution.py:831
  165.8 25.5 %collective-permute-start.24 = (bf16[4,2,224,768]{3,2,1,0:T(8,128)(2,1)}, bf16[4,2,224,768]{3,2,1,0:T(8,128)(2,1)S(1)}, u32[]{:S(2)}, u32[]{:S(2)}) collective-permute-start(bf16[4,2,224,768]{3,2,1,0:T(8,128)(2,1)} %get-tuple-element.195), channel_id=1, source_target_pairs={{0,4},{4,0},{8,12},{12,8},{16,20},{20,16},{24,28},{28,24},{1,5},{5... | collective-permute-start | bytes 8257544 | tf_op jit(solution)/shard_map/ppermute | solution.py:831
  172.9 20.4 %collective-permute-start.22 = (bf16[256,768]{1,0:T(8,128)(2,1)S(1)}, bf16[256,768]{1,0:T(8,128)(2,1)S(1)}, u32[]{:S(2)}, u32[]{:S(2)}) collective-permute-start(bf16[256,768]{1,0:T(8,128)(2,1)S(1)} %get-tuple-element.192), channel_id=1, source_target_pairs={{0,2},{1,3},{2,0},{3,1},{4,6},{5,7},{6,4},{7,5},{8,10},{9,11},{10,... | collective-permute-start | bytes 1179656 | tf_op jit(solution)/shard_map/ppermute | solution.py:827
  193.3 31.4 %collective-permute-start.25 = (bf16[2,2,224,768]{3,2,1,0:T(8,128)(2,1)S(1)}, bf16[2,2,224,768]{3,2,1,0:T(8,128)(2,1)S(1)}, u32[]{:S(2)}, u32[]{:S(2)}) collective-permute-start(bf16[2,2,224,768]{3,2,1,0:T(8,128)(2,1)S(1)} %add_convert_fusion.1), channel_id=1, source_target_pairs={{0,8},{4,12},{8,0},{12,4},{16,24},{20,28},{24,16},{28,20},{1,9},{5... | collective-permute-start | bytes 4128776 | tf_op jit(solution)/shard_map/ppermute | solution.py:831
  194.8 31.2 %collective-permute-start.26 = (bf16[2,2,224,768]{3,2,1,0:T(8,128)(2,1)S(1)}, bf16[2,2,224,768]{3,2,1,0:T(8,128)(2,1)}, u32[]{:S(2)}, u32[]{:S(2)}) collective-permute-start(bf16[2,2,224,768]{3,2,1,0:T(8,128)(2,1)S(1)} %add_convert_fusion), channel_id=1, source_target_pairs={{0,16},{4,20},{8,24},{12,28},{16,0},{20,4},{24,8},{28,12},{1,17},{... | collective-permute-start | bytes 4128776 | tf_op jit(solution)/shard_map/ppermute | solution.py:831
  196.3 20.3 %collective-permute-start.27 = (bf16[256,768]{1,0:T(8,128)(2,1)S(1)}, bf16[256,768]{1,0:T(8,128)(2,1)S(1)}, u32[]{:S(2)}, u32[]{:S(2)}) collective-permute-start(bf16[256,768]{1,0:T(8,128)(2,1)S(1)} %get-tuple-element.203), channel_id=1, source_target_pairs={{0,3},{1,0},{2,1},{3,2},{4,7},{5,4},{6,5},{7,6},{8,11},{9,8},{10,9... | collective-permute-start | bytes 1179656 | tf_op jit(solution)/shard_map/ppermute | solution.py:827
  198.6 18.1 %collective-permute-start.28 = (bf16[256,768]{1,0:T(8,128)(2,1)S(1)}, bf16[256,768]{1,0:T(8,128)(2,1)S(1)}, u32[]{:S(2)}, u32[]{:S(2)}) collective-permute-start(bf16[256,768]{1,0:T(8,128)(2,1)S(1)} %get-tuple-element.204), channel_id=1, source_target_pairs={{0,1},{1,2},{2,3},{3,0},{4,5},{5,6},{6,7},{7,4},{8,9},{9,10},{10,1... | collective-permute-start | bytes 1179656 | tf_op jit(solution)/shard_map/ppermute | solution.py:827
  230.4 18.4 %collective-permute-start.33 = (bf16[1,2,224,768]{3,2,1,0:T(8,128)(2,1)S(1)}, bf16[1,2,224,768]{3,2,1,0:T(8,128)(2,1)S(1)}, u32[]{:S(2)}, u32[]{:S(2)}) collective-permute-start(bf16[1,2,224,768]{3,2,1,0:T(8,128)(2,1)S(1)} %add_convert_fusion.6), channel_id=1, source_target_pairs={{0,16},{4,20},{8,24},{12,28},{16,0},{20,4},{24,8},{28,12},{1,17},{... | collective-permute-start | bytes 2064392 | tf_op jit(solution)/shard_map/ppermute | solution.py:831
  232.0 18.3 %collective-permute-start.34 = (bf16[1,2,224,768]{3,2,1,0:T(8,128)(2,1)S(1)}, bf16[1,2,224,768]{3,2,1,0:T(8,128)(2,1)S(1)}, u32[]{:S(2)}, u32[]{:S(2)}) collective-permute-start(bf16[1,2,224,768]{3,2,1,0:T(8,128)(2,1)S(1)} %add_convert_fusion.5), channel_id=1, source_target_pairs={{0,8},{4,12},{8,0},{12,4},{16,24},{20,28},{24,16},{28,20},{1,9},{5... | collective-permute-start | bytes 2064392 | tf_op jit(solution)/shard_map/ppermute | solution.py:831
  236.3 29.6 %collective-permute-start.31 = (bf16[2,3,64,1024]{3,2,1,0:T(8,128)(2,1)S(1)}, bf16[2,3,64,1024]{3,2,1,0:T(8,128)(2,1)S(1)}, u32[]{:S(2)}, u32[]{:S(2)}) collective-permute-start(bf16[2,3,64,1024]{3,2,1,0:T(8,128)(2,1)S(1)} %add_convert_fusion.3), channel_id=1, source_target_pairs={{0,8},{4,12},{8,0},{12,4},{16,24},{20,28},{24,16},{28,20},{1,9},{5... | collective-permute-start | bytes 2359304 | tf_op jit(solution)/shard_map/ppermute | solution.py:831
  237.1 30.0 %collective-permute-start.32 = (bf16[2,3,64,1024]{3,2,1,0:T(8,128)(2,1)S(1)}, bf16[2,3,64,1024]{3,2,1,0:T(8,128)(2,1)S(1)}, u32[]{:S(2)}, u32[]{:S(2)}) collective-permute-start(bf16[2,3,64,1024]{3,2,1,0:T(8,128)(2,1)S(1)} %add_convert_fusion.2), channel_id=1, source_target_pairs={{0,16},{4,20},{8,24},{12,28},{16,0},{20,4},{24,8},{28,12},{1,17},{... | collective-permute-start | bytes 2359304 | tf_op jit(solution)/shard_map/ppermute | solution.py:831
  270.6 22.0 %collective-permute-start.45 = (bf16[224,768]{1,0:T(8,128)(2,1)S(1)}, bf16[224,768]{1,0:T(8,128)(2,1)S(1)}, u32[]{:S(2)}, u32[]{:S(2)}) collective-permute-start(bf16[224,768]{1,0:T(8,128)(2,1)S(1)} %fusion), channel_id=1, source_target_pairs={{0,1},{1,2},{2,3},{3,0},{4,5},{5,6},{6,7},{7,4},{8,9},{9,10},{10,1... | collective-permute-start | bytes 1032200 | tf_op jit(solution)/shard_map/ppermute | solution.py:827
  272.1 20.5 %collective-permute-start.46 = (bf16[224,768]{1,0:T(8,128)(2,1)S(1)}, bf16[224,768]{1,0:T(8,128)(2,1)S(1)}, u32[]{:S(2)}, u32[]{:S(2)}) collective-permute-start(bf16[224,768]{1,0:T(8,128)(2,1)S(1)} %get-tuple-element.230), channel_id=1, source_target_pairs={{0,3},{1,0},{2,1},{3,2},{4,7},{5,4},{6,5},{7,6},{8,11},{9,8},{10,9... | collective-permute-start | bytes 1032200 | tf_op jit(solution)/shard_map/ppermute | solution.py:827
  280.4 19.3 %collective-permute-start.41 = (bf16[1,4,32,768]{3,2,1,0:T(8,128)(2,1)}, bf16[1,4,32,768]{3,2,1,0:T(8,128)(2,1)}, u32[]{:S(2)}, u32[]{:S(2)}) collective-permute-start(bf16[1,4,32,768]{3,2,1,0:T(8,128)(2,1)} %get-tuple-element.266), channel_id=1, source_target_pairs={{0,24},{4,28},{8,16},{12,20},{16,8},{20,12},{24,0},{28,4},{1,25},{... | collective-permute-start | bytes 589832 | tf_op jit(solution)/shard_map/ppermute | solution.py:831
  281.6 18.1 %collective-permute-start.40 = (bf16[1,4,32,768]{3,2,1,0:T(8,128)(2,1)}, bf16[1,4,32,768]{3,2,1,0:T(8,128)(2,1)}, u32[]{:S(2)}, u32[]{:S(2)}) collective-permute-start(bf16[1,4,32,768]{3,2,1,0:T(8,128)(2,1)} %get-tuple-element.267), channel_id=1, source_target_pairs={{0,16},{4,20},{8,24},{12,28},{16,0},{20,4},{24,8},{28,12},{1,17},{... | collective-permute-start | bytes 589832 | tf_op jit(solution)/shard_map/ppermute | solution.py:831
  (76 other events, 922.8 us)
Sparse Core Ops, SparseCore 0:
  11.5 66.4 all-gather.1

commit v4 on v3

--- a/solution.py
+++ b/solution.py
@@ -330,7 +330,7 @@
             grads[d][...] = interleave(mine, heads, size).astype(BF16)
 
 
-def feed(place, pieces, x, cot, project, gain, up, up_bias, down, down_bias, heads, c, blocks):
+def feed(place, pieces, x, cot, project, gain, up, up_bias, down, down_bias, heads, c, chunks, earlier):
     zones = len(pieces)
     count, rows, depth = x.shape
     size = depth // zones // heads
@@ -339,13 +339,12 @@
     steps = hidden // tile
     tokens = count * rows
     wide = pieces[0].shape[1]
-    earlier = [] if blocks is None else [blocks]
     shapes = [jax.ShapeDtypeStruct((rows, wide), BF16)] * zones + [
-        far((2 * count, rows, depth), BF16),
-        far((hidden, tokens), BF16),
-        far((hidden, tokens), BF16),
-        far((tokens, depth), BF16),
-        far((depth, tokens), BF16),
+        far((chunks * count, rows, depth), BF16),
+        far((hidden, chunks * tokens), BF16),
+        far((hidden, chunks * tokens), BF16),
+        far((chunks * tokens, depth), BF16),
+        far((depth, chunks * tokens), BF16),
         jax.ShapeDtypeStruct((1, hidden), F32),
         jax.ShapeDtypeStruct((2, depth), F32),
     ]
@@ -373,10 +372,14 @@
                     lambda *_: (c, 0, 0),
                     pipeline_mode=pl.Buffered(buffer_count=1),
                 ),
-                pl.BlockSpec((tile, tokens), lambda f, *_: (f, 0)),
-                pl.BlockSpec((tile, tokens), lambda f, *_: (f, 0)),
-                pl.BlockSpec((tokens, depth // steps), lambda f, *_: (0, f)),
-                whole((depth, tokens)),
+                pl.BlockSpec((tile, tokens), lambda f, *_: (f, c)),
+                pl.BlockSpec((tile, tokens), lambda f, *_: (f, c)),
+                pl.BlockSpec((tokens, depth // steps), lambda f, *_: (c, f)),
+                pl.BlockSpec(
+                    (depth, tokens),
+                    lambda *_: (0, c),
+                    pipeline_mode=pl.Buffered(buffer_count=1),
+                ),
                 pl.BlockSpec((1, tile), lambda f, *_: (0, f)),
                 whole((2, depth)),
             ],
@@ -397,7 +400,7 @@
             4 * depth * hidden + 4 * tokens * hidden + 20 * tokens * depth,
             tokens * hidden,
         ),
-        input_output_aliases={zones + 9: zones} if earlier else {},
+        input_output_aliases={zones + 9 + i: zones + i for i in range(len(earlier))},
         name="feed",
     )(
         place,
@@ -444,14 +447,12 @@
 
 
 def weights_kernel(zones, chunks, heads, place_ref, *refs):
-    acts, pres = refs[:chunks], refs[chunks : 2 * chunks]
-    attends = refs[2 * chunks : 3 * chunks]
-    norms, cots = refs[3 * chunks : 4 * chunks], refs[4 * chunks : 5 * chunks]
-    pieces = refs[5 * chunks : (5 + zones) * chunks]
-    first_ref, second_ref, scratch_ref, mixed_ref = refs[(5 + zones) * chunks :]
-    mixes = [mixed_ref.at[c] for c in range(chunks)]
+    act_ref, pre_ref, attended_ref, norm_ref, cot_ref = refs[:5]
+    pieces = refs[5 : 5 + zones * chunks]
+    first_ref, second_ref, scratch_ref, mixed_ref = refs[5 + zones * chunks :]
+    part = scratch_ref.shape[1] // zones
     rows, wide = pieces[0].shape
-    count = norms[0].shape[0] // rows
+    count = norm_ref.shape[0] // rows // chunks
 
     @pl.when(pl.program_id(0) == 0)
     def _():
@@ -462,18 +463,12 @@
                     separate(piece[...], seq, count, heads, wide // heads // count)
                     for piece in group
                 ]
-                mixed_ref[c, seq * rows : (seq + 1) * rows, :] = jnp.concatenate(parts, axis=1)
-    part = scratch_ref.shape[1] // zones
-
-    def total(lefts, rights):
-        result = dot_nn(lefts[0][...], rights[0][...])
-        for left, right in zip(lefts[1:], rights[1:]):
-            result = result + dot_nn(left[...], right[...])
-        return result
-
-    scratch_ref[0] = total(pres, norms)
-    scratch_ref[1] = total(acts, cots)
-    square = total(attends, mixes)
+                at = (c * count + seq) * rows
+                mixed_ref[at : at + rows, :] = jnp.concatenate(parts, axis=1)
+
+    scratch_ref[0] = dot_nn(pre_ref[...], norm_ref[...])
+    scratch_ref[1] = dot_nn(act_ref[...], cot_ref[...])
+    square = dot_nn(attended_ref[...], mixed_ref[...])
     for d in range(zones):
         at = pl.ds(pl.multiple_of(lax.rem(place_ref[0] + d, zones) * part, 8), part)
         parts = [scratch_ref[0, at, :], scratch_ref[1, at, :], pack(square, -d % zones, zones)]
@@ -483,10 +478,10 @@
         side[0, number] = jnp.concatenate(parts, axis=0).astype(BF16)
 
 
-def weight_grads(place, acts, pres, attends, norms, cots, pieces, heads, odd, zones, ranks):
-    chunks = len(acts)
-    hidden, tokens = acts[0].shape
-    depth = norms[0].shape[1]
+def weight_grads(place, act, pre, attended, norm, cot, pieces, heads, odd, zones, ranks):
+    chunks = len(pieces)
+    hidden, tokens = act.shape
+    depth = norm.shape[1]
     tile, square = hidden // ranks, depth // ranks
     rows = 2 * tile // zones + group_rows(square, zones)
     rows = -(-rows // 16) * 16
@@ -507,30 +502,26 @@
         grid_spec=pltpu.PrefetchScalarGridSpec(
             num_scalar_prefetch=1,
             grid=(ranks // 2,),
-            in_specs=[pl.BlockSpec((tile, tokens), tall)] * (2 * chunks)
-            + [pl.BlockSpec((square, tokens), tall)] * chunks
-            + [whole((tokens, depth))] * (2 * chunks)
+            in_specs=[pl.BlockSpec((tile, tokens), tall)] * 2
+            + [pl.BlockSpec((square, tokens), tall)]
+            + [whole((tokens, depth))] * 2
             + [whole(pieces[0][0].shape)] * (zones * chunks),
             out_specs=[pl.BlockSpec((1, *shape[1:]), first), pl.BlockSpec((1, *shape[1:]), second)],
             scratch_shapes=[
                 pltpu.VMEM((2, tile, depth), F32),
-                pltpu.VMEM((chunks, tokens, depth), BF16),
+                pltpu.VMEM((tokens, depth), BF16),
             ],
         ),
         out_shape=[far(shape, BF16)] * 2,
         compiler_params=params(24),
         cost_estimate=cost(
-            2 * chunks * hidden * tokens * depth,
-            2 * chunks * hidden * tokens + 2 * hidden * depth + 4 * chunks * tokens * depth,
+            2 * hidden * tokens * depth,
+            2 * hidden * tokens + 2 * hidden * depth + 4 * tokens * depth,
         ),
         name="weights",
     )(
         place,
-        *map(kept, acts),
-        *map(kept, pres),
-        *map(kept, attends),
-        *map(kept, norms),
-        *map(kept, cots),
+        *map(kept, (act, pre, attended, norm, cot)),
         *(kept(piece) for group in pieces for piece in group),
     )
 
@@ -677,8 +668,8 @@
 def input_kernel(zones, heads, size, ranks, count, place_ref, *refs):
     pieces = refs[:zones]
     x_ref, gain_ref, weight_ref, extra_in_ref = refs[zones : zones + 4]
-    resids = refs[zones + 4 : zones + 6]
-    grad_ref, send_ref, keep_ref, total_ref, gain_sum_ref, extra_ref = refs[zones + 6 :]
+    resid_ref = refs[zones + 4]
+    grad_ref, send_ref, keep_ref, total_ref, gain_sum_ref, extra_ref = refs[zones + 5 :]
     depth = x_ref.shape[2]
     seq = pl.program_id(0)
 
@@ -701,7 +692,7 @@
     back = jnp.concatenate(parts, axis=1).astype(BF16)
     grad_norm = dot_nn(back, weight_ref[...])
     gain_sum_ref[...] += jnp.sum(grad_norm * hat, 0, keepdims=True)
-    resid = jnp.where(seq < count // 2, resids[0][...], resids[1][...]).astype(F32).T
+    resid = resid_ref[...].astype(F32).T
     grad = resid + norm_back(grad_norm * gain_ref[...], hat, inverse)
     grad_ref[0] = grad.astype(BF16)
     total_ref[...] += dot_tn(norm, back)
@@ -717,7 +708,7 @@
         store_square(place_ref, (send_ref, keep_ref), total_ref, extra_ref, zones, ranks)
 
 
-def input_grads(place, pieces, x, gain, weight, resids, extra, heads, ranks):
+def input_grads(place, pieces, x, gain, weight, resid, extra, heads, ranks):
     zones = len(pieces)
     count, rows, depth = x.shape
     size = depth // zones // heads
@@ -735,8 +726,7 @@
                 whole(gain.shape),
                 whole(weight.shape),
                 whole(extra.shape),
-                pl.BlockSpec((depth, rows), lambda s, *_: (0, jnp.minimum(s, count // 2 - 1))),
-                pl.BlockSpec((depth, rows), lambda s, *_: (0, jnp.maximum(s - count // 2, 0))),
+                pl.BlockSpec((depth, rows), lambda s, *_: (0, s)),
             ],
             out_specs=[
                 pl.BlockSpec((1, rows, depth), lambda s, *_: (s, 0, 0)),
@@ -759,7 +749,7 @@
             4 * count * rows * depth * depth, 12 * count * rows * depth + 8 * depth * depth
         ),
         name="input",
-    )(place, *map(kept, pieces), kept(x), gain, kept(weight), extra, *map(kept, resids))
+    )(place, *map(kept, pieces), kept(x), gain, kept(weight), extra, kept(resid))
 
 
 def total_of(terms):
@@ -778,7 +768,7 @@
 def feed_sums_kernel(zones, tile, square, *refs):
     up_ref, down_ref, square_ref = refs[zones:]
     total = total_of(refs[:zones])
-    up_ref[...] = total[:tile].T
+    up_ref[...] = total[:tile]
     down_ref[...] = total[tile : 2 * tile]
     packed = total[2 * tile : 2 * tile + group_rows(square, zones)]
     square_ref[...] = unpack(packed, square, zones).T
@@ -790,9 +780,9 @@
         functools.partial(feed_sums_kernel, zones, tile, square),
         grid=(1,),
         in_specs=[whole(term.shape) for term in terms],
-        out_specs=[whole((depth, tile)), whole((tile, depth)), whole((depth // zones, square))],
+        out_specs=[whole((tile, depth)), whole((tile, depth)), whole((depth // zones, square))],
         out_shape=[
-            far((depth, tile), F32),
+            far((tile, depth), F32),
             far((tile, depth), F32),
             far((depth // zones, square), F32),
         ],
@@ -871,7 +861,7 @@
             for keep, came in zip(keeps, self.came)
         ]
         if results:
-            sent = lax.optimization_barrier((*sent, *results))[:2]
+            sent = [after(value, *results) for value in sent]
         self.keeps, self.sent = keeps, sent
         self.went = [
             flip(value, "dp", self.ranks, masks[0]) for value, masks in zip(sent, self.masks)
@@ -889,7 +879,7 @@
     def second(self, *results):
         sent = [value.astype(BF16) for value in self.rest(self.ranks // 8, self.ranks // 4)]
         if results:
-            sent = lax.optimization_barrier((*sent, *results))[:2]
+            sent = [after(value, *results) for value in sent]
         self.last = [
             flip(value, "dp", self.ranks, masks[1]) for value, masks in zip(sent, self.masks)
         ]
@@ -975,7 +965,7 @@
     def call_values(place, c, weights):
         return make_values(place, part(block_input, c), gain1, weights, zones, heads, c == 0)
 
-    def call_feed(place, c, pieces, blocks):
+    def call_feed(place, c, pieces, earlier):
         return feed(
             place,
             pieces,
@@ -989,7 +979,8 @@
             down_bias[None],
             heads,
             c,
-            blocks,
+            2,
+            earlier,
         )
 
     made = call_values(place, 0, [own, *mine, others])
@@ -1007,24 +998,25 @@
     place = after(place, made[0])
     mixed1 = exchange(made, zones, 1, *mixed0)
 
-    feed0 = call_feed(place, 0, mixed0, None)
+    feed0 = call_feed(place, 0, mixed0, ())
     place = after(place, feed0[0])
     grads0 = exchange(feed0[:zones], zones, -1, *mixed1)
-    feed1 = call_feed(place, 1, mixed1, feed0[zones])
+    feed1 = call_feed(place, 1, mixed1, feed0[zones : zones + 5])
     place = after(place, feed1[0], *grads0)
-    acts, pres, norms, attends, up_sums, sums = zip(feed0[zones + 1 :], feed1[zones + 1 :])
-    cots = [part(cotangent, c).reshape(count * rows, depth) for c in range(2)]
+    act, pre, norm, attended = feed1[zones + 1 : zones + 5]
+    up_sums, sums = zip(feed0[zones + 5 :], feed1[zones + 5 :])
+    cot = cotangent.reshape(seq_count * rows, depth)
 
     weight_sum, rand_sum = Reduce(ranks), Reduce(ranks)
 
     def call_weights(place, odd):
         return weight_grads(
             place,
-            acts,
-            pres,
-            attends,
-            norms,
-            cots,
+            act,
+            pre,
+            attended,
+            norm,
+            cot,
             (mixed0, mixed1),
             heads,
             odd,
@@ -1064,7 +1056,7 @@
 
     rand_sum.first(rand[2:], *backs)
     grad_x, value_send, value_keep = input_grads(
-        place, backs, block_input, gain1, weight, attends, extra, heads, ranks
+        place, backs, block_input, gain1, weight, attended, extra, heads, ranks
     )
     sides = weight_sum.finish(*rand_sum.sent)
     terms = [side[d] for side in sides for d in range(zones // 2)]
@@ -1077,12 +1069,14 @@
     rand_sum.second(value_send, terms[far_apart])
     value_own = reduce_direct(value_send, value_keep, ranks, *rand_sum.went)
     tile, square = hidden // ranks // zones, depth // ranks
-    terms = lax.optimization_barrier((*terms, *rand_sum.last))[:zones]
+    value_blocks = [value_own[d].astype(F32 if d == 0 else BF16) for d in range(zones)]
+    value_blocks[1:] = [after(value, *terms[1:]) for value in value_blocks[1:]]
+    value_terms = spread_head(value_blocks, zones)
+    terms = lax.optimization_barrier((*terms, *value_blocks[1:]))[:zones]
     grad_up, grad_down, grad_out = feed_sums(terms, tile, square, zones)
-    value_terms = spread_head([value_own[d] for d in range(zones)], zones)
     grad_value, line = value_sums(value_terms, square, zones)
     line = line[0]
-    grad_rand = jnp.concatenate(rand_sum.finish(), 1)
+    grad_rand = jnp.concatenate(rand_sum.finish(*value_blocks[1:]), 1)
     return (
         feed1[zones],
         grad_x,
@@ -1091,7 +1085,7 @@
         grad_out,
         line[:gain_size],
         line[gain_size : 2 * gain_size],
-        grad_up,
+        grad_up.T,
         line[3 * gain_size : 3 * gain_size + up_size],
         grad_down,
         line[2 * gain_size : 3 * gain_size],

time: 317 us -> 309 us (0.975)
  starting transfers between devices: 67.1 us -> 63.3 us
    unnamed x105 -> x98, local copies, waits for them, and re-layouts: 7.02 us -> 3.12 us
  transfers between devices with their start and end apart: 48 -> 48, of which waited for: 16 -> 17; matrix products, arithmetic and copies ran while one was open for 8% -> 8% of each run, Pallas kernels for 43% -> 44%
where the time goes in v4:
time: 309 us; the launch traced here: 308 us
  Pallas kernels  135 us (44%)
  waiting for transfers between devices  64.9 us (21%)
  starting transfers between devices  63.3 us (20%)
  other arithmetic  19.4 us (6%)
  between operations  14.9 us (5%)
  local copies, waits for them, and re-layouts  9.97 us (3%)
    ppermute x30, starting transfers between devices, shift(): lax.ppermute(value, axis, [(i, (i + by) % extent) for i in range(extent)])  50.6 us
    pallas_call x2, Pallas kernels, feed(): pl.pallas_call(functools.partial(feed_kernel, zones, heads, size, steps,...  41 us
    ppermute x17, waiting for transfers between devices, flip(): return lax.ppermute(value, axis, [(i, i ^ mask) for i in range(extent)])  33.9 us
    ppermute x30, waiting for transfers between devices, shift(): lax.ppermute(value, axis, [(i, (i + by) % extent) for i in range(extent)])  31 us
    pallas_call x2, Pallas kernels, weight_grads(): pl.pallas_call(functools.partial(weights_kernel, zones, chunks, heads), g...  27.9 us
    pallas_call x1, Pallas kernels, logit_grads(): pl.pallas_call(functools.partial(logits_kernel, zones, chunks, count, hea...  18 us
    pallas_call x3, Pallas kernels, mix(): pl.pallas_call(functools.partial(mix_kernel, zones, chunks, count, lanes...  17 us
    pallas_call x1, Pallas kernels, make_probs(): pl.pallas_call(probs_kernel, grid=(heads, rows // SHORT), in_specs=[pl.Bl...  13.9 us
  transfers between devices with their start and end apart: 48, of which 17 were waited for; matrix products, arithmetic and copies ran while one was open for 8% of the time, Pallas kernels for 44%

profile of v4, /device:TPU:0, one launch (start us, length us, event | category | flops | bytes accessed | tf_op | source)
XLA Modules:
  0.0 307.9 jit_solution(400314174082428357)
XLA Ops:
  9.7 5.1 %collective-permute-start = (bf16[96,768]{1,0:T(8,128)(2,1)S(1)}, bf16[96,768]{1,0:T(8,128)(2,1)S(1)}, u32[]{:S(2)}, u32[]{:S(2)}) collective-permute-start(bf16[96,768]{1,0:T(8,128)(2,1)S(1)} %dynamic-slice_bitcast_fusion), channel_id=1, source_target_pairs={{0,3},{1,0},{2,1},{3,2},{4,7},{5,4},{6,5},{7,6},{8,11},{9,8},{10,9... | collective-permute-start | bytes 442376 | tf_op jit(solution)/shard_map/ppermute | solution.py:817
  15.9 13.9 %probs.1 = (bf16[3,1024,1024]{2,1,0:T(8,128)(2,1)}, bf16[3,1024,1024]{2,1,0:T(8,128)(2,1)}, bf16[3,256,256]{2,1,0:T(8,128)(2,1)S(1)}, bf16[3,256,256]{2,1,0:T(8,128)(2,1)S(1)}) custom-call(bf16[3,1024,1024]{2,1,0:T(8,128)(2,1)} %refs_16_.1), custom_call_target="tpu_custom_call" | custom-call | flops 31457280 | bytes 18874368 | tf_op jit(solution)/shard_map/probs/pallas_call | solution.py:109
  41.4 3.5 %collective-permute-done.4.refs_1_.refs_9_ = bf16[256,384]{1,0:T(8,128)(2,1)S(1)} collective-permute-done((bf16[256,384]{1,0:T(8,128)(2,1)S(1)}, bf16[256,384]{1,0:T(8,128)(2,1)S(1)}, u32[]{:S(2)}, u32[]{:S(2)}) %collective-permute-start.4) | collective-permute-done | bytes 196640 | tf_op jit(solution)/shard_map/ppermute | solution.py:817
  44.8 8.6 %collective-permute-done.5.refs_2_.refs_10_ = bf16[256,384]{1,0:T(8,128)(2,1)S(1)} collective-permute-done((bf16[256,384]{1,0:T(8,128)(2,1)S(1)}, bf16[256,384]{1,0:T(8,128)(2,1)S(1)}, u32[]{:S(2)}, u32[]{:S(2)}) %collective-permute-start.5) | collective-permute-done | bytes 196640 | tf_op jit(solution)/shard_map/ppermute | solution.py:817
  53.5 4.9 %collective-permute-start.7 = (bf16[256,384]{1,0:T(8,128)(2,1)S(1)}, bf16[256,384]{1,0:T(8,128)(2,1)S(1)}, u32[]{:S(2)}, u32[]{:S(2)}) collective-permute-start(bf16[256,384]{1,0:T(8,128)(2,1)S(1)} %get-tuple-element.147), channel_id=1, source_target_pairs={{0,1},{1,2},{2,3},{3,0},{4,5},{5,6},{6,7},{7,4},{8,9},{9,10},{10,1... | collective-permute-start | bytes 589832 | tf_op jit(solution)/shard_map/ppermute | solution.py:817
  60.8 5.7 %mix.3 = (bf16[256,384]{1,0:T(8,128)(2,1)S(1)}, bf16[256,384]{1,0:T(8,128)(2,1)S(1)}, bf16[256,384]{1,0:T(8,128)(2,1)S(1)}, bf16[256,384]{1,0:T(8,128)(2,1)S(1)}) custom-call(s32[2]{0:T(128)S(1)} %pad_add_fusion.place_ref, s32[2]{0:T(128)S(1)} %get-tuple-element.269.long_flags, bf16[256,384]{1,0:T(8,128)(2,1)S(1)} %get-tuple-element.137.refs_0_.refs_8_, ...), custom_call_target="tpu_custom_call" | custom-call | flops 805306368 | bytes 7864320 | tf_op jit(solution)/shard_map/mix/pallas_call | solution.py:213
  66.6 8.3 %collective-permute-done.8.refs_2_.refs_14_ = bf16[256,384]{1,0:T(8,128)(2,1)S(1)} collective-permute-done((bf16[256,384]{1,0:T(8,128)(2,1)S(1)}, bf16[256,384]{1,0:T(8,128)(2,1)S(1)}, u32[]{:S(2)}, u32[]{:S(2)}) %collective-permute-start.8) | collective-permute-done | bytes 196640 | tf_op jit(solution)/shard_map/ppermute | solution.py:817
  74.9 5.4 %collective-permute-start.10 = (bf16[256,384]{1,0:T(8,128)(2,1)S(1)}, bf16[256,384]{1,0:T(8,128)(2,1)S(1)}, u32[]{:S(2)}, u32[]{:S(2)}) collective-permute-start(bf16[256,384]{1,0:T(8,128)(2,1)S(1)} %get-tuple-element.155), channel_id=1, source_target_pairs={{0,1},{1,2},{2,3},{3,0},{4,5},{5,6},{6,7},{7,4},{8,9},{9,10},{10,1... | collective-permute-start | bytes 589832 | tf_op jit(solution)/shard_map/ppermute | solution.py:817
  84.1 5.5 %mix.4 = (bf16[256,384]{1,0:T(8,128)(2,1)S(1)}, bf16[256,384]{1,0:T(8,128)(2,1)S(1)}, bf16[256,384]{1,0:T(8,128)(2,1)S(1)}, bf16[256,384]{1,0:T(8,128)(2,1)S(1)}) custom-call(s32[2]{0:T(128)S(1)} %pad_add_fusion.place_ref, s32[2]{0:T(128)S(1)} %get-tuple-element.268.long_flags, bf16[256,384]{1,0:T(8,128)(2,1)S(1)} %get-tuple-element.135.refs_0_.refs_12_, ...), custom_call_target="tpu_custom_call" | custom-call | flops 805306368 | bytes 7864320 | tf_op jit(solution)/shard_map/mix/pallas_call | solution.py:213
  90.3 4.7 %collective-permute-done.11.refs_2_.refs_7_ = bf16[256,384]{1,0:T(8,128)(2,1)S(1)} collective-permute-done((bf16[256,384]{1,0:T(8,128)(2,1)S(1)}, bf16[256,384]{1,0:T(8,128)(2,1)S(1)}, u32[]{:S(2)}, u32[]{:S(2)}) %collective-permute-start.11) | collective-permute-done | bytes 196640 | tf_op jit(solution)/shard_map/ppermute | solution.py:817
  95.0 4.7 %collective-permute-start.13 = (bf16[256,384]{1,0:T(8,128)(2,1)S(1)}, bf16[256,384]{1,0:T(8,128)(2,1)S(1)}, u32[]{:S(2)}, u32[]{:S(2)}) collective-permute-start(bf16[256,384]{1,0:T(8,128)(2,1)S(1)} %get-tuple-element.163), channel_id=1, source_target_pairs={{0,1},{1,2},{2,3},{3,0},{4,5},{5,6},{6,7},{7,4},{8,9},{9,10},{10,1... | collective-permute-start | bytes 589832 | tf_op jit(solution)/shard_map/ppermute | solution.py:817
  102.1 20.5 %feed.2 = (bf16[256,384]{1,0:T(8,128)(2,1)S(1)}, bf16[256,384]{1,0:T(8,128)(2,1)S(1)}, bf16[256,384]{1,0:T(8,128)(2,1)S(1)}, bf16[256,384]{1,0:T(8,128)(2,1)S(1)...) custom-call(s32[2]{0:T(128)S(1)} %pad_add_fusion.place_ref, ...), custom_call_target="tpu_custom_call" | custom-call | flops 10871635968 | bytes 23592960 | tf_op jit(solution)/shard_map/feed/pallas_call | solution.py:351
  125.4 20.5 %feed.3 = (bf16[256,384]{1,0:T(8,128)(2,1)S(1)}, bf16[256,384]{1,0:T(8,128)(2,1)S(1)}, bf16[256,384]{1,0:T(8,128)(2,1)S(1)}, bf16[256,384]{1,0:T(8,128)(2,1)S(1)...) custom-call(s32[2]{0:T(128)S(1)} %pad_add_fusion.place_ref, ...), custom_call_target="tpu_custom_call", output_to_operand_aliasing={{4}: (13, {}), {5}: (14, {}), {6}: (15, {}), {7}: (16, {}),... | custom-call | flops 10871635968 | bytes 23592960 | tf_op jit(solution)/shard_map/feed/pallas_call | solution.py:351
  146.0 3.6 %collective-permute-start.19 = (bf16[256,384]{1,0:T(8,128)(2,1)S(1)}, bf16[256,384]{1,0:T(8,128)(2,1)S(1)}, u32[]{:S(2)}, u32[]{:S(2)}) collective-permute-start(bf16[256,384]{1,0:T(8,128)(2,1)S(1)} %get-tuple-element.188), channel_id=1, source_target_pairs={{0,3},{1,0},{2,1},{3,2},{4,7},{5,4},{6,5},{7,6},{8,11},{9,8},{10,9... | collective-permute-start | bytes 589832 | tf_op jit(solution)/shard_map/ppermute | solution.py:817
  150.4 13.9 %weights.2 = (bf16[4,2,224,768]{3,2,1,0:T(8,128)(2,1)}, bf16[4,2,224,768]{3,2,1,0:T(8,128)(2,1)}) custom-call(s32[2]{0:T(128)S(1)} %pad_add_fusion.place_ref, bf16[3072,1024]{1,0:T(8,128)(2,1)} %get-tuple-element.180.refs_0_, bf16[3072,1024]{1,0:T(8,128)(2,1)} %get-tuple-element.181.refs_1_, bf16[768,1024]{1,0:T(8,128)(2,1)} %get-tuple-element.182.refs_2_.refs_8_, ...), custom_call_target="tpu_custom_call" | custom-call | flops 4831838208 | bytes 14155776 | tf_op jit(solution)/shard_map/weights/pallas_call | solution.py:500
  166.7 5.8 %mix.5 = (bf16[256,768]{1,0:T(8,128)(2,1)S(1)}, bf16[256,768]{1,0:T(8,128)(2,1)S(1)}, bf16[256,768]{1,0:T(8,128)(2,1)S(1)}, bf16[256,768]{1,0:T(8,128)(2,1)S(1)}) custom-call(s32[2]{0:T(128)S(1)} %pad_add_fusion.place_ref, s32[4]{0:T(128)S(1)} %copy-done.23, bf16[256,384]{1,0:T(8,128)(2,1)S(1)} %get-tuple-element.158.refs_0_, ...), custom_call_target="tpu_custom_call" | custom-call | flops 1610612736 | bytes 9437184 | tf_op jit(solution)/shard_map/mix/pallas_call | solution.py:213
  174.8 13.9 %weights.3 = (bf16[4,2,224,768]{3,2,1,0:T(8,128)(2,1)}, bf16[4,2,224,768]{3,2,1,0:T(8,128)(2,1)}) custom-call(s32[2]{0:T(128)S(1)} %pad_add_fusion.place_ref, bf16[3072,1024]{1,0:T(8,128)(2,1)} %get-tuple-element.180.refs_0_, bf16[3072,1024]{1,0:T(8,128)(2,1)} %get-tuple-element.181.refs_1_, bf16[768,1024]{1,0:T(8,128)(2,1)} %get-tuple-element.182.refs_2_.refs_8_, ...), custom_call_target="tpu_custom_call" | custom-call | flops 4831838208 | bytes 14155776 | tf_op jit(solution)/shard_map/weights/pallas_call | solution.py:500
  188.8 3.5 %add_convert_fusion = (bf16[2,2,224,768]{3,2,1,0:T(8,128)(2,1)S(1)}, bf16[2,2,224,768]{3,2,1,0:T(8,128)(2,1)S(1)}) fusion(bf16[4,2,224,768]{3,2,1,0:T(8,128)(2,1)S(1)} %collective-permute-done.24, bf16[4,2,224,768]{3,2,1,0:T(8,128)(2,1)} %get-tuple-element.204, bf16[4,2,224,768]{3,2,1,0:T(8,128)(2,1)S(1)} %collective-permute-done.23, ...), kind=kLoop, calls=%fused_computation | loop fusion | flops 5505024 | bytes 8257536 | tf_op jit(solution)/shard_map/convert_element_type | solution.py:860
  199.0 18.0 %logits.1 = (bf16[4,3,64,1024]{3,2,1,0:T(8,128)(2,1)}, bf16[4,3,64,1024]{3,2,1,0:T(8,128)(2,1)}, bf16[4,3,64,1024]{3,2,1,0:T(8,128)(2,1)}, bf16[4,3,64,1024]{3,2,1,0:T(8,128)(2,1)}) custom-call(s32[2]{0:T(128)S(1)} %pad_add_fusion.place_ref, s32[4]{0:T(128)S(1)} %copy-done.23, bf16[256,384]{1,0:T(8,128)(2,1)} %copy-done.14, bf16[256,384]{1,0:T(8,128)(2,1)} %copy-done.15, ...), custom_call_target="tpu_custom_call" | custom-call | flops 1610612736 | bytes 12582912 | tf_op jit(solution)/shard_map/logits/pallas_call | solution.py:642
  217.1 8.4 %collective-permute-done.26 = bf16[2,2,224,768]{3,2,1,0:T(8,128)(2,1)} collective-permute-done((bf16[2,2,224,768]{3,2,1,0:T(8,128)(2,1)S(1)}, bf16[2,2,224,768]{3,2,1,0:T(8,128)(2,1)}, u32[]{:S(2)}, u32[]{:S(2)}) %collective-permute-start.26) | collective-permute-done | bytes 1376288 | tf_op jit(solution)/shard_map/ppermute | solution.py:821
  238.7 9.6 %collective-permute-done.33 = bf16[1,2,224,768]{3,2,1,0:T(8,128)(2,1)S(1)} collective-permute-done((bf16[1,2,224,768]{3,2,1,0:T(8,128)(2,1)S(1)}, bf16[1,2,224,768]{3,2,1,0:T(8,128)(2,1)S(1)}, u32[]{:S(2)}, u32[]{:S(2)}) %collective-permute-start.33) | collective-permute-done | bytes 688160 | tf_op jit(solution)/shard_map/ppermute | solution.py:821
  253.6 10.0 %input.1 = (bf16[4,256,768]{2,1,0:T(8,128)(2,1)}, bf16[4,4,32,768]{3,2,1,0:T(8,128)(2,1)S(1)}, bf16[4,4,32,768]{3,2,1,0:T(8,128)(2,1)S(1)}) custom-call(s32[2]{0:T(128)S(1)} %pad_add_fusion.place_ref, bf16[256,768]{1,0:T(8,128)(2,1)} %copy-done.24, bf16[256,768]{1,0:T(8,128)(2,1)} %copy-done.47, bf16[256,768]{1,0:T(8,128)(2,1)} %copy-done.46, ...), custom_call_target="tpu_custom_call" | custom-call | flops 2415919104 | bytes 14155776 | tf_op jit(solution)/shard_map/input/pallas_call | solution.py:718
  277.5 3.0 collective-permute-done.39
  281.2 3.6 %collective-permute-done.40 = bf16[1,4,32,768]{3,2,1,0:T(8,128)(2,1)S(1)} collective-permute-done((bf16[1,4,32,768]{3,2,1,0:T(8,128)(2,1)S(1)}, bf16[1,4,32,768]{3,2,1,0:T(8,128)(2,1)S(1)}, u32[]{:S(2)}, u32[]{:S(2)}) %collective-permute-start.40) | collective-permute-done | bytes 196640 | tf_op jit(solution)/shard_map/ppermute | solution.py:821
  (226 shorter events, 88.2 us)
Async XLA Ops:
  7.2 94.9 %all-gather.2.cloned.1.call-start = ((), (), s32[]{:S(2)}) async-start(), calls=%async_computation | async-start | bytes 1216512 | tf_op jit(solution)/shard_map/all_gather | solution.py:951
  9.7 20.0 %collective-permute-start = (bf16[96,768]{1,0:T(8,128)(2,1)S(1)}, bf16[96,768]{1,0:T(8,128)(2,1)S(1)}, u32[]{:S(2)}, u32[]{:S(2)}) collective-permute-start(bf16[96,768]{1,0:T(8,128)(2,1)S(1)} %dynamic-slice_bitcast_fusion), channel_id=1, source_target_pairs={{0,3},{1,0},{2,1},{3,2},{4,7},{5,4},{6,5},{7,6},{8,11},{9,8},{10,9... | collective-permute-start | bytes 442376 | tf_op jit(solution)/shard_map/ppermute | solution.py:817
  37.2 16.3 %collective-permute-start.5 = (bf16[256,384]{1,0:T(8,128)(2,1)S(1)}, bf16[256,384]{1,0:T(8,128)(2,1)S(1)}, u32[]{:S(2)}, u32[]{:S(2)}) collective-permute-start(bf16[256,384]{1,0:T(8,128)(2,1)S(1)} %get-tuple-element.139), channel_id=1, source_target_pairs={{0,2},{1,3},{2,0},{3,1},{4,6},{5,7},{6,4},{7,5},{8,10},{9,11},{10,... | collective-permute-start | bytes 589832 | tf_op jit(solution)/shard_map/ppermute | solution.py:817
  58.4 16.5 %collective-permute-start.8 = (bf16[256,384]{1,0:T(8,128)(2,1)S(1)}, bf16[256,384]{1,0:T(8,128)(2,1)S(1)}, u32[]{:S(2)}, u32[]{:S(2)}) collective-permute-start(bf16[256,384]{1,0:T(8,128)(2,1)S(1)} %get-tuple-element.148), channel_id=1, source_target_pairs={{0,2},{1,3},{2,0},{3,1},{4,6},{5,7},{6,4},{7,5},{8,10},{9,11},{10,... | collective-permute-start | bytes 589832 | tf_op jit(solution)/shard_map/ppermute | solution.py:817
  95.0 27.6 %collective-permute-start.13 = (bf16[256,384]{1,0:T(8,128)(2,1)S(1)}, bf16[256,384]{1,0:T(8,128)(2,1)S(1)}, u32[]{:S(2)}, u32[]{:S(2)}) collective-permute-start(bf16[256,384]{1,0:T(8,128)(2,1)S(1)} %get-tuple-element.163), channel_id=1, source_target_pairs={{0,1},{1,2},{2,3},{3,0},{4,5},{5,6},{6,7},{7,4},{8,9},{9,10},{10,1... | collective-permute-start | bytes 589832 | tf_op jit(solution)/shard_map/ppermute | solution.py:817
  99.7 22.9 %collective-permute-start.14 = (bf16[256,384]{1,0:T(8,128)(2,1)S(1)}, bf16[256,384]{1,0:T(8,128)(2,1)S(1)}, u32[]{:S(2)}, u32[]{:S(2)}) collective-permute-start(bf16[256,384]{1,0:T(8,128)(2,1)S(1)} %get-tuple-element.164), channel_id=1, source_target_pairs={{0,2},{1,3},{2,0},{3,1},{4,6},{5,7},{6,4},{7,5},{8,10},{9,11},{10,... | collective-permute-start | bytes 589832 | tf_op jit(solution)/shard_map/ppermute | solution.py:817
  101.0 21.6 %collective-permute-start.15 = (bf16[256,384]{1,0:T(8,128)(2,1)S(1)}, bf16[256,384]{1,0:T(8,128)(2,1)S(1)}, u32[]{:S(2)}, u32[]{:S(2)}) collective-permute-start(bf16[256,384]{1,0:T(8,128)(2,1)S(1)} %get-tuple-element.165), channel_id=1, source_target_pairs={{0,3},{1,0},{2,1},{3,2},{4,7},{5,4},{6,5},{7,6},{8,11},{9,8},{10,9... | collective-permute-start | bytes 589832 | tf_op jit(solution)/shard_map/ppermute | solution.py:817
  122.7 23.3 %collective-permute-start.16 = (bf16[256,384]{1,0:T(8,128)(2,1)S(1)}, bf16[256,384]{1,0:T(8,128)(2,1)S(1)}, u32[]{:S(2)}, u32[]{:S(2)}) collective-permute-start(bf16[256,384]{1,0:T(8,128)(2,1)S(1)} %get-tuple-element.176), channel_id=1, source_target_pairs={{0,3},{1,0},{2,1},{3,2},{4,7},{5,4},{6,5},{7,6},{8,11},{9,8},{10,9... | collective-permute-start | bytes 589832 | tf_op jit(solution)/shard_map/ppermute | solution.py:817
  124.7 21.2 %collective-permute-start.17 = (bf16[256,384]{1,0:T(8,128)(2,1)S(1)}, bf16[256,384]{1,0:T(8,128)(2,1)S(1)}, u32[]{:S(2)}, u32[]{:S(2)}) collective-permute-start(bf16[256,384]{1,0:T(8,128)(2,1)S(1)} %get-tuple-element.177), channel_id=1, source_target_pairs={{0,2},{1,3},{2,0},{3,1},{4,6},{5,7},{6,4},{7,5},{8,10},{9,11},{10,... | collective-permute-start | bytes 589832 | tf_op jit(solution)/shard_map/ppermute | solution.py:817
  125.1 20.8 %collective-permute-start.18 = (bf16[256,384]{1,0:T(8,128)(2,1)S(1)}, bf16[256,384]{1,0:T(8,128)(2,1)S(1)}, u32[]{:S(2)}, u32[]{:S(2)}) collective-permute-start(bf16[256,384]{1,0:T(8,128)(2,1)S(1)} %get-tuple-element.178), channel_id=1, source_target_pairs={{0,1},{1,2},{2,3},{3,0},{4,5},{5,6},{6,7},{7,4},{8,9},{9,10},{10,1... | collective-permute-start | bytes 589832 | tf_op jit(solution)/shard_map/ppermute | solution.py:817
  146.0 18.3 %collective-permute-start.19 = (bf16[256,384]{1,0:T(8,128)(2,1)S(1)}, bf16[256,384]{1,0:T(8,128)(2,1)S(1)}, u32[]{:S(2)}, u32[]{:S(2)}) collective-permute-start(bf16[256,384]{1,0:T(8,128)(2,1)S(1)} %get-tuple-element.188), channel_id=1, source_target_pairs={{0,3},{1,0},{2,1},{3,2},{4,7},{5,4},{6,5},{7,6},{8,11},{9,8},{10,9... | collective-permute-start | bytes 589832 | tf_op jit(solution)/shard_map/ppermute | solution.py:817
  149.6 16.5 %collective-permute-start.20 = (bf16[256,384]{1,0:T(8,128)(2,1)S(1)}, bf16[256,384]{1,0:T(8,128)(2,1)S(1)}, u32[]{:S(2)}, u32[]{:S(2)}) collective-permute-start(bf16[256,384]{1,0:T(8,128)(2,1)S(1)} %get-tuple-element.189), channel_id=1, source_target_pairs={{0,2},{1,3},{2,0},{3,1},{4,6},{5,7},{6,4},{7,5},{8,10},{9,11},{10,... | collective-permute-start | bytes 589832 | tf_op jit(solution)/shard_map/ppermute | solution.py:817
  166.1 22.6 %collective-permute-start.24 = (bf16[4,2,224,768]{3,2,1,0:T(8,128)(2,1)}, bf16[4,2,224,768]{3,2,1,0:T(8,128)(2,1)S(1)}, u32[]{:S(2)}, u32[]{:S(2)}) collective-permute-start(bf16[4,2,224,768]{3,2,1,0:T(8,128)(2,1)} %get-tuple-element.200), channel_id=1, source_target_pairs={{0,4},{4,0},{8,12},{12,8},{16,20},{20,16},{24,28},{28,24},{1,5},{5... | collective-permute-start | bytes 8257544 | tf_op jit(solution)/shard_map/ppermute | solution.py:821
  166.2 22.6 %collective-permute-start.23 = (bf16[4,2,224,768]{3,2,1,0:T(8,128)(2,1)}, bf16[4,2,224,768]{3,2,1,0:T(8,128)(2,1)S(1)}, u32[]{:S(2)}, u32[]{:S(2)}) collective-permute-start(bf16[4,2,224,768]{3,2,1,0:T(8,128)(2,1)} %get-tuple-element.198), channel_id=1, source_target_pairs={{0,4},{4,0},{8,12},{12,8},{16,20},{20,16},{24,28},{28,24},{1,5},{5... | collective-permute-start | bytes 8257544 | tf_op jit(solution)/shard_map/ppermute | solution.py:821
  173.3 20.4 %collective-permute-start.22 = (bf16[256,768]{1,0:T(8,128)(2,1)S(1)}, bf16[256,768]{1,0:T(8,128)(2,1)S(1)}, u32[]{:S(2)}, u32[]{:S(2)}) collective-permute-start(bf16[256,768]{1,0:T(8,128)(2,1)S(1)} %get-tuple-element.197), channel_id=1, source_target_pairs={{0,2},{1,3},{2,0},{3,1},{4,6},{5,7},{6,4},{7,5},{8,10},{9,11},{10,... | collective-permute-start | bytes 1179656 | tf_op jit(solution)/shard_map/ppermute | solution.py:817
  193.7 31.8 %collective-permute-start.26 = (bf16[2,2,224,768]{3,2,1,0:T(8,128)(2,1)S(1)}, bf16[2,2,224,768]{3,2,1,0:T(8,128)(2,1)}, u32[]{:S(2)}, u32[]{:S(2)}) collective-permute-start(bf16[2,2,224,768]{3,2,1,0:T(8,128)(2,1)S(1)} %get-tuple-element.205), channel_id=1, source_target_pairs={{0,16},{4,20},{8,24},{12,28},{16,0},{20,4},{24,8},{28,12},{1,17},{... | collective-permute-start | bytes 4128776 | tf_op jit(solution)/shard_map/ppermute | solution.py:821
  195.3 31.4 %collective-permute-start.25 = (bf16[2,2,224,768]{3,2,1,0:T(8,128)(2,1)S(1)}, bf16[2,2,224,768]{3,2,1,0:T(8,128)(2,1)S(1)}, u32[]{:S(2)}, u32[]{:S(2)}) collective-permute-start(bf16[2,2,224,768]{3,2,1,0:T(8,128)(2,1)S(1)} %get-tuple-element.203), channel_id=1, source_target_pairs={{0,8},{4,12},{8,0},{12,4},{16,24},{20,28},{24,16},{28,20},{1,9},{5... | collective-permute-start | bytes 4128776 | tf_op jit(solution)/shard_map/ppermute | solution.py:821
  196.8 20.3 %collective-permute-start.27 = (bf16[256,768]{1,0:T(8,128)(2,1)S(1)}, bf16[256,768]{1,0:T(8,128)(2,1)S(1)}, u32[]{:S(2)}, u32[]{:S(2)}) collective-permute-start(bf16[256,768]{1,0:T(8,128)(2,1)S(1)} %get-tuple-element.208), channel_id=1, source_target_pairs={{0,3},{1,0},{2,1},{3,2},{4,7},{5,4},{6,5},{7,6},{8,11},{9,8},{10,9... | collective-permute-start | bytes 1179656 | tf_op jit(solution)/shard_map/ppermute | solution.py:817
  199.0 18.1 %collective-permute-start.28 = (bf16[256,768]{1,0:T(8,128)(2,1)S(1)}, bf16[256,768]{1,0:T(8,128)(2,1)S(1)}, u32[]{:S(2)}, u32[]{:S(2)}) collective-permute-start(bf16[256,768]{1,0:T(8,128)(2,1)S(1)} %get-tuple-element.209), channel_id=1, source_target_pairs={{0,1},{1,2},{2,3},{3,0},{4,5},{5,6},{6,7},{7,4},{8,9},{9,10},{10,1... | collective-permute-start | bytes 1179656 | tf_op jit(solution)/shard_map/ppermute | solution.py:817
  229.8 18.4 %collective-permute-start.33 = (bf16[1,2,224,768]{3,2,1,0:T(8,128)(2,1)S(1)}, bf16[1,2,224,768]{3,2,1,0:T(8,128)(2,1)S(1)}, u32[]{:S(2)}, u32[]{:S(2)}) collective-permute-start(bf16[1,2,224,768]{3,2,1,0:T(8,128)(2,1)S(1)} %add_convert_fusion.5), channel_id=1, source_target_pairs={{0,8},{4,12},{8,0},{12,4},{16,24},{20,28},{24,16},{28,20},{1,9},{5... | collective-permute-start | bytes 2064392 | tf_op jit(solution)/shard_map/ppermute | solution.py:821
  232.8 18.4 %collective-permute-start.32 = (bf16[1,2,224,768]{3,2,1,0:T(8,128)(2,1)S(1)}, bf16[1,2,224,768]{3,2,1,0:T(8,128)(2,1)S(1)}, u32[]{:S(2)}, u32[]{:S(2)}) collective-permute-start(bf16[1,2,224,768]{3,2,1,0:T(8,128)(2,1)S(1)} %add_convert_fusion.6), channel_id=1, source_target_pairs={{0,16},{4,20},{8,24},{12,28},{16,0},{20,4},{24,8},{28,12},{1,17},{... | collective-permute-start | bytes 2064392 | tf_op jit(solution)/shard_map/ppermute | solution.py:821
  236.6 29.7 %collective-permute-start.36 = (bf16[2,3,64,1024]{3,2,1,0:T(8,128)(2,1)S(1)}, bf16[2,3,64,1024]{3,2,1,0:T(8,128)(2,1)S(1)}, u32[]{:S(2)}, u32[]{:S(2)}) collective-permute-start(bf16[2,3,64,1024]{3,2,1,0:T(8,128)(2,1)S(1)} %add_convert_fusion.2), channel_id=1, source_target_pairs={{0,16},{4,20},{8,24},{12,28},{16,0},{20,4},{24,8},{28,12},{1,17},{... | collective-permute-start | bytes 2359304 | tf_op jit(solution)/shard_map/ppermute | solution.py:821
  238.0 28.2 %collective-permute-start.31 = (bf16[2,3,64,1024]{3,2,1,0:T(8,128)(2,1)S(1)}, bf16[2,3,64,1024]{3,2,1,0:T(8,128)(2,1)S(1)}, u32[]{:S(2)}, u32[]{:S(2)}) collective-permute-start(bf16[2,3,64,1024]{3,2,1,0:T(8,128)(2,1)S(1)} %add_convert_fusion.3), channel_id=1, source_target_pairs={{0,8},{4,12},{8,0},{12,4},{16,24},{20,28},{24,16},{28,20},{1,9},{5... | collective-permute-start | bytes 2359304 | tf_op jit(solution)/shard_map/ppermute | solution.py:821
  268.6 16.3 %collective-permute-start.43 = (bf16[224,768]{1,0:T(8,128)(2,1)S(1)}, bf16[224,768]{1,0:T(8,128)(2,1)S(1)}, u32[]{:S(2)}, u32[]{:S(2)}) collective-permute-start(bf16[224,768]{1,0:T(8,128)(2,1)S(1)} %get-tuple-element.234), channel_id=1, source_target_pairs={{0,3},{1,0},{2,1},{3,2},{4,7},{5,4},{6,5},{7,6},{8,11},{9,8},{10,9... | collective-permute-start | bytes 1032200 | tf_op jit(solution)/shard_map/ppermute | solution.py:817
  (73 other events, 890.2 us)
Sparse Core Ops, SparseCore 0:
  11.5 67.8 all-gather.1

commit v5 on v4

--- a/solution.py
+++ b/solution.py
@@ -993,7 +993,8 @@
 
     made = mix(place, part(lengths, 0), [values0], probs, corner, count, 1)
     place = after(place, made[0])
-    mixed0 = exchange(made, zones, 1, *values1)
+    mixed0 = [made[0]] + exchange_some(made, range(1, zones - 1), zones, 1)
+    mixed0 += exchange_some(made, (zones - 1,), zones, 1, *values1)
     made = mix(place, part(lengths, 1), [values1], probs, corner, count, 1)
     place = after(place, made[0])
     mixed1 = exchange(made, zones, 1, *mixed0)

time: 309 us -> 306 us (level)
  starting transfers between devices: 63.3 us -> 54.9 us
  waiting for transfers between devices: 64.9 us -> 70.2 us
    ppermute x30, starting transfers between devices: 50.6 us -> 42.2 us  [shift(): lax.ppermute(value, axis, [(i, (i + by) % extent) for i in range(extent)])]
    ppermute x30, waiting for transfers between devices: 31 us -> 36.5 us  [shift(): lax.ppermute(value, axis, [(i, (i + by) % extent) for i in range(extent)])]
  transfers between devices with their start and end apart: 48 -> 48, of which waited for: 17 -> 19; matrix products, arithmetic and copies ran while one was open for 8% -> 8% of each run, Pallas kernels for 44% -> 44%
where the time goes in v5:
time: 306 us; the launch traced here: 305 us
  Pallas kernels  135 us (44%)
  waiting for transfers between devices  70.2 us (23%)
  starting transfers between devices  54.9 us (18%)
  other arithmetic  19.4 us (6%)
  between operations  14.9 us (5%)
  local copies, waits for them, and re-layouts  9.97 us (3%)
    ppermute x30, starting transfers between devices, shift(): lax.ppermute(value, axis, [(i, (i + by) % extent) for i in range(extent)])  42.2 us
    pallas_call x2, Pallas kernels, feed(): pl.pallas_call(functools.partial(feed_kernel, zones, heads, size, steps,...  41 us
    ppermute x30, waiting for transfers between devices, shift(): lax.ppermute(value, axis, [(i, (i + by) % extent) for i in range(extent)])  36.5 us
    ppermute x17, waiting for transfers between devices, flip(): return lax.ppermute(value, axis, [(i, i ^ mask) for i in range(extent)])  33.7 us
    pallas_call x2, Pallas kernels, weight_grads(): pl.pallas_call(functools.partial(weights_kernel, zones, chunks, heads), g...  27.9 us
    pallas_call x1, Pallas kernels, logit_grads(): pl.pallas_call(functools.partial(logits_kernel, zones, chunks, count, hea...  18 us
    pallas_call x3, Pallas kernels, mix(): pl.pallas_call(functools.partial(mix_kernel, zones, chunks, count, lanes...  17 us
    pallas_call x1, Pallas kernels, make_probs(): pl.pallas_call(probs_kernel, grid=(heads, rows // SHORT), in_specs=[pl.Bl...  13.9 us
  transfers between devices with their start and end apart: 48, of which 19 were waited for; matrix products, arithmetic and copies ran while one was open for 8% of the time, Pallas kernels for 44%

profile of v5, /device:TPU:0, one launch (start us, length us, event | category | flops | bytes accessed | tf_op | source)
XLA Modules:
  0.0 304.8 jit_solution(5828898359259715757)
XLA Ops:
  9.7 5.1 %collective-permute-start = (bf16[96,768]{1,0:T(8,128)(2,1)S(1)}, bf16[96,768]{1,0:T(8,128)(2,1)S(1)}, u32[]{:S(2)}, u32[]{:S(2)}) collective-permute-start(bf16[96,768]{1,0:T(8,128)(2,1)S(1)} %dynamic-slice_bitcast_fusion), channel_id=1, source_target_pairs={{0,3},{1,0},{2,1},{3,2},{4,7},{5,4},{6,5},{7,6},{8,11},{9,8},{10,9... | collective-permute-start | bytes 442376 | tf_op jit(solution)/shard_map/ppermute | solution.py:817
  15.9 13.9 %probs.1 = (bf16[3,1024,1024]{2,1,0:T(8,128)(2,1)}, bf16[3,1024,1024]{2,1,0:T(8,128)(2,1)}, bf16[3,256,256]{2,1,0:T(8,128)(2,1)S(1)}, bf16[3,256,256]{2,1,0:T(8,128)(2,1)S(1)}) custom-call(bf16[3,1024,1024]{2,1,0:T(8,128)(2,1)} %refs_16_.1), custom_call_target="tpu_custom_call" | custom-call | flops 31457280 | bytes 18874368 | tf_op jit(solution)/shard_map/probs/pallas_call | solution.py:109
  31.8 2.8 values.2
  34.6 2.5 collective-permute-start.4
  41.4 3.5 %collective-permute-done.4.refs_1_.refs_9_ = bf16[256,384]{1,0:T(8,128)(2,1)S(1)} collective-permute-done((bf16[256,384]{1,0:T(8,128)(2,1)S(1)}, bf16[256,384]{1,0:T(8,128)(2,1)S(1)}, u32[]{:S(2)}, u32[]{:S(2)}) %collective-permute-start.4) | collective-permute-done | bytes 196640 | tf_op jit(solution)/shard_map/ppermute | solution.py:817
  44.8 8.6 %collective-permute-done.5.refs_2_.refs_10_ = bf16[256,384]{1,0:T(8,128)(2,1)S(1)} collective-permute-done((bf16[256,384]{1,0:T(8,128)(2,1)S(1)}, bf16[256,384]{1,0:T(8,128)(2,1)S(1)}, u32[]{:S(2)}, u32[]{:S(2)}) %collective-permute-start.5) | collective-permute-done | bytes 196640 | tf_op jit(solution)/shard_map/ppermute | solution.py:817
  53.5 4.9 %collective-permute-start.7 = (bf16[256,384]{1,0:T(8,128)(2,1)S(1)}, bf16[256,384]{1,0:T(8,128)(2,1)S(1)}, u32[]{:S(2)}, u32[]{:S(2)}) collective-permute-start(bf16[256,384]{1,0:T(8,128)(2,1)S(1)} %get-tuple-element.145), channel_id=1, source_target_pairs={{0,1},{1,2},{2,3},{3,0},{4,5},{5,6},{6,7},{7,4},{8,9},{9,10},{10,1... | collective-permute-start | bytes 589832 | tf_op jit(solution)/shard_map/ppermute | solution.py:817
  60.8 5.7 %mix.3 = (bf16[256,384]{1,0:T(8,128)(2,1)S(1)}, bf16[256,384]{1,0:T(8,128)(2,1)S(1)}, bf16[256,384]{1,0:T(8,128)(2,1)S(1)}, bf16[256,384]{1,0:T(8,128)(2,1)S(1)}) custom-call(s32[2]{0:T(128)S(1)} %pad_add_fusion.place_ref, s32[2]{0:T(128)S(1)} %get-tuple-element.265.long_flags, bf16[256,384]{1,0:T(8,128)(2,1)S(1)} %get-tuple-element.135.refs_0_.refs_8_, ...), custom_call_target="tpu_custom_call" | custom-call | flops 805306368 | bytes 7864320 | tf_op jit(solution)/shard_map/mix/pallas_call | solution.py:213
  69.0 15.0 %collective-permute-done.8.refs_2_.refs_14_ = bf16[256,384]{1,0:T(8,128)(2,1)S(1)} collective-permute-done((bf16[256,384]{1,0:T(8,128)(2,1)S(1)}, bf16[256,384]{1,0:T(8,128)(2,1)S(1)}, u32[]{:S(2)}, u32[]{:S(2)}) %collective-permute-start.8) | collective-permute-done | bytes 196640 | tf_op jit(solution)/shard_map/ppermute | solution.py:817
  85.5 5.5 %mix.4 = (bf16[256,384]{1,0:T(8,128)(2,1)S(1)}, bf16[256,384]{1,0:T(8,128)(2,1)S(1)}, bf16[256,384]{1,0:T(8,128)(2,1)S(1)}, bf16[256,384]{1,0:T(8,128)(2,1)S(1)}) custom-call(s32[2]{0:T(128)S(1)} %pad_add_fusion.place_ref, s32[2]{0:T(128)S(1)} %get-tuple-element.264.long_flags, bf16[256,384]{1,0:T(8,128)(2,1)S(1)} %get-tuple-element.133.refs_0_.refs_12_, ...), custom_call_target="tpu_custom_call" | custom-call | flops 805306368 | bytes 7864320 | tf_op jit(solution)/shard_map/mix/pallas_call | solution.py:213
  92.5 4.1 %collective-permute-done.12.refs_3_.refs_8_ = bf16[256,384]{1,0:T(8,128)(2,1)S(1)} collective-permute-done((bf16[256,384]{1,0:T(8,128)(2,1)S(1)}, bf16[256,384]{1,0:T(8,128)(2,1)S(1)}, u32[]{:S(2)}, u32[]{:S(2)}) %collective-permute-start.12) | collective-permute-done | bytes 196640 | tf_op jit(solution)/shard_map/ppermute | solution.py:817
  100.9 20.5 %feed.2 = (bf16[256,384]{1,0:T(8,128)(2,1)S(1)}, bf16[256,384]{1,0:T(8,128)(2,1)S(1)}, bf16[256,384]{1,0:T(8,128)(2,1)S(1)}, bf16[256,384]{1,0:T(8,128)(2,1)S(1)...) custom-call(s32[2]{0:T(128)S(1)} %pad_add_fusion.place_ref, ...), custom_call_target="tpu_custom_call" | custom-call | flops 10871635968 | bytes 23592960 | tf_op jit(solution)/shard_map/feed/pallas_call | solution.py:351
  125.1 20.5 %feed.3 = (bf16[256,384]{1,0:T(8,128)(2,1)S(1)}, bf16[256,384]{1,0:T(8,128)(2,1)S(1)}, bf16[256,384]{1,0:T(8,128)(2,1)S(1)}, bf16[256,384]{1,0:T(8,128)(2,1)S(1)...) custom-call(s32[2]{0:T(128)S(1)} %pad_add_fusion.place_ref, ...), custom_call_target="tpu_custom_call", output_to_operand_aliasing={{4}: (13, {}), {5}: (14, {}), {6}: (15, {}), {7}: (16, {}),... | custom-call | flops 10871635968 | bytes 23592960 | tf_op jit(solution)/shard_map/feed/pallas_call | solution.py:351
  149.1 13.9 %weights.2 = (bf16[4,2,224,768]{3,2,1,0:T(8,128)(2,1)}, bf16[4,2,224,768]{3,2,1,0:T(8,128)(2,1)}) custom-call(s32[2]{0:T(128)S(1)} %pad_add_fusion.place_ref, bf16[3072,1024]{1,0:T(8,128)(2,1)} %get-tuple-element.176.refs_0_, bf16[3072,1024]{1,0:T(8,128)(2,1)} %get-tuple-element.177.refs_1_, bf16[768,1024]{1,0:T(8,128)(2,1)} %get-tuple-element.178.refs_2_.refs_8_, ...), custom_call_target="tpu_custom_call" | custom-call | flops 4831838208 | bytes 14155776 | tf_op jit(solution)/shard_map/weights/pallas_call | solution.py:500
  164.7 5.8 %mix.5 = (bf16[256,768]{1,0:T(8,128)(2,1)S(1)}, bf16[256,768]{1,0:T(8,128)(2,1)S(1)}, bf16[256,768]{1,0:T(8,128)(2,1)S(1)}, bf16[256,768]{1,0:T(8,128)(2,1)S(1)}) custom-call(s32[2]{0:T(128)S(1)} %pad_add_fusion.place_ref, s32[4]{0:T(128)S(1)} %copy-done.23, bf16[256,384]{1,0:T(8,128)(2,1)S(1)} %get-tuple-element.154.refs_0_, ...), custom_call_target="tpu_custom_call" | custom-call | flops 1610612736 | bytes 9437184 | tf_op jit(solution)/shard_map/mix/pallas_call | solution.py:213
  173.1 13.9 %weights.3 = (bf16[4,2,224,768]{3,2,1,0:T(8,128)(2,1)}, bf16[4,2,224,768]{3,2,1,0:T(8,128)(2,1)}) custom-call(s32[2]{0:T(128)S(1)} %pad_add_fusion.place_ref, bf16[3072,1024]{1,0:T(8,128)(2,1)} %get-tuple-element.176.refs_0_, bf16[3072,1024]{1,0:T(8,128)(2,1)} %get-tuple-element.177.refs_1_, bf16[768,1024]{1,0:T(8,128)(2,1)} %get-tuple-element.178.refs_2_.refs_8_, ...), custom_call_target="tpu_custom_call" | custom-call | flops 4831838208 | bytes 14155776 | tf_op jit(solution)/shard_map/weights/pallas_call | solution.py:500
  187.1 3.5 %add_convert_fusion = (bf16[2,2,224,768]{3,2,1,0:T(8,128)(2,1)S(1)}, bf16[2,2,224,768]{3,2,1,0:T(8,128)(2,1)S(1)}) fusion(bf16[4,2,224,768]{3,2,1,0:T(8,128)(2,1)S(1)} %collective-permute-done.24, bf16[4,2,224,768]{3,2,1,0:T(8,128)(2,1)} %get-tuple-element.200, bf16[4,2,224,768]{3,2,1,0:T(8,128)(2,1)S(1)} %collective-permute-done.23, ...), kind=kLoop, calls=%fused_computation | loop fusion | flops 5505024 | bytes 8257536 | tf_op jit(solution)/shard_map/convert_element_type | solution.py:860
  196.8 18.0 %logits.1 = (bf16[4,3,64,1024]{3,2,1,0:T(8,128)(2,1)}, bf16[4,3,64,1024]{3,2,1,0:T(8,128)(2,1)}, bf16[4,3,64,1024]{3,2,1,0:T(8,128)(2,1)}, bf16[4,3,64,1024]{3,2,1,0:T(8,128)(2,1)}) custom-call(s32[2]{0:T(128)S(1)} %pad_add_fusion.place_ref, s32[4]{0:T(128)S(1)} %copy-done.23, bf16[256,384]{1,0:T(8,128)(2,1)} %copy-done.14, bf16[256,384]{1,0:T(8,128)(2,1)} %copy-done.15, ...), custom_call_target="tpu_custom_call" | custom-call | flops 1610612736 | bytes 12582912 | tf_op jit(solution)/shard_map/logits/pallas_call | solution.py:642
  214.9 8.5 %collective-permute-done.26 = bf16[2,2,224,768]{3,2,1,0:T(8,128)(2,1)} collective-permute-done((bf16[2,2,224,768]{3,2,1,0:T(8,128)(2,1)S(1)}, bf16[2,2,224,768]{3,2,1,0:T(8,128)(2,1)}, u32[]{:S(2)}, u32[]{:S(2)}) %collective-permute-start.26) | collective-permute-done | bytes 1376288 | tf_op jit(solution)/shard_map/ppermute | solution.py:821
  236.5 9.6 %collective-permute-done.33 = bf16[1,2,224,768]{3,2,1,0:T(8,128)(2,1)S(1)} collective-permute-done((bf16[1,2,224,768]{3,2,1,0:T(8,128)(2,1)S(1)}, bf16[1,2,224,768]{3,2,1,0:T(8,128)(2,1)S(1)}, u32[]{:S(2)}, u32[]{:S(2)}) %collective-permute-start.33) | collective-permute-done | bytes 688160 | tf_op jit(solution)/shard_map/ppermute | solution.py:821
  246.1 3.0 collective-permute-done.32
  251.6 10.0 %input.1 = (bf16[4,256,768]{2,1,0:T(8,128)(2,1)}, bf16[4,4,32,768]{3,2,1,0:T(8,128)(2,1)S(1)}, bf16[4,4,32,768]{3,2,1,0:T(8,128)(2,1)S(1)}) custom-call(s32[2]{0:T(128)S(1)} %pad_add_fusion.place_ref, bf16[256,768]{1,0:T(8,128)(2,1)} %copy-done.24, bf16[256,768]{1,0:T(8,128)(2,1)} %copy-done.47, bf16[256,768]{1,0:T(8,128)(2,1)} %copy-done.46, ...), custom_call_target="tpu_custom_call" | custom-call | flops 2415919104 | bytes 14155776 | tf_op jit(solution)/shard_map/input/pallas_call | solution.py:718
  261.6 2.5 collective-permute-done.36
  274.6 3.1 %collective-permute-done.39 = bf16[1,4,32,768]{3,2,1,0:T(8,128)(2,1)S(1)} collective-permute-done((bf16[1,4,32,768]{3,2,1,0:T(8,128)(2,1)S(1)}, bf16[1,4,32,768]{3,2,1,0:T(8,128)(2,1)S(1)}, u32[]{:S(2)}, u32[]{:S(2)}) %collective-permute-start.39) | collective-permute-done | bytes 196640 | tf_op jit(solution)/shard_map/ppermute | solution.py:821
  (226 shorter events, 85.5 us)
Async XLA Ops:
  7.2 93.6 %all-gather.2.cloned.1.call-start = ((), (), s32[]{:S(2)}) async-start(), calls=%async_computation | async-start | bytes 1216512 | tf_op jit(solution)/shard_map/all_gather | solution.py:951
  9.7 20.0 %collective-permute-start = (bf16[96,768]{1,0:T(8,128)(2,1)S(1)}, bf16[96,768]{1,0:T(8,128)(2,1)S(1)}, u32[]{:S(2)}, u32[]{:S(2)}) collective-permute-start(bf16[96,768]{1,0:T(8,128)(2,1)S(1)} %dynamic-slice_bitcast_fusion), channel_id=1, source_target_pairs={{0,3},{1,0},{2,1},{3,2},{4,7},{5,4},{6,5},{7,6},{8,11},{9,8},{10,9... | collective-permute-start | bytes 442376 | tf_op jit(solution)/shard_map/ppermute | solution.py:817
  58.4 25.6 %collective-permute-start.8 = (bf16[256,384]{1,0:T(8,128)(2,1)S(1)}, bf16[256,384]{1,0:T(8,128)(2,1)S(1)}, u32[]{:S(2)}, u32[]{:S(2)}) collective-permute-start(bf16[256,384]{1,0:T(8,128)(2,1)S(1)} %get-tuple-element.146), channel_id=1, source_target_pairs={{0,2},{1,3},{2,0},{3,1},{4,6},{5,7},{6,4},{7,5},{8,10},{9,11},{10,... | collective-permute-start | bytes 589832 | tf_op jit(solution)/shard_map/ppermute | solution.py:817
  59.7 24.3 %collective-permute-start.9 = (bf16[256,384]{1,0:T(8,128)(2,1)S(1)}, bf16[256,384]{1,0:T(8,128)(2,1)S(1)}, u32[]{:S(2)}, u32[]{:S(2)}) collective-permute-start(bf16[256,384]{1,0:T(8,128)(2,1)S(1)} %get-tuple-element.147), channel_id=1, source_target_pairs={{0,3},{1,0},{2,1},{3,2},{4,7},{5,4},{6,5},{7,6},{8,11},{9,8},{10,9... | collective-permute-start | bytes 589832 | tf_op jit(solution)/shard_map/ppermute | solution.py:817
  66.5 25.1 %collective-permute-start.10 = (bf16[256,384]{1,0:T(8,128)(2,1)S(1)}, bf16[256,384]{1,0:T(8,128)(2,1)S(1)}, u32[]{:S(2)}, u32[]{:S(2)}) collective-permute-start(bf16[256,384]{1,0:T(8,128)(2,1)S(1)} %get-tuple-element.150), channel_id=1, source_target_pairs={{0,1},{1,2},{2,3},{3,0},{4,5},{5,6},{6,7},{7,4},{8,9},{9,10},{10,1... | collective-permute-start | bytes 589832 | tf_op jit(solution)/shard_map/ppermute | solution.py:817
  67.4 25.1 %collective-permute-start.11 = (bf16[256,384]{1,0:T(8,128)(2,1)S(1)}, bf16[256,384]{1,0:T(8,128)(2,1)S(1)}, u32[]{:S(2)}, u32[]{:S(2)}) collective-permute-start(bf16[256,384]{1,0:T(8,128)(2,1)S(1)} %get-tuple-element.151), channel_id=1, source_target_pairs={{0,2},{1,3},{2,0},{3,1},{4,6},{5,7},{6,4},{7,5},{8,10},{9,11},{10,... | collective-permute-start | bytes 589832 | tf_op jit(solution)/shard_map/ppermute | solution.py:817
  96.6 24.8 %collective-permute-start.13 = (bf16[256,384]{1,0:T(8,128)(2,1)S(1)}, bf16[256,384]{1,0:T(8,128)(2,1)S(1)}, u32[]{:S(2)}, u32[]{:S(2)}) collective-permute-start(bf16[256,384]{1,0:T(8,128)(2,1)S(1)} %get-tuple-element.159), channel_id=1, source_target_pairs={{0,1},{1,2},{2,3},{3,0},{4,5},{5,6},{6,7},{7,4},{8,9},{9,10},{10,1... | collective-permute-start | bytes 589832 | tf_op jit(solution)/shard_map/ppermute | solution.py:817
  97.2 24.2 %collective-permute-start.14 = (bf16[256,384]{1,0:T(8,128)(2,1)S(1)}, bf16[256,384]{1,0:T(8,128)(2,1)S(1)}, u32[]{:S(2)}, u32[]{:S(2)}) collective-permute-start(bf16[256,384]{1,0:T(8,128)(2,1)S(1)} %get-tuple-element.160), channel_id=1, source_target_pairs={{0,2},{1,3},{2,0},{3,1},{4,6},{5,7},{6,4},{7,5},{8,10},{9,11},{10,... | collective-permute-start | bytes 589832 | tf_op jit(solution)/shard_map/ppermute | solution.py:817
  99.2 22.2 %collective-permute-start.15 = (bf16[256,384]{1,0:T(8,128)(2,1)S(1)}, bf16[256,384]{1,0:T(8,128)(2,1)S(1)}, u32[]{:S(2)}, u32[]{:S(2)}) collective-permute-start(bf16[256,384]{1,0:T(8,128)(2,1)S(1)} %get-tuple-element.161), channel_id=1, source_target_pairs={{0,3},{1,0},{2,1},{3,2},{4,7},{5,4},{6,5},{7,6},{8,11},{9,8},{10,9... | collective-permute-start | bytes 589832 | tf_op jit(solution)/shard_map/ppermute | solution.py:817
  121.5 24.2 %collective-permute-start.16 = (bf16[256,384]{1,0:T(8,128)(2,1)S(1)}, bf16[256,384]{1,0:T(8,128)(2,1)S(1)}, u32[]{:S(2)}, u32[]{:S(2)}) collective-permute-start(bf16[256,384]{1,0:T(8,128)(2,1)S(1)} %get-tuple-element.172), channel_id=1, source_target_pairs={{0,3},{1,0},{2,1},{3,2},{4,7},{5,4},{6,5},{7,6},{8,11},{9,8},{10,9... | collective-permute-start | bytes 589832 | tf_op jit(solution)/shard_map/ppermute | solution.py:817
  122.2 23.5 %collective-permute-start.17 = (bf16[256,384]{1,0:T(8,128)(2,1)S(1)}, bf16[256,384]{1,0:T(8,128)(2,1)S(1)}, u32[]{:S(2)}, u32[]{:S(2)}) collective-permute-start(bf16[256,384]{1,0:T(8,128)(2,1)S(1)} %get-tuple-element.173), channel_id=1, source_target_pairs={{0,2},{1,3},{2,0},{3,1},{4,6},{5,7},{6,4},{7,5},{8,10},{9,11},{10,... | collective-permute-start | bytes 589832 | tf_op jit(solution)/shard_map/ppermute | solution.py:817
  123.3 22.4 %collective-permute-start.18 = (bf16[256,384]{1,0:T(8,128)(2,1)S(1)}, bf16[256,384]{1,0:T(8,128)(2,1)S(1)}, u32[]{:S(2)}, u32[]{:S(2)}) collective-permute-start(bf16[256,384]{1,0:T(8,128)(2,1)S(1)} %get-tuple-element.174), channel_id=1, source_target_pairs={{0,1},{1,2},{2,3},{3,0},{4,5},{5,6},{6,7},{7,4},{8,9},{9,10},{10,1... | collective-permute-start | bytes 589832 | tf_op jit(solution)/shard_map/ppermute | solution.py:817
  145.7 17.3 %collective-permute-start.19 = (bf16[256,384]{1,0:T(8,128)(2,1)S(1)}, bf16[256,384]{1,0:T(8,128)(2,1)S(1)}, u32[]{:S(2)}, u32[]{:S(2)}) collective-permute-start(bf16[256,384]{1,0:T(8,128)(2,1)S(1)} %get-tuple-element.184), channel_id=1, source_target_pairs={{0,3},{1,0},{2,1},{3,2},{4,7},{5,4},{6,5},{7,6},{8,11},{9,8},{10,9... | collective-permute-start | bytes 589832 | tf_op jit(solution)/shard_map/ppermute | solution.py:817
  164.1 22.9 %collective-permute-start.24 = (bf16[4,2,224,768]{3,2,1,0:T(8,128)(2,1)}, bf16[4,2,224,768]{3,2,1,0:T(8,128)(2,1)S(1)}, u32[]{:S(2)}, u32[]{:S(2)}) collective-permute-start(bf16[4,2,224,768]{3,2,1,0:T(8,128)(2,1)} %get-tuple-element.196), channel_id=1, source_target_pairs={{0,4},{4,0},{8,12},{12,8},{16,20},{20,16},{24,28},{28,24},{1,5},{5... | collective-permute-start | bytes 8257544 | tf_op jit(solution)/shard_map/ppermute | solution.py:821
  164.2 22.9 %collective-permute-start.23 = (bf16[4,2,224,768]{3,2,1,0:T(8,128)(2,1)}, bf16[4,2,224,768]{3,2,1,0:T(8,128)(2,1)S(1)}, u32[]{:S(2)}, u32[]{:S(2)}) collective-permute-start(bf16[4,2,224,768]{3,2,1,0:T(8,128)(2,1)} %get-tuple-element.194), channel_id=1, source_target_pairs={{0,4},{4,0},{8,12},{12,8},{16,20},{20,16},{24,28},{28,24},{1,5},{5... | collective-permute-start | bytes 8257544 | tf_op jit(solution)/shard_map/ppermute | solution.py:821
  171.3 20.4 %collective-permute-start.22 = (bf16[256,768]{1,0:T(8,128)(2,1)S(1)}, bf16[256,768]{1,0:T(8,128)(2,1)S(1)}, u32[]{:S(2)}, u32[]{:S(2)}) collective-permute-start(bf16[256,768]{1,0:T(8,128)(2,1)S(1)} %get-tuple-element.193), channel_id=1, source_target_pairs={{0,2},{1,3},{2,0},{3,1},{4,6},{5,7},{6,4},{7,5},{8,10},{9,11},{10,... | collective-permute-start | bytes 1179656 | tf_op jit(solution)/shard_map/ppermute | solution.py:817
  191.8 31.6 %collective-permute-start.26 = (bf16[2,2,224,768]{3,2,1,0:T(8,128)(2,1)S(1)}, bf16[2,2,224,768]{3,2,1,0:T(8,128)(2,1)}, u32[]{:S(2)}, u32[]{:S(2)}) collective-permute-start(bf16[2,2,224,768]{3,2,1,0:T(8,128)(2,1)S(1)} %get-tuple-element.201), channel_id=1, source_target_pairs={{0,16},{4,20},{8,24},{12,28},{16,0},{20,4},{24,8},{28,12},{1,17},{... | collective-permute-start | bytes 4128776 | tf_op jit(solution)/shard_map/ppermute | solution.py:821
  193.3 31.2 %collective-permute-start.25 = (bf16[2,2,224,768]{3,2,1,0:T(8,128)(2,1)S(1)}, bf16[2,2,224,768]{3,2,1,0:T(8,128)(2,1)S(1)}, u32[]{:S(2)}, u32[]{:S(2)}) collective-permute-start(bf16[2,2,224,768]{3,2,1,0:T(8,128)(2,1)S(1)} %get-tuple-element.199), channel_id=1, source_target_pairs={{0,8},{4,12},{8,0},{12,4},{16,24},{20,28},{24,16},{28,20},{1,9},{5... | collective-permute-start | bytes 4128776 | tf_op jit(solution)/shard_map/ppermute | solution.py:821
  194.8 20.1 %collective-permute-start.27 = (bf16[256,768]{1,0:T(8,128)(2,1)S(1)}, bf16[256,768]{1,0:T(8,128)(2,1)S(1)}, u32[]{:S(2)}, u32[]{:S(2)}) collective-permute-start(bf16[256,768]{1,0:T(8,128)(2,1)S(1)} %get-tuple-element.204), channel_id=1, source_target_pairs={{0,3},{1,0},{2,1},{3,2},{4,7},{5,4},{6,5},{7,6},{8,11},{9,8},{10,9... | collective-permute-start | bytes 1179656 | tf_op jit(solution)/shard_map/ppermute | solution.py:817
  196.5 18.4 %collective-permute-start.28 = (bf16[256,768]{1,0:T(8,128)(2,1)S(1)}, bf16[256,768]{1,0:T(8,128)(2,1)S(1)}, u32[]{:S(2)}, u32[]{:S(2)}) collective-permute-start(bf16[256,768]{1,0:T(8,128)(2,1)S(1)} %get-tuple-element.205), channel_id=1, source_target_pairs={{0,1},{1,2},{2,3},{3,0},{4,5},{5,6},{6,7},{7,4},{8,9},{9,10},{10,1... | collective-permute-start | bytes 1179656 | tf_op jit(solution)/shard_map/ppermute | solution.py:817
  227.7 18.4 %collective-permute-start.33 = (bf16[1,2,224,768]{3,2,1,0:T(8,128)(2,1)S(1)}, bf16[1,2,224,768]{3,2,1,0:T(8,128)(2,1)S(1)}, u32[]{:S(2)}, u32[]{:S(2)}) collective-permute-start(bf16[1,2,224,768]{3,2,1,0:T(8,128)(2,1)S(1)} %add_convert_fusion.5), channel_id=1, source_target_pairs={{0,8},{4,12},{8,0},{12,4},{16,24},{20,28},{24,16},{28,20},{1,9},{5... | collective-permute-start | bytes 2064392 | tf_op jit(solution)/shard_map/ppermute | solution.py:821
  230.6 18.4 %collective-permute-start.32 = (bf16[1,2,224,768]{3,2,1,0:T(8,128)(2,1)S(1)}, bf16[1,2,224,768]{3,2,1,0:T(8,128)(2,1)S(1)}, u32[]{:S(2)}, u32[]{:S(2)}) collective-permute-start(bf16[1,2,224,768]{3,2,1,0:T(8,128)(2,1)S(1)} %add_convert_fusion.6), channel_id=1, source_target_pairs={{0,16},{4,20},{8,24},{12,28},{16,0},{20,4},{24,8},{28,12},{1,17},{... | collective-permute-start | bytes 2064392 | tf_op jit(solution)/shard_map/ppermute | solution.py:821
  234.4 29.6 %collective-permute-start.36 = (bf16[2,3,64,1024]{3,2,1,0:T(8,128)(2,1)S(1)}, bf16[2,3,64,1024]{3,2,1,0:T(8,128)(2,1)S(1)}, u32[]{:S(2)}, u32[]{:S(2)}) collective-permute-start(bf16[2,3,64,1024]{3,2,1,0:T(8,128)(2,1)S(1)} %add_convert_fusion.2), channel_id=1, source_target_pairs={{0,16},{4,20},{8,24},{12,28},{16,0},{20,4},{24,8},{28,12},{1,17},{... | collective-permute-start | bytes 2359304 | tf_op jit(solution)/shard_map/ppermute | solution.py:821
  235.8 28.2 %collective-permute-start.31 = (bf16[2,3,64,1024]{3,2,1,0:T(8,128)(2,1)S(1)}, bf16[2,3,64,1024]{3,2,1,0:T(8,128)(2,1)S(1)}, u32[]{:S(2)}, u32[]{:S(2)}) collective-permute-start(bf16[2,3,64,1024]{3,2,1,0:T(8,128)(2,1)S(1)} %add_convert_fusion.3), channel_id=1, source_target_pairs={{0,8},{4,12},{8,0},{12,4},{16,24},{20,28},{24,16},{28,20},{1,9},{5... | collective-permute-start | bytes 2359304 | tf_op jit(solution)/shard_map/ppermute | solution.py:821
  (73 other events, 853.6 us)
Sparse Core Ops, SparseCore 0:
  11.5 74.2 all-gather.1

commit v6 on v5

--- a/solution.py
+++ b/solution.py
@@ -812,6 +812,32 @@
     )(*terms)
 
 
+def logit_sums_kernel(*refs):
+    out_ref = refs[-1]
+    middle = out_ref.shape[1] // 2
+    for side in range(2):
+        keep, came, went, last = (ref[0].astype(F32) for ref in refs[4 * side : 4 * side + 4])
+        out_ref[:, side * middle : (side + 1) * middle, :] = keep + came + went + last
+
+
+def logit_sums(keeps, cames, wents, lasts):
+    half = keeps[0].shape[0] // 2
+    _, heads, middle, full = keeps[0].shape
+    block = (1, heads, middle, full)
+    later = pl.BlockSpec(block, lambda _: (half, 0, 0, 0))
+    early = pl.BlockSpec(block, lambda _: (0, 0, 0, 0))
+    operands = [v for group in zip(keeps, cames, wents, lasts) for v in group]
+    return pl.pallas_call(
+        logit_sums_kernel,
+        grid=(1,),
+        in_specs=[later, later, early, early] * 2,
+        out_specs=whole((heads, 2 * middle, full)),
+        out_shape=far((heads, 2 * middle, full), F32),
+        compiler_params=params(16),
+        name="logit_sums",
+    )(*map(kept, operands))
+
+
 def shift(value, axis, extent, by):
     by = by % extent
     return lax.ppermute(value, axis, [(i, (i + by) % extent) for i in range(extent)])
@@ -1077,7 +1103,11 @@
     grad_up, grad_down, grad_out = feed_sums(terms, tile, square, zones)
     grad_value, line = value_sums(value_terms, square, zones)
     line = line[0]
-    grad_rand = jnp.concatenate(rand_sum.finish(*value_blocks[1:]), 1)
+    if ranks == 8:
+        lasts = lax.optimization_barrier((*rand_sum.last, *value_blocks[1:]))[:2]
+        grad_rand = logit_sums(rand_sum.keeps, rand_sum.came, rand_sum.went, lasts)
+    else:
+        grad_rand = jnp.concatenate(rand_sum.finish(*value_blocks[1:]), 1)
     return (
         feed1[zones],
         grad_x,

time: 306 us -> 305 us (level)
  Pallas kernels: 135 us -> 139 us
  other arithmetic: 19.4 us -> 16 us
    pallas_call x0 -> x1, Pallas kernels: none -> 3.37 us  [logit_sums(): pl.pallas_call(logit_sums_kernel, grid=(1,), in_specs=[later, later, earl...]
  transfers between devices with their start and end apart: 48 -> 48, of which waited for: 19 -> 19; matrix products, arithmetic and copies ran while one was open for 8% -> 6% of each run, Pallas kernels for 44% -> 45%
where the time goes in v6:
time: 305 us; the launch traced here: 304 us
  Pallas kernels  139 us (46%)
  waiting for transfers between devices  71.2 us (23%)
  starting transfers between devices  55 us (18%)
  other arithmetic  16 us (5%)
  between operations  15 us (5%)
  local copies, waits for them, and re-layouts  8.49 us (3%)
    ppermute x30, starting transfers between devices, shift(): lax.ppermute(value, axis, [(i, (i + by) % extent) for i in range(extent)])  42.3 us
    pallas_call x2, Pallas kernels, feed(): pl.pallas_call(functools.partial(feed_kernel, zones, heads, size, steps,...  40.9 us
    ppermute x30, waiting for transfers between devices, shift(): lax.ppermute(value, axis, [(i, (i + by) % extent) for i in range(extent)])  35.7 us
    ppermute x17, waiting for transfers between devices, flip(): return lax.ppermute(value, axis, [(i, i ^ mask) for i in range(extent)])  35.5 us
    pallas_call x2, Pallas kernels, weight_grads(): pl.pallas_call(functools.partial(weights_kernel, zones, chunks, heads), g...  27.8 us
    pallas_call x1, Pallas kernels, logit_grads(): pl.pallas_call(functools.partial(logits_kernel, zones, chunks, count, hea...  18 us
    pallas_call x3, Pallas kernels, mix(): pl.pallas_call(functools.partial(mix_kernel, zones, chunks, count, lanes...  16.8 us
    pallas_call x1, Pallas kernels, make_probs(): pl.pallas_call(probs_kernel, grid=(heads, rows // SHORT), in_specs=[pl.Bl...  14 us
  transfers between devices with their start and end apart: 48, of which 19 were waited for; matrix products, arithmetic and copies ran while one was open for 6% of the time, Pallas kernels for 45%

profile of v6, /device:TPU:0, one launch (start us, length us, event | category | flops | bytes accessed | tf_op | source)
XLA Modules:
  0.0 304.4 jit_solution(7189241052165143946)
XLA Ops:
  9.7 5.1 %collective-permute-start = (bf16[96,768]{1,0:T(8,128)(2,1)S(1)}, bf16[96,768]{1,0:T(8,128)(2,1)S(1)}, u32[]{:S(2)}, u32[]{:S(2)}) collective-permute-start(bf16[96,768]{1,0:T(8,128)(2,1)S(1)} %dynamic-slice_bitcast_fusion), channel_id=1, source_target_pairs={{0,3},{1,0},{2,1},{3,2},{4,7},{5,4},{6,5},{7,6},{8,11},{9,8},{10,9... | collective-permute-start | bytes 442376 | tf_op jit(solution)/shard_map/ppermute | solution.py:843
  15.9 14.0 %probs.1 = (bf16[3,1024,1024]{2,1,0:T(8,128)(2,1)}, bf16[3,1024,1024]{2,1,0:T(8,128)(2,1)}, bf16[3,256,256]{2,1,0:T(8,128)(2,1)S(1)}, bf16[3,256,256]{2,1,0:T(8,128)(2,1)S(1)}) custom-call(bf16[3,1024,1024]{2,1,0:T(8,128)(2,1)} %refs_16_.1), custom_call_target="tpu_custom_call" | custom-call | flops 31457280 | bytes 18874368 | tf_op jit(solution)/shard_map/probs/pallas_call | solution.py:109
  31.9 2.8 values.2
  41.5 3.5 %collective-permute-done.4.refs_1_.refs_9_ = bf16[256,384]{1,0:T(8,128)(2,1)S(1)} collective-permute-done((bf16[256,384]{1,0:T(8,128)(2,1)S(1)}, bf16[256,384]{1,0:T(8,128)(2,1)S(1)}, u32[]{:S(2)}, u32[]{:S(2)}) %collective-permute-start.4) | collective-permute-done | bytes 196640 | tf_op jit(solution)/shard_map/ppermute | solution.py:843
  44.9 8.5 %collective-permute-done.5.refs_2_.refs_10_ = bf16[256,384]{1,0:T(8,128)(2,1)S(1)} collective-permute-done((bf16[256,384]{1,0:T(8,128)(2,1)S(1)}, bf16[256,384]{1,0:T(8,128)(2,1)S(1)}, u32[]{:S(2)}, u32[]{:S(2)}) %collective-permute-start.5) | collective-permute-done | bytes 196640 | tf_op jit(solution)/shard_map/ppermute | solution.py:843
  53.5 4.9 %collective-permute-start.7 = (bf16[256,384]{1,0:T(8,128)(2,1)S(1)}, bf16[256,384]{1,0:T(8,128)(2,1)S(1)}, u32[]{:S(2)}, u32[]{:S(2)}) collective-permute-start(bf16[256,384]{1,0:T(8,128)(2,1)S(1)} %get-tuple-element.145), channel_id=1, source_target_pairs={{0,1},{1,2},{2,3},{3,0},{4,5},{5,6},{6,7},{7,4},{8,9},{9,10},{10,1... | collective-permute-start | bytes 589832 | tf_op jit(solution)/shard_map/ppermute | solution.py:843
  60.8 5.6 %mix.3 = (bf16[256,384]{1,0:T(8,128)(2,1)S(1)}, bf16[256,384]{1,0:T(8,128)(2,1)S(1)}, bf16[256,384]{1,0:T(8,128)(2,1)S(1)}, bf16[256,384]{1,0:T(8,128)(2,1)S(1)}) custom-call(s32[2]{0:T(128)S(1)} %pad_add_fusion.place_ref, s32[2]{0:T(128)S(1)} %get-tuple-element.265.long_flags, bf16[256,384]{1,0:T(8,128)(2,1)S(1)} %get-tuple-element.135.refs_0_.refs_8_, ...), custom_call_target="tpu_custom_call" | custom-call | flops 805306368 | bytes 7864320 | tf_op jit(solution)/shard_map/mix/pallas_call | solution.py:213
  69.0 14.9 %collective-permute-done.8.refs_2_.refs_14_ = bf16[256,384]{1,0:T(8,128)(2,1)S(1)} collective-permute-done((bf16[256,384]{1,0:T(8,128)(2,1)S(1)}, bf16[256,384]{1,0:T(8,128)(2,1)S(1)}, u32[]{:S(2)}, u32[]{:S(2)}) %collective-permute-start.8) | collective-permute-done | bytes 196640 | tf_op jit(solution)/shard_map/ppermute | solution.py:843
  85.4 5.5 %mix.4 = (bf16[256,384]{1,0:T(8,128)(2,1)S(1)}, bf16[256,384]{1,0:T(8,128)(2,1)S(1)}, bf16[256,384]{1,0:T(8,128)(2,1)S(1)}, bf16[256,384]{1,0:T(8,128)(2,1)S(1)}) custom-call(s32[2]{0:T(128)S(1)} %pad_add_fusion.place_ref, s32[2]{0:T(128)S(1)} %get-tuple-element.264.long_flags, bf16[256,384]{1,0:T(8,128)(2,1)S(1)} %get-tuple-element.133.refs_0_.refs_12_, ...), custom_call_target="tpu_custom_call" | custom-call | flops 805306368 | bytes 7864320 | tf_op jit(solution)/shard_map/mix/pallas_call | solution.py:213
  92.4 4.1 %collective-permute-done.12.refs_3_.refs_8_ = bf16[256,384]{1,0:T(8,128)(2,1)S(1)} collective-permute-done((bf16[256,384]{1,0:T(8,128)(2,1)S(1)}, bf16[256,384]{1,0:T(8,128)(2,1)S(1)}, u32[]{:S(2)}, u32[]{:S(2)}) %collective-permute-start.12) | collective-permute-done | bytes 196640 | tf_op jit(solution)/shard_map/ppermute | solution.py:843
  100.7 20.5 %feed.2 = (bf16[256,384]{1,0:T(8,128)(2,1)S(1)}, bf16[256,384]{1,0:T(8,128)(2,1)S(1)}, bf16[256,384]{1,0:T(8,128)(2,1)S(1)}, bf16[256,384]{1,0:T(8,128)(2,1)S(1)...) custom-call(s32[2]{0:T(128)S(1)} %pad_add_fusion.place_ref, ...), custom_call_target="tpu_custom_call" | custom-call | flops 10871635968 | bytes 23592960 | tf_op jit(solution)/shard_map/feed/pallas_call | solution.py:351
  124.9 20.4 %feed.3 = (bf16[256,384]{1,0:T(8,128)(2,1)S(1)}, bf16[256,384]{1,0:T(8,128)(2,1)S(1)}, bf16[256,384]{1,0:T(8,128)(2,1)S(1)}, bf16[256,384]{1,0:T(8,128)(2,1)S(1)...) custom-call(s32[2]{0:T(128)S(1)} %pad_add_fusion.place_ref, ...), custom_call_target="tpu_custom_call", output_to_operand_aliasing={{4}: (13, {}), {5}: (14, {}), {6}: (15, {}), {7}: (16, {}),... | custom-call | flops 10871635968 | bytes 23592960 | tf_op jit(solution)/shard_map/feed/pallas_call | solution.py:351
  148.9 13.8 %weights.2 = (bf16[4,2,224,768]{3,2,1,0:T(8,128)(2,1)}, bf16[4,2,224,768]{3,2,1,0:T(8,128)(2,1)}) custom-call(s32[2]{0:T(128)S(1)} %pad_add_fusion.place_ref, bf16[3072,1024]{1,0:T(8,128)(2,1)} %get-tuple-element.176.refs_0_, bf16[3072,1024]{1,0:T(8,128)(2,1)} %get-tuple-element.177.refs_1_, bf16[768,1024]{1,0:T(8,128)(2,1)} %get-tuple-element.178.refs_2_.refs_8_, ...), custom_call_target="tpu_custom_call" | custom-call | flops 4831838208 | bytes 14155776 | tf_op jit(solution)/shard_map/weights/pallas_call | solution.py:500
  164.5 5.8 %mix.5 = (bf16[256,768]{1,0:T(8,128)(2,1)S(1)}, bf16[256,768]{1,0:T(8,128)(2,1)S(1)}, bf16[256,768]{1,0:T(8,128)(2,1)S(1)}, bf16[256,768]{1,0:T(8,128)(2,1)S(1)}) custom-call(s32[2]{0:T(128)S(1)} %pad_add_fusion.place_ref, s32[4]{0:T(128)S(1)} %copy-done.23, bf16[256,384]{1,0:T(8,128)(2,1)S(1)} %get-tuple-element.154.refs_0_, ...), custom_call_target="tpu_custom_call" | custom-call | flops 1610612736 | bytes 9437184 | tf_op jit(solution)/shard_map/mix/pallas_call | solution.py:213
  172.9 13.9 %weights.3 = (bf16[4,2,224,768]{3,2,1,0:T(8,128)(2,1)}, bf16[4,2,224,768]{3,2,1,0:T(8,128)(2,1)}) custom-call(s32[2]{0:T(128)S(1)} %pad_add_fusion.place_ref, bf16[3072,1024]{1,0:T(8,128)(2,1)} %get-tuple-element.176.refs_0_, bf16[3072,1024]{1,0:T(8,128)(2,1)} %get-tuple-element.177.refs_1_, bf16[768,1024]{1,0:T(8,128)(2,1)} %get-tuple-element.178.refs_2_.refs_8_, ...), custom_call_target="tpu_custom_call" | custom-call | flops 4831838208 | bytes 14155776 | tf_op jit(solution)/shard_map/weights/pallas_call | solution.py:500
  186.8 3.5 %add_convert_fusion = (bf16[2,2,224,768]{3,2,1,0:T(8,128)(2,1)S(1)}, bf16[2,2,224,768]{3,2,1,0:T(8,128)(2,1)S(1)}) fusion(bf16[4,2,224,768]{3,2,1,0:T(8,128)(2,1)S(1)} %collective-permute-done.24, bf16[4,2,224,768]{3,2,1,0:T(8,128)(2,1)} %get-tuple-element.200, bf16[4,2,224,768]{3,2,1,0:T(8,128)(2,1)S(1)} %collective-permute-done.23, ...), kind=kLoop, calls=%fused_computation | loop fusion | flops 5505024 | bytes 8257536 | tf_op jit(solution)/shard_map/convert_element_type | solution.py:886
  196.5 18.0 %logits.1 = (bf16[4,3,64,1024]{3,2,1,0:T(8,128)(2,1)}, bf16[4,3,64,1024]{3,2,1,0:T(8,128)(2,1)}, bf16[4,3,64,1024]{3,2,1,0:T(8,128)(2,1)}, bf16[4,3,64,1024]{3,2,1,0:T(8,128)(2,1)}) custom-call(s32[2]{0:T(128)S(1)} %pad_add_fusion.place_ref, s32[4]{0:T(128)S(1)} %copy-done.23, bf16[256,384]{1,0:T(8,128)(2,1)} %copy-done.14, bf16[256,384]{1,0:T(8,128)(2,1)} %copy-done.15, ...), custom_call_target="tpu_custom_call" | custom-call | flops 1610612736 | bytes 12582912 | tf_op jit(solution)/shard_map/logits/pallas_call | solution.py:642
  214.6 8.4 %collective-permute-done.26 = bf16[2,2,224,768]{3,2,1,0:T(8,128)(2,1)S(1)} collective-permute-done((bf16[2,2,224,768]{3,2,1,0:T(8,128)(2,1)S(1)}, bf16[2,2,224,768]{3,2,1,0:T(8,128)(2,1)S(1)}, u32[]{:S(2)}, u32[]{:S(2)}) %collective-permute-start.26) | collective-permute-done | bytes 1376288 | tf_op jit(solution)/shard_map/ppermute | solution.py:847
  236.4 9.4 %collective-permute-done.33 = bf16[1,2,224,768]{3,2,1,0:T(8,128)(2,1)S(1)} collective-permute-done((bf16[1,2,224,768]{3,2,1,0:T(8,128)(2,1)S(1)}, bf16[1,2,224,768]{3,2,1,0:T(8,128)(2,1)S(1)}, u32[]{:S(2)}, u32[]{:S(2)}) %collective-permute-start.33) | collective-permute-done | bytes 688160 | tf_op jit(solution)/shard_map/ppermute | solution.py:847
  245.8 3.1 %collective-permute-done.32 = bf16[1,2,224,768]{3,2,1,0:T(8,128)(2,1)S(1)} collective-permute-done((bf16[1,2,224,768]{3,2,1,0:T(8,128)(2,1)S(1)}, bf16[1,2,224,768]{3,2,1,0:T(8,128)(2,1)S(1)}, u32[]{:S(2)}, u32[]{:S(2)}) %collective-permute-start.32) | collective-permute-done | bytes 688160 | tf_op jit(solution)/shard_map/ppermute | solution.py:847
  250.9 10.0 %input.1 = (bf16[4,256,768]{2,1,0:T(8,128)(2,1)}, bf16[4,4,32,768]{3,2,1,0:T(8,128)(2,1)S(1)}, bf16[4,4,32,768]{3,2,1,0:T(8,128)(2,1)S(1)}) custom-call(s32[2]{0:T(128)S(1)} %pad_add_fusion.place_ref, bf16[256,768]{1,0:T(8,128)(2,1)} %copy-done.24, bf16[256,768]{1,0:T(8,128)(2,1)} %copy-done.54, bf16[256,768]{1,0:T(8,128)(2,1)} %copy-done.53, ...), custom_call_target="tpu_custom_call" | custom-call | flops 2415919104 | bytes 14155776 | tf_op jit(solution)/shard_map/input/pallas_call | solution.py:718
  260.9 3.0 collective-permute-done.36.refs_6_
  275.0 3.1 %collective-permute-done.39 = bf16[1,4,32,768]{3,2,1,0:T(8,128)(2,1)S(1)} collective-permute-done((bf16[1,4,32,768]{3,2,1,0:T(8,128)(2,1)S(1)}, bf16[1,4,32,768]{3,2,1,0:T(8,128)(2,1)S(1)}, u32[]{:S(2)}, u32[]{:S(2)}) %collective-permute-start.39) | collective-permute-done | bytes 196640 | tf_op jit(solution)/shard_map/ppermute | solution.py:847
  292.2 3.4 %logit_sums.1 = f32[3,128,1024]{2,1,0:T(8,128)} custom-call(bf16[4,3,64,1024]{3,2,1,0:T(8,128)(2,1)} %get-tuple-element.216.refs_0_, bf16[4,3,64,1024]{3,2,1,0:T(8,128)(2,1)} %collective-permute-done.29.refs_1_, bf16[2,3,64,1024]{3,2,1,0:T(8,128)(2,1)} %copy-done.33, bf16[1,3,64,1024]{3,2,1,0:T(8,128)(2,1)} %copy-done.46, ...), custom_call_target="tpu_custom_call" | custom-call | tf_op jit(solution)/shard_map/logit_sums/pallas_call | solution.py:830
  (238 shorter events, 84.3 us)
Async XLA Ops:
  7.2 93.5 %all-gather.2.cloned.1.call-start = ((), (), s32[]{:S(2)}) async-start(), calls=%async_computation | async-start | bytes 1216512 | tf_op jit(solution)/shard_map/all_gather | solution.py:977
  9.7 20.1 %collective-permute-start = (bf16[96,768]{1,0:T(8,128)(2,1)S(1)}, bf16[96,768]{1,0:T(8,128)(2,1)S(1)}, u32[]{:S(2)}, u32[]{:S(2)}) collective-permute-start(bf16[96,768]{1,0:T(8,128)(2,1)S(1)} %dynamic-slice_bitcast_fusion), channel_id=1, source_target_pairs={{0,3},{1,0},{2,1},{3,2},{4,7},{5,4},{6,5},{7,6},{8,11},{9,8},{10,9... | collective-permute-start | bytes 442376 | tf_op jit(solution)/shard_map/ppermute | solution.py:843
  58.4 25.5 %collective-permute-start.8 = (bf16[256,384]{1,0:T(8,128)(2,1)S(1)}, bf16[256,384]{1,0:T(8,128)(2,1)S(1)}, u32[]{:S(2)}, u32[]{:S(2)}) collective-permute-start(bf16[256,384]{1,0:T(8,128)(2,1)S(1)} %get-tuple-element.146), channel_id=1, source_target_pairs={{0,2},{1,3},{2,0},{3,1},{4,6},{5,7},{6,4},{7,5},{8,10},{9,11},{10,... | collective-permute-start | bytes 589832 | tf_op jit(solution)/shard_map/ppermute | solution.py:843
  59.7 24.2 %collective-permute-start.9 = (bf16[256,384]{1,0:T(8,128)(2,1)S(1)}, bf16[256,384]{1,0:T(8,128)(2,1)S(1)}, u32[]{:S(2)}, u32[]{:S(2)}) collective-permute-start(bf16[256,384]{1,0:T(8,128)(2,1)S(1)} %get-tuple-element.147), channel_id=1, source_target_pairs={{0,3},{1,0},{2,1},{3,2},{4,7},{5,4},{6,5},{7,6},{8,11},{9,8},{10,9... | collective-permute-start | bytes 589832 | tf_op jit(solution)/shard_map/ppermute | solution.py:843
  66.5 25.1 %collective-permute-start.10 = (bf16[256,384]{1,0:T(8,128)(2,1)S(1)}, bf16[256,384]{1,0:T(8,128)(2,1)S(1)}, u32[]{:S(2)}, u32[]{:S(2)}) collective-permute-start(bf16[256,384]{1,0:T(8,128)(2,1)S(1)} %get-tuple-element.150), channel_id=1, source_target_pairs={{0,1},{1,2},{2,3},{3,0},{4,5},{5,6},{6,7},{7,4},{8,9},{9,10},{10,1... | collective-permute-start | bytes 589832 | tf_op jit(solution)/shard_map/ppermute | solution.py:843
  67.4 25.0 %collective-permute-start.11 = (bf16[256,384]{1,0:T(8,128)(2,1)S(1)}, bf16[256,384]{1,0:T(8,128)(2,1)S(1)}, u32[]{:S(2)}, u32[]{:S(2)}) collective-permute-start(bf16[256,384]{1,0:T(8,128)(2,1)S(1)} %get-tuple-element.151), channel_id=1, source_target_pairs={{0,2},{1,3},{2,0},{3,1},{4,6},{5,7},{6,4},{7,5},{8,10},{9,11},{10,... | collective-permute-start | bytes 589832 | tf_op jit(solution)/shard_map/ppermute | solution.py:843
  96.4 24.8 %collective-permute-start.13 = (bf16[256,384]{1,0:T(8,128)(2,1)S(1)}, bf16[256,384]{1,0:T(8,128)(2,1)S(1)}, u32[]{:S(2)}, u32[]{:S(2)}) collective-permute-start(bf16[256,384]{1,0:T(8,128)(2,1)S(1)} %get-tuple-element.159), channel_id=1, source_target_pairs={{0,1},{1,2},{2,3},{3,0},{4,5},{5,6},{6,7},{7,4},{8,9},{9,10},{10,1... | collective-permute-start | bytes 589832 | tf_op jit(solution)/shard_map/ppermute | solution.py:843
  97.0 24.2 %collective-permute-start.14 = (bf16[256,384]{1,0:T(8,128)(2,1)S(1)}, bf16[256,384]{1,0:T(8,128)(2,1)S(1)}, u32[]{:S(2)}, u32[]{:S(2)}) collective-permute-start(bf16[256,384]{1,0:T(8,128)(2,1)S(1)} %get-tuple-element.160), channel_id=1, source_target_pairs={{0,2},{1,3},{2,0},{3,1},{4,6},{5,7},{6,4},{7,5},{8,10},{9,11},{10,... | collective-permute-start | bytes 589832 | tf_op jit(solution)/shard_map/ppermute | solution.py:843
  99.1 22.1 %collective-permute-start.15 = (bf16[256,384]{1,0:T(8,128)(2,1)S(1)}, bf16[256,384]{1,0:T(8,128)(2,1)S(1)}, u32[]{:S(2)}, u32[]{:S(2)}) collective-permute-start(bf16[256,384]{1,0:T(8,128)(2,1)S(1)} %get-tuple-element.161), channel_id=1, source_target_pairs={{0,3},{1,0},{2,1},{3,2},{4,7},{5,4},{6,5},{7,6},{8,11},{9,8},{10,9... | collective-permute-start | bytes 589832 | tf_op jit(solution)/shard_map/ppermute | solution.py:843
  121.3 24.1 %collective-permute-start.16 = (bf16[256,384]{1,0:T(8,128)(2,1)S(1)}, bf16[256,384]{1,0:T(8,128)(2,1)S(1)}, u32[]{:S(2)}, u32[]{:S(2)}) collective-permute-start(bf16[256,384]{1,0:T(8,128)(2,1)S(1)} %get-tuple-element.172), channel_id=1, source_target_pairs={{0,3},{1,0},{2,1},{3,2},{4,7},{5,4},{6,5},{7,6},{8,11},{9,8},{10,9... | collective-permute-start | bytes 589832 | tf_op jit(solution)/shard_map/ppermute | solution.py:843
  122.0 23.4 %collective-permute-start.17 = (bf16[256,384]{1,0:T(8,128)(2,1)S(1)}, bf16[256,384]{1,0:T(8,128)(2,1)S(1)}, u32[]{:S(2)}, u32[]{:S(2)}) collective-permute-start(bf16[256,384]{1,0:T(8,128)(2,1)S(1)} %get-tuple-element.173), channel_id=1, source_target_pairs={{0,2},{1,3},{2,0},{3,1},{4,6},{5,7},{6,4},{7,5},{8,10},{9,11},{10,... | collective-permute-start | bytes 589832 | tf_op jit(solution)/shard_map/ppermute | solution.py:843
  123.2 22.2 %collective-permute-start.18 = (bf16[256,384]{1,0:T(8,128)(2,1)S(1)}, bf16[256,384]{1,0:T(8,128)(2,1)S(1)}, u32[]{:S(2)}, u32[]{:S(2)}) collective-permute-start(bf16[256,384]{1,0:T(8,128)(2,1)S(1)} %get-tuple-element.174), channel_id=1, source_target_pairs={{0,1},{1,2},{2,3},{3,0},{4,5},{5,6},{6,7},{7,4},{8,9},{9,10},{10,1... | collective-permute-start | bytes 589832 | tf_op jit(solution)/shard_map/ppermute | solution.py:843
  145.5 17.3 %collective-permute-start.19 = (bf16[256,384]{1,0:T(8,128)(2,1)S(1)}, bf16[256,384]{1,0:T(8,128)(2,1)S(1)}, u32[]{:S(2)}, u32[]{:S(2)}) collective-permute-start(bf16[256,384]{1,0:T(8,128)(2,1)S(1)} %get-tuple-element.184), channel_id=1, source_target_pairs={{0,3},{1,0},{2,1},{3,2},{4,7},{5,4},{6,5},{7,6},{8,11},{9,8},{10,9... | collective-permute-start | bytes 589832 | tf_op jit(solution)/shard_map/ppermute | solution.py:843
  163.9 22.9 %collective-permute-start.24 = (bf16[4,2,224,768]{3,2,1,0:T(8,128)(2,1)}, bf16[4,2,224,768]{3,2,1,0:T(8,128)(2,1)S(1)}, u32[]{:S(2)}, u32[]{:S(2)}) collective-permute-start(bf16[4,2,224,768]{3,2,1,0:T(8,128)(2,1)} %get-tuple-element.196), channel_id=1, source_target_pairs={{0,4},{4,0},{8,12},{12,8},{16,20},{20,16},{24,28},{28,24},{1,5},{5... | collective-permute-start | bytes 8257544 | tf_op jit(solution)/shard_map/ppermute | solution.py:847
  164.0 22.8 %collective-permute-start.23 = (bf16[4,2,224,768]{3,2,1,0:T(8,128)(2,1)}, bf16[4,2,224,768]{3,2,1,0:T(8,128)(2,1)S(1)}, u32[]{:S(2)}, u32[]{:S(2)}) collective-permute-start(bf16[4,2,224,768]{3,2,1,0:T(8,128)(2,1)} %get-tuple-element.194), channel_id=1, source_target_pairs={{0,4},{4,0},{8,12},{12,8},{16,20},{20,16},{24,28},{28,24},{1,5},{5... | collective-permute-start | bytes 8257544 | tf_op jit(solution)/shard_map/ppermute | solution.py:847
  171.1 20.4 %collective-permute-start.22 = (bf16[256,768]{1,0:T(8,128)(2,1)S(1)}, bf16[256,768]{1,0:T(8,128)(2,1)S(1)}, u32[]{:S(2)}, u32[]{:S(2)}) collective-permute-start(bf16[256,768]{1,0:T(8,128)(2,1)S(1)} %get-tuple-element.193), channel_id=1, source_target_pairs={{0,2},{1,3},{2,0},{3,1},{4,6},{5,7},{6,4},{7,5},{8,10},{9,11},{10,... | collective-permute-start | bytes 1179656 | tf_op jit(solution)/shard_map/ppermute | solution.py:843
  191.5 31.5 %collective-permute-start.26 = (bf16[2,2,224,768]{3,2,1,0:T(8,128)(2,1)S(1)}, bf16[2,2,224,768]{3,2,1,0:T(8,128)(2,1)S(1)}, u32[]{:S(2)}, u32[]{:S(2)}) collective-permute-start(bf16[2,2,224,768]{3,2,1,0:T(8,128)(2,1)S(1)} %get-tuple-element.201), channel_id=1, source_target_pairs={{0,16},{4,20},{8,24},{12,28},{16,0},{20,4},{24,8},{28,12},{1,17},{... | collective-permute-start | bytes 4128776 | tf_op jit(solution)/shard_map/ppermute | solution.py:847
  193.0 31.3 %collective-permute-start.25 = (bf16[2,2,224,768]{3,2,1,0:T(8,128)(2,1)S(1)}, bf16[2,2,224,768]{3,2,1,0:T(8,128)(2,1)S(1)}, u32[]{:S(2)}, u32[]{:S(2)}) collective-permute-start(bf16[2,2,224,768]{3,2,1,0:T(8,128)(2,1)S(1)} %get-tuple-element.199), channel_id=1, source_target_pairs={{0,8},{4,12},{8,0},{12,4},{16,24},{20,28},{24,16},{28,20},{1,9},{5... | collective-permute-start | bytes 4128776 | tf_op jit(solution)/shard_map/ppermute | solution.py:847
  194.5 20.1 %collective-permute-start.27 = (bf16[256,768]{1,0:T(8,128)(2,1)S(1)}, bf16[256,768]{1,0:T(8,128)(2,1)S(1)}, u32[]{:S(2)}, u32[]{:S(2)}) collective-permute-start(bf16[256,768]{1,0:T(8,128)(2,1)S(1)} %get-tuple-element.204), channel_id=1, source_target_pairs={{0,3},{1,0},{2,1},{3,2},{4,7},{5,4},{6,5},{7,6},{8,11},{9,8},{10,9... | collective-permute-start | bytes 1179656 | tf_op jit(solution)/shard_map/ppermute | solution.py:843
  196.1 18.5 %collective-permute-start.28 = (bf16[256,768]{1,0:T(8,128)(2,1)S(1)}, bf16[256,768]{1,0:T(8,128)(2,1)S(1)}, u32[]{:S(2)}, u32[]{:S(2)}) collective-permute-start(bf16[256,768]{1,0:T(8,128)(2,1)S(1)} %get-tuple-element.205), channel_id=1, source_target_pairs={{0,1},{1,2},{2,3},{3,0},{4,5},{5,6},{6,7},{7,4},{8,9},{9,10},{10,1... | collective-permute-start | bytes 1179656 | tf_op jit(solution)/shard_map/ppermute | solution.py:843
  227.4 18.4 %collective-permute-start.33 = (bf16[1,2,224,768]{3,2,1,0:T(8,128)(2,1)S(1)}, bf16[1,2,224,768]{3,2,1,0:T(8,128)(2,1)S(1)}, u32[]{:S(2)}, u32[]{:S(2)}) collective-permute-start(bf16[1,2,224,768]{3,2,1,0:T(8,128)(2,1)S(1)} %add_convert_fusion.5), channel_id=1, source_target_pairs={{0,8},{4,12},{8,0},{12,4},{16,24},{20,28},{24,16},{28,20},{1,9},{5... | collective-permute-start | bytes 2064392 | tf_op jit(solution)/shard_map/ppermute | solution.py:847
  230.4 18.4 %collective-permute-start.32 = (bf16[1,2,224,768]{3,2,1,0:T(8,128)(2,1)S(1)}, bf16[1,2,224,768]{3,2,1,0:T(8,128)(2,1)S(1)}, u32[]{:S(2)}, u32[]{:S(2)}) collective-permute-start(bf16[1,2,224,768]{3,2,1,0:T(8,128)(2,1)S(1)} %add_convert_fusion.6), channel_id=1, source_target_pairs={{0,16},{4,20},{8,24},{12,28},{16,0},{20,4},{24,8},{28,12},{1,17},{... | collective-permute-start | bytes 2064392 | tf_op jit(solution)/shard_map/ppermute | solution.py:847
  234.4 29.5 %collective-permute-start.36 = (bf16[2,3,64,1024]{3,2,1,0:T(8,128)(2,1)S(1)}, bf16[2,3,64,1024]{3,2,1,0:T(8,128)(2,1)S(1)}, u32[]{:S(2)}, u32[]{:S(2)}) collective-permute-start(bf16[2,3,64,1024]{3,2,1,0:T(8,128)(2,1)S(1)} %add_convert_fusion.2), channel_id=1, source_target_pairs={{0,16},{4,20},{8,24},{12,28},{16,0},{20,4},{24,8},{28,12},{1,17},{... | collective-permute-start | bytes 2359304 | tf_op jit(solution)/shard_map/ppermute | solution.py:847
  235.7 28.2 %collective-permute-start.31 = (bf16[2,3,64,1024]{3,2,1,0:T(8,128)(2,1)S(1)}, bf16[2,3,64,1024]{3,2,1,0:T(8,128)(2,1)S(1)}, u32[]{:S(2)}, u32[]{:S(2)}) collective-permute-start(bf16[2,3,64,1024]{3,2,1,0:T(8,128)(2,1)S(1)} %add_convert_fusion.3), channel_id=1, source_target_pairs={{0,8},{4,12},{8,0},{12,4},{16,24},{20,28},{24,16},{28,20},{1,9},{5... | collective-permute-start | bytes 2359304 | tf_op jit(solution)/shard_map/ppermute | solution.py:847
  (80 other events, 901.4 us)
Sparse Core Ops, SparseCore 0:
  11.5 69.6 all-gather.1
